TPU v7x, 768 devices: a whole 4x8x12 slice. The times are simulated.
768 devices in a mesh: fsdp: 192 (over x, z_lo, y, core), tp: 4 (over z_hi).
Axes of the slice: x: 4, y: 8, z: 12 (z_hi: 4, z_lo: 3; z = z_hi * 3 + z_lo), core: 2. Of those that a mesh axis runs over, the one named last changes fastest.
Arguments:
- tokens: bfloat16 [384, 8192], P('fsdp', 'tp'), may hold values from -6 to 6
- gate_weight: bfloat16 [27648, 8192], P('fsdp', 'tp'), may hold values from -0.0625 to 0.0625
- up_weight: bfloat16 [27648, 8192], P('fsdp', 'tp'), may hold values from -0.0625 to 0.0625
- down_weight: bfloat16 [27648, 8192], P('fsdp', 'tp'), may hold values from -0.0390625 to 0.0390625
Outputs:
- mixed: bfloat16 [384, 8192], P('fsdp', 'tp')
All inputs are finite; a program needn't handle non-finite values.
Results may differ from a plain program's by a relative error of at most 0.0049.
Values may be sent and summed in bfloat16 or wider, within the bound.
No kernel may reach another device: no remote copies, remote signals or barrier semaphores. Data moves between devices by JAX's collectives and lax.ppermute only.
A program may use at most 32 MiB of HBM per device.

v0:
```python
import jax
import jax.numpy as jnp
from jax import lax
from jax.sharding import PartitionSpec as P


def body(tokens, gate_weight, up_weight, down_weight):
    hidden_width = gate_weight.shape[0]
    contract = (((1,), (1,)), ((), ()))
    block_rows = lax.all_gather(tokens, "fsdp", axis=0, tiled=True)
    gate_part = lax.dot_general(
        block_rows, gate_weight, contract, preferred_element_type=jnp.float32
    )
    up_part = lax.dot_general(block_rows, up_weight, contract, preferred_element_type=jnp.float32)
    partial_value = jnp.concatenate([gate_part, up_part], axis=1)
    share_rows = lax.psum_scatter(partial_value, "tp", scatter_dimension=0, tiled=True)
    quarter = (jax.nn.silu(share_rows[:, :hidden_width]) * share_rows[:, hidden_width:]).astype(
        jnp.bfloat16
    )
    hidden = lax.all_gather(quarter, "tp", axis=0, tiled=True)
    down_terms = jnp.dot(hidden, down_weight, preferred_element_type=jnp.float32)
    mixed = lax.psum_scatter(down_terms, "fsdp", scatter_dimension=0, tiled=True)
    return mixed.astype(jnp.bfloat16)


def solution(mesh):
    placed = (P("fsdp", "tp"), P("fsdp", "tp"), P("fsdp", "tp"), P("fsdp", "tp"))
    return jax.shard_map(
        body, mesh=mesh, in_specs=placed, out_specs=P("fsdp", "tp"), check_vma=False
    )
```

profile of v0, /device:TPU:192, one launch (start us, length us, event | category | flops | bytes accessed | tf_op | source)
XLA Modules:
  0.0 2103.0 jit_solution(10752201050432469008)
XLA Ops:
  6.5 0.0 copy-start
  6.5 0.0 all-gather.4.cloned.1.call-start
  6.5 0.7 all-gather.4.cloned.1.call-update
  7.3 0.0 copy-start.1
  7.3 0.0 reduce-scatter.4.cloned.1.call-start
  7.3 975.0 %all-gather.4.cloned.1.call-done = bf16[192,2,2048]{2,1,0:T(2,128)(2,1)} async-done(((bf16[1,2,2048]{2,1,0:T(2,128)(2,1)}), bf16[192,2,2048]{2,1,0:T(2,128)(2,1)}) %all-gather.4.cloned.1.call-update) | async-done | bytes 1572880 | tf_op jit(solution)/shard_map/all_gather | solution.py:10
  982.3 2.5 reshape.1
  984.8 0.0 copy-done.1
  984.9 0.0 copy-start.2
  984.9 0.6 fusion.2
  985.5 0.4 copy-done.2
  985.9 0.6 fusion.3
  986.6 1.1 copy.7
  987.6 0.0 reduce-scatter.4.cloned.1.call-update
  987.7 1.3 dynamic-slice
  989.6 33.5 %reduce-scatter.4.cloned.1.call-done = f32[96,288]{1,0:T(8,128)} async-done(((f32[384,288]{1,0:T(8,128)}), f32[96,288]{1,0:T(8,128)}) %reduce-scatter.4.cloned.1.call-update) | async-done | bytes 110608
  1023.1 1.1 fusion.1
  1024.2 0.1 copy.10
  1024.3 0.1 copy.9
  1024.4 16.1 all-gather.1
  1040.5 0.1 copy.6
  1040.6 0.1 reshape.3
  1040.7 0.0 copy-done
  1040.7 2.3 fusion.4
  1043.0 1052.5 %all-reduce.2 = bf16[384,2048]{1,0:T(8,128)(2,1)S(1)} all-reduce(f32[384,2048]{1,0:T(8,128)} %fusion.4), channel_id=3, replica_groups=mesh['fsdp'=192,'tp'=4] {'fsdp'}, use_global_device_ids=true, to_apply=%region_1.2.clone | all-reduce | flops 786432 | bytes 4718592
  2095.5 0.6 dynamic-slice_convert_fusion
  (2 shorter events, 0.1 us)
Async XLA Ops:
  6.5 1034.2 %copy-start = (bf16[144,2048]{1,0:T(8,128)(2,1)S(1)}, bf16[144,2048]{1,0:T(8,128)(2,1)}, u32[]{:S(2)}) copy-start(bf16[144,2048]{1,0:T(8,128)(2,1)} %param.7) | copy-start | bytes 1769476
  6.5 975.8 %all-gather.4.cloned.1.call-start = ((), (), s32[]{:S(2)}) async-start(), calls=%async_computation.1 | async-start | bytes 1581056 | tf_op jit(solution)/shard_map/all_gather | solution.py:10
  7.3 977.6 %copy-start.1 = (bf16[144,2048]{1,0:T(8,128)(2,1)S(1)}, bf16[144,2048]{1,0:T(8,128)(2,1)}, u32[]{:S(2)}) copy-start(bf16[144,2048]{1,0:T(8,128)(2,1)} %param.5) | copy-start | bytes 1769476
  7.3 1015.8 %reduce-scatter.4.cloned.1.call-start = ((), (), s32[]{:S(2)}) async-start(), calls=%async_computation.2 | async-start | bytes 737280
  984.9 1.1 copy-start.2
Sparse Core Ops, SparseCore 0:
  9.7 972.5 all-gather.3
  987.8 35.2 reduce-scatter.3
where the time goes:
time: 2100 us
  blocking collectives  1070 us (51%)
  waiting for transfers between devices  1010 us (48%)
    unnamed x1, blocking collectives  1050 us
    all_gather x1, waiting for transfers between devices, body(): block_rows = lax.all_gather(tokens, 'fsdp', axis=0, tiled=True)  975 us
  transfers between devices with their start and end apart: 2, of which 2 were waited for; matrix products, arithmetic and copies ran while one was open for 0% of the time, Pallas kernels for 0%

commit v1 on v0

v1 whole, which is shorter than its diff:
```python
import jax
import jax.numpy as jnp
from jax import lax
from jax.sharding import Mesh
from jax.sharding import PartitionSpec as P

CHIPS = "chips"
CORE = "core"
TP = "tp"


def body(tokens, gate_weight, up_weight, down_weight):
    chips = lax.axis_size(CHIPS)
    tp = lax.axis_size(TP)
    mine, width = tokens.shape
    hidden_width = gate_weight.shape[0]
    swap = [(0, 1), (1, 0)]
    rows = chips * mine

    spread = jnp.broadcast_to(tokens[None], (chips, mine, width))
    own = lax.all_to_all(spread, CHIPS, split_axis=0, concat_axis=0, tiled=True)
    own = own.reshape(rows, width)
    other = lax.ppermute(own, CORE, swap)
    block_rows = jnp.concatenate([own, other], axis=0)

    contract = (((1,), (1,)), ((), ()))
    gate_part = lax.dot_general(
        gate_weight, block_rows, contract, preferred_element_type=jnp.float32
    )
    up_part = lax.dot_general(up_weight, block_rows, contract, preferred_element_type=jnp.float32)
    share = hidden_width // tp
    parts = jnp.concatenate(
        [gate_part.reshape(tp, share, 2 * rows), up_part.reshape(tp, share, 2 * rows)], axis=1
    )
    parts = lax.all_to_all(
        parts.astype(jnp.bfloat16), TP, split_axis=0, concat_axis=0, tiled=True
    )
    sums = jnp.sum(parts.astype(jnp.float32), axis=0)
    quarter = (jax.nn.silu(sums[:share]) * sums[share:]).astype(jnp.bfloat16)
    hidden = lax.all_gather(quarter, TP, axis=0, tiled=True)

    down_terms = lax.dot_general(
        hidden, down_weight, (((0,), (0,)), ((), ())), preferred_element_type=jnp.float32
    )
    sent = lax.ppermute(down_terms[rows:].astype(jnp.bfloat16), CORE, swap)
    chip_terms = (down_terms[:rows] + sent.astype(jnp.float32)).astype(jnp.bfloat16)
    chip_terms = lax.all_to_all(
        chip_terms.reshape(chips, mine, width), CHIPS, split_axis=0, concat_axis=0, tiled=True
    )
    return jnp.sum(chip_terms.astype(jnp.float32), axis=0).astype(jnp.bfloat16)


def solution(mesh):
    cores = 2
    fsdp, tp = mesh.devices.shape
    fine = Mesh(mesh.devices.reshape(fsdp // cores, cores, tp), (CHIPS, CORE, TP))
    placed = P((CHIPS, CORE), TP)
    return jax.shard_map(
        body, mesh=fine, in_specs=(placed,) * 4, out_specs=placed, check_vma=False
    )
```

time: 2100 us -> 126 us (0.06)
  the two profiles are of different devices: /device:TPU:192 before, /device:TPU:1 now
where the time goes in v1:
time: 126 us; the launch traced here: 124 us
  blocking collectives  102 us (81%)
  starting transfers between devices  12.8 us (10%)
  waiting for transfers between devices  3.71 us (3%)
  local copies, waits for them, and re-layouts  2.28 us (2%)
  matrix products  1.85 us (1%)
  other arithmetic  1.54 us (1%)
    all_to_all x1, blocking collectives, body(): own = lax.all_to_all(spread, CHIPS, split_axis=0, concat_axis=0, tiled=True)  36.1 us
    all_to_all x1, blocking collectives, body(): lax.all_to_all(chip_terms.reshape(chips, mine, width), CHIPS, split_axis=...  27.8 us
    all_to_all x1, blocking collectives, body(): lax.all_to_all(parts.astype(jnp.bfloat16), TP, split_axis=0, concat_axis=...  23.3 us
    all_gather x1, blocking collectives, body(): hidden = lax.all_gather(quarter, TP, axis=0, tiled=True)  14.7 us
    ppermute x1, starting transfers between devices, body(): sent = lax.ppermute(down_terms[rows:].astype(jnp.bfloat16), CORE, swap)  7.55 us
    ppermute x1, starting transfers between devices, body(): other = lax.ppermute(own, CORE, swap)  5.3 us
  transfers between devices with their start and end apart: 2, of which 2 were waited for; matrix products, arithmetic and copies ran while one was open for 0% of the time, Pallas kernels for 0%

profile of v1, /device:TPU:1, one launch (start us, length us, event | category | flops | bytes accessed | tf_op | source)
XLA Modules:
  0.0 124.2 jit_solution(3969652583560027001)
XLA Ops:
  0.0 0.0 copy-start
  0.0 1.2 broadcast_in_dim.2
  1.2 36.1 %all_to_all.15 = bf16[96,2,2048]{2,1,0:T(2,128)(2,1)S(1)} all-to-all(bf16[96,2,2048]{2,1,0:T(2,128)(2,1)S(1)} %broadcast_in_dim.2), channel_id=1, replica_groups=mesh['chips'=96,'core'=2,'tp'=4] {'chips'}, dimensions={0} | all-to-all | bytes 1572864 | tf_op jit(solution)/shard_map/all_to_all | solution.py:21
  37.3 0.3 reshape.15
  37.6 0.0 copy-start.1
  37.6 5.3 %collective-permute-start = (bf16[192,2048]{1,0:T(8,128)(2,1)S(1)}, bf16[192,2048]{1,0:T(8,128)(2,1)S(1)}, u32[]{:S(2)}, u32[]{:S(2)}) collective-permute-start(bf16[192,2048]{1,0:T(8,128)(2,1)S(1)} %reshape.15), channel_id=1, source_target_pairs={{0,4},{4,0},{1,5},{5,1},{2,6},{6,2},{3,7},{7,3},{8,12},{12,8},{9,1... | collective-permute-start | bytes 2359304 | tf_op jit(solution)/shard_map/ppermute | solution.py:23
  42.9 0.1 constant_dynamic-update-slice_fusion.1
  43.0 0.0 copy-start.2
  43.0 1.8 %collective-permute-done = bf16[192,2048]{1,0:T(8,128)(2,1)S(1)} collective-permute-done((bf16[192,2048]{1,0:T(8,128)(2,1)S(1)}, bf16[192,2048]{1,0:T(8,128)(2,1)S(1)}, u32[]{:S(2)}, u32[]{:S(2)}) %collective-permute-start) | collective-permute-done | bytes 786464 | tf_op jit(solution)/shard_map/ppermute | solution.py:23
  44.8 0.1 constant_dynamic-update-slice_fusion
  44.9 0.0 copy-done.1
  44.9 0.6 fusion.2
  45.5 0.0 copy-done.2
  45.5 0.6 fusion.1
  46.3 23.3 %all_to_all.16 = bf16[4,72,384]{2,1,0:T(8,128)(2,1)S(1)} all-to-all(bf16[4,72,384]{2,1,0:T(8,128)(2,1)S(1)} %pad_maximum_fusion), channel_id=1, replica_groups=mesh['chips'=96,'core'=2,'tp'=4] {'tp'}, dimensions={0} | all-to-all | bytes 442368 | tf_op jit(solution)/shard_map/all_to_all | solution.py:35
  69.7 14.7 %all-gather = bf16[4,36,384]{2,1,0:T(8,128)(2,1)S(1)} all-gather(bf16[1,36,384]{2,1,0:T(8,128)(2,1)S(1)} %fusion.4), channel_id=1, replica_groups=mesh['chips'=96,'core'=2,'tp'=4] {'tp'}, dimensions={0}, use_global_device_ids=true | all-gather | bytes 138240 | tf_op jit(solution)/shard_map/all_gather | solution.py:40
  84.3 0.0 copy-done
  84.3 0.6 fusion.5
  85.0 0.1 slice.33
  85.1 7.5 %collective-permute-start.1 = (bf16[192,2048]{1,0:T(8,128)(2,1)S(1)}, bf16[192,2048]{1,0:T(8,128)(2,1)S(1)}, u32[]{:S(2)}, u32[]{:S(2)}) collective-permute-start(bf16[192,2048]{1,0:T(8,128)(2,1)S(1)} %slice.33), channel_id=1, source_target_pairs={{0,4},{4,0},{1,5},{5,1},{2,6},{6,2},{3,7},{7,3},{8,12},{12,8},{9,1... | collective-permute-start | bytes 2359304 | tf_op jit(solution)/shard_map/ppermute | solution.py:45
  92.6 1.9 %collective-permute-done.1 = bf16[192,2048]{1,0:T(8,128)(2,1)S(1)} collective-permute-done((bf16[192,2048]{1,0:T(8,128)(2,1)S(1)}, bf16[192,2048]{1,0:T(8,128)(2,1)S(1)}, u32[]{:S(2)}, u32[]{:S(2)}) %collective-permute-start.1) | collective-permute-done | bytes 786464 | tf_op jit(solution)/shard_map/ppermute | solution.py:45
  94.5 0.2 fusion
  94.7 0.5 reshape.18
  95.2 27.8 %all_to_all.17 = bf16[96,2,2048]{2,1,0:T(2,128)(2,1)S(1)} all-to-all(bf16[96,2,2048]{2,1,0:T(2,128)(2,1)S(1)} %reshape.18), channel_id=1, replica_groups=mesh['chips'=96,'core'=2,'tp'=4] {'chips'}, dimensions={0} | all-to-all | bytes 1572864 | tf_op jit(solution)/shard_map/all_to_all | solution.py:47
  123.0 1.3 %reduce_sum.22 = bf16[2,2048]{1,0:T(2,128)(2,1)} reduce(bf16[96,2,2048]{2,1,0:T(2,128)(2,1)S(1)} %all_to_all.17, bf16[]{:T(256)} %constant.6.clone.1), dimensions={0}, to_apply=%region_1.2 | reduce | flops 389120 | bytes 794626 | tf_op jit(solution)/shard_map/reduce_sum | solution.py:50
  (6 shorter events, 0.2 us)
Async XLA Ops:
  0.0 84.3 %copy-start = (bf16[144,2048]{1,0:T(8,128)(2,1)S(1)}, bf16[144,2048]{1,0:T(8,128)(2,1)}, u32[]{:S(2)}) copy-start(bf16[144,2048]{1,0:T(8,128)(2,1)} %param.7) | copy-start | bytes 1769476
  37.6 7.3 %copy-start.1 = (bf16[144,2048]{1,0:T(8,128)(2,1)S(1)}, bf16[144,2048]{1,0:T(8,128)(2,1)}, u32[]{:S(2)}) copy-start(bf16[144,2048]{1,0:T(8,128)(2,1)} %param.6) | copy-start | bytes 1769476
  37.6 7.2 %collective-permute-start = (bf16[192,2048]{1,0:T(8,128)(2,1)S(1)}, bf16[192,2048]{1,0:T(8,128)(2,1)S(1)}, u32[]{:S(2)}, u32[]{:S(2)}) collective-permute-start(bf16[192,2048]{1,0:T(8,128)(2,1)S(1)} %reshape.15), channel_id=1, source_target_pairs={{0,4},{4,0},{1,5},{5,1},{2,6},{6,2},{3,7},{7,3},{8,12},{12,8},{9,1... | collective-permute-start | bytes 2359304 | tf_op jit(solution)/shard_map/ppermute | solution.py:23
  43.0 2.5 %copy-start.2 = (bf16[144,2048]{1,0:T(8,128)(2,1)S(1)}, bf16[144,2048]{1,0:T(8,128)(2,1)}, u32[]{:S(2)}) copy-start(bf16[144,2048]{1,0:T(8,128)(2,1)} %param.5) | copy-start | bytes 1769476
  85.1 9.4 %collective-permute-start.1 = (bf16[192,2048]{1,0:T(8,128)(2,1)S(1)}, bf16[192,2048]{1,0:T(8,128)(2,1)S(1)}, u32[]{:S(2)}, u32[]{:S(2)}) collective-permute-start(bf16[192,2048]{1,0:T(8,128)(2,1)S(1)} %slice.33), channel_id=1, source_target_pairs={{0,4},{4,0},{1,5},{5,1},{2,6},{6,2},{3,7},{7,3},{8,12},{12,8},{9,1... | collective-permute-start | bytes 2359304 | tf_op jit(solution)/shard_map/ppermute | solution.py:45

commit v2 on v1

v2 whole, which is shorter than its diff:
```python
import jax
import jax.numpy as jnp
from jax import lax
from jax.sharding import Mesh
from jax.sharding import PartitionSpec as P

CHIPS = "chips"
CORE = "core"
TP = "tp"


def body(tokens, gate_weight, up_weight, down_weight):
    chips = lax.axis_size(CHIPS)
    tp = lax.axis_size(TP)
    mine, width = tokens.shape
    hidden_width = 2 * gate_weight.shape[0]
    share = hidden_width // tp
    swap = [(0, 1), (1, 0)]
    rows = chips * mine

    gate_weight, up_weight, down_weight = (
        jnp.concatenate([part, lax.ppermute(part, CORE, swap)], axis=0)
        for part in (gate_weight, up_weight, down_weight)
    )
    spread = jnp.broadcast_to(tokens[None], (chips, mine, width))
    block_rows = lax.all_to_all(spread, CHIPS, split_axis=0, concat_axis=0, tiled=True)
    block_rows = block_rows.reshape(rows, width)

    contract = (((1,), (1,)), ((), ()))
    gate_part = lax.dot_general(
        gate_weight, block_rows, contract, preferred_element_type=jnp.float32
    )
    up_part = lax.dot_general(up_weight, block_rows, contract, preferred_element_type=jnp.float32)
    parts = jnp.concatenate([gate_part, up_part], axis=1).reshape(tp, share, 2 * rows)
    parts = lax.all_to_all(
        parts.astype(jnp.bfloat16), TP, split_axis=0, concat_axis=0, tiled=True
    )
    sums = jnp.sum(parts.astype(jnp.float32), axis=0)
    quarter = (jax.nn.silu(sums[:, :rows]) * sums[:, rows:]).astype(jnp.bfloat16)
    hidden = lax.all_gather(quarter, TP, axis=0, tiled=True)

    chip_terms = lax.dot_general(
        hidden, down_weight, (((0,), (0,)), ((), ())), preferred_element_type=jnp.float32
    ).astype(jnp.bfloat16)
    chip_terms = lax.all_to_all(
        chip_terms.reshape(chips, mine, width), CHIPS, split_axis=0, concat_axis=0, tiled=True
    )
    return jnp.sum(chip_terms.astype(jnp.float32), axis=0).astype(jnp.bfloat16)


def solution(mesh):
    cores = 2
    fsdp, tp = mesh.devices.shape
    fine = Mesh(mesh.devices.reshape(fsdp // cores, cores, tp), (CHIPS, CORE, TP))
    placed = P((CHIPS, CORE), TP)
    return jax.shard_map(
        body, mesh=fine, in_specs=(placed,) * 4, out_specs=placed, check_vma=False
    )
```

time: 126 us -> 117 us (0.929)
  the two profiles are of different devices: /device:TPU:1 before, /device:TPU:8 now
where the time goes in v2:
time: 117 us; the launch traced here: 116 us
  blocking collectives  43.4 us (37%)
  starting transfers between devices  34.3 us (29%)
  waiting for transfers between devices  30.9 us (26%)
  local copies, waits for them, and re-layouts  2.8 us (2%)
  matrix products  2.65 us (2%)
  other arithmetic  2.17 us (2%)
    all_to_all x1, blocking collectives, body(): lax.all_to_all(chip_terms.reshape(chips, mine, width), CHIPS, split_axis=...  27.7 us
    all_to_all x1, waiting for transfers between devices, body(): lax.all_to_all(spread, CHIPS, split_axis=0, concat_axis=0, tiled=True)  18.8 us
    all_gather x1, blocking collectives, body(): hidden = lax.all_gather(quarter, TP, axis=0, tiled=True)  15.7 us
    all_to_all x1, starting transfers between devices, body(): lax.all_to_all(spread, CHIPS, split_axis=0, concat_axis=0, tiled=True)  14.8 us
    all_to_all x1, starting transfers between devices, body(): lax.all_to_all(parts.astype(jnp.bfloat16), TP, split_axis=0, concat_axis=...  13.3 us
    all_to_all x1, waiting for transfers between devices, body(): lax.all_to_all(parts.astype(jnp.bfloat16), TP, split_axis=0, concat_axis=...  12.1 us
    ppermute x3, starting transfers between devices, body(): lax.ppermute(part, CORE, swap)  6.24 us
  transfers between devices with their start and end apart: 5, of which 2 were waited for; matrix products, arithmetic and copies ran while one was open for 2% of the time, Pallas kernels for 0%

profile of v2, /device:TPU:8, one launch (start us, length us, event | category | flops | bytes accessed | tf_op | source)
XLA Modules:
  0.0 116.3 jit_solution(3160502502650350351)
XLA Ops:
  0.0 2.0 %broadcast_in_dim.2 = bf16[96,2,2048]{2,1,0:T(2,128)(2,1)} broadcast(bf16[2,2048]{1,0:T(2,128)(2,1)} %param.4), dimensions={1,2} | broadcast | bytes 794624 | tf_op jit(solution)/shard_map/broadcast_in_dim | solution.py:25
  2.0 0.0 copy-start
  2.0 0.0 copy-start.1
  2.0 14.8 %all-to-all-start = ((bf16[96,2,2048]{2,1,0:T(2,128)(2,1)}), bf16[96,2,2048]{2,1,0:T(2,128)(2,1)S(1)}, u32[]{:S(2)}, u32[]{:S(2)}) async-start(bf16[96,2,2048]{2,1,0:T(2,128)(2,1)} %broadcast_in_dim.2), calls=%async_computation | async-start | bytes 1572864 | tf_op jit(solution)/shard_map/all_to_all | solution.py:26
  16.8 0.0 copy-done
  16.8 1.9 %collective-permute-start.1 = (bf16[144,2048]{1,0:T(8,128)(2,1)S(1)}, bf16[144,2048]{1,0:T(8,128)(2,1)}, u32[]{:S(2)}, u32[]{:S(2)}) collective-permute-start(bf16[144,2048]{1,0:T(8,128)(2,1)S(1)} %copy-done), channel_id=1, source_target_pairs={{0,4},{4,0},{1,5},{5,1},{2,6},{6,2},{3,7},{7,3},{8,12},{12,8},{9,1... | collective-permute-start | bytes 1769480 | tf_op jit(solution)/shard_map/ppermute | solution.py:22
  18.7 0.0 copy-done.1
  18.7 2.4 %collective-permute-start = (bf16[144,2048]{1,0:T(8,128)(2,1)S(1)}, bf16[144,2048]{1,0:T(8,128)(2,1)S(1)}, u32[]{:S(2)}, u32[]{:S(2)}) collective-permute-start(bf16[144,2048]{1,0:T(8,128)(2,1)S(1)} %copy-done.1), channel_id=1, source_target_pairs={{0,4},{4,0},{1,5},{5,1},{2,6},{6,2},{3,7},{7,3},{8,12},{12,8},{9,1... | collective-permute-start | bytes 1769480 | tf_op jit(solution)/shard_map/ppermute | solution.py:22
  21.1 18.8 %all-to-all-done = bf16[96,2,2048]{2,1,0:T(2,128)(2,1)S(1)} async-done(((bf16[96,2,2048]{2,1,0:T(2,128)(2,1)}), bf16[96,2,2048]{2,1,0:T(2,128)(2,1)S(1)}, u32[]{:S(2)}, u32[]{:S(2)}) %all-to-all-start) | async-done | bytes 786464 | tf_op jit(solution)/shard_map/all_to_all | solution.py:26
  39.9 0.3 reshape.9
  40.2 0.0 collective-permute-done.1
  40.3 1.6 %fusion.11 = bf16[288,192]{1,0:T(8,128)(2,1)S(1)} fusion(bf16[192,2048]{1,0:T(8,128)(2,1)S(1)} %reshape.9, bf16[144,2048]{1,0:T(8,128)(2,1)} %collective-permute-done.1, bf16[144,2048]{1,0:T(8,128)(2,1)S(1)} %copy-done), kind=kOutput, calls=%fused_computation.12 | convolution fusion | flops 228907008 | bytes 2076672 | tf_op jit(solution)/shard_map/dot_general | solution.py:33
  41.8 0.0 collective-permute-done
  41.8 0.5 fusion.14
  42.3 0.0 copy-start.2
  42.3 0.8 pad_maximum_fusion
  43.1 13.3 %all-to-all-start.1 = ((bf16[4,72,384]{2,1,0:T(8,128)(2,1)}), bf16[4,72,384]{2,1,0:T(8,128)(2,1)S(1)}, u32[]{:S(2)}, u32[]{:S(2)}) async-start(bf16[4,72,384]{2,1,0:T(8,128)(2,1)} %bitcast), calls=%async_computation.1 | async-start | bytes 442368 | tf_op jit(solution)/shard_map/all_to_all | solution.py:35
  56.4 0.0 copy-done.2
  56.4 1.9 %collective-permute-start.2 = (bf16[144,2048]{1,0:T(8,128)(2,1)S(1)}, bf16[144,2048]{1,0:T(8,128)(2,1)S(1)}, u32[]{:S(2)}, u32[]{:S(2)}) collective-permute-start(bf16[144,2048]{1,0:T(8,128)(2,1)S(1)} %copy-done.2), channel_id=1, source_target_pairs={{0,4},{4,0},{1,5},{5,1},{2,6},{6,2},{3,7},{7,3},{8,12},{12,8},{9,1... | collective-permute-start | bytes 1769480 | tf_op jit(solution)/shard_map/ppermute | solution.py:22
  58.3 12.1 %all-to-all-done.1 = bf16[4,72,384]{2,1,0:T(8,128)(2,1)S(1)} async-done(((bf16[4,72,384]{2,1,0:T(8,128)(2,1)}), bf16[4,72,384]{2,1,0:T(8,128)(2,1)S(1)}, u32[]{:S(2)}, u32[]{:S(2)}) %all-to-all-start.1) | async-done | bytes 221216 | tf_op jit(solution)/shard_map/all_to_all | solution.py:35
  70.4 0.1 fusion.17
  70.5 15.7 %all_gather.3 = bf16[288,192]{1,0:T(8,128)(2,1)S(1)} all-gather(bf16[72,192]{1,0:T(8,128)(2,1)S(1)} %fusion.17), channel_id=1, replica_groups=mesh['chips'=96,'core'=2,'tp'=4] {'tp'}, dimensions={0}, use_global_device_ids=true | all-gather | bytes 138240 | tf_op jit(solution)/shard_map/all_gather | solution.py:40
  86.3 0.0 collective-permute-done.2
  86.3 0.6 convolution_convert_fusion
  86.9 0.5 reshape.10
  87.4 27.7 %all_to_all.15 = bf16[96,2,2048]{2,1,0:T(2,128)(2,1)S(1)} all-to-all(bf16[96,2,2048]{2,1,0:T(2,128)(2,1)S(1)} %reshape.10), channel_id=1, replica_groups=mesh['chips'=96,'core'=2,'tp'=4] {'chips'}, dimensions={0} | all-to-all | bytes 1572864 | tf_op jit(solution)/shard_map/all_to_all | solution.py:45
  115.1 1.3 %reduce_sum.22 = bf16[2,2048]{1,0:T(2,128)(2,1)} reduce(bf16[96,2,2048]{2,1,0:T(2,128)(2,1)S(1)} %all_to_all.15, bf16[]{:T(256)} %constant.6.clone.1), dimensions={0}, to_apply=%region_1.2 | reduce | flops 389120 | bytes 794626 | tf_op jit(solution)/shard_map/reduce_sum | solution.py:48
  (1 shorter events, 0.0 us)
Async XLA Ops:
  2.0 14.8 %copy-start = (bf16[144,2048]{1,0:T(8,128)(2,1)S(1)}, bf16[144,2048]{1,0:T(8,128)(2,1)}, u32[]{:S(2)}) copy-start(bf16[144,2048]{1,0:T(8,128)(2,1)} %param.6) | copy-start | bytes 1769476
  2.0 16.7 %copy-start.1 = (bf16[144,2048]{1,0:T(8,128)(2,1)S(1)}, bf16[144,2048]{1,0:T(8,128)(2,1)}, u32[]{:S(2)}) copy-start(bf16[144,2048]{1,0:T(8,128)(2,1)} %param.5) | copy-start | bytes 1769476
  2.0 37.9 %all-to-all-start = ((bf16[96,2,2048]{2,1,0:T(2,128)(2,1)}), bf16[96,2,2048]{2,1,0:T(2,128)(2,1)S(1)}, u32[]{:S(2)}, u32[]{:S(2)}) async-start(bf16[96,2,2048]{2,1,0:T(2,128)(2,1)} %broadcast_in_dim.2), calls=%async_computation | async-start | bytes 1572864 | tf_op jit(solution)/shard_map/all_to_all | solution.py:26
  16.8 23.5 %collective-permute-start.1 = (bf16[144,2048]{1,0:T(8,128)(2,1)S(1)}, bf16[144,2048]{1,0:T(8,128)(2,1)}, u32[]{:S(2)}, u32[]{:S(2)}) collective-permute-start(bf16[144,2048]{1,0:T(8,128)(2,1)S(1)} %copy-done), channel_id=1, source_target_pairs={{0,4},{4,0},{1,5},{5,1},{2,6},{6,2},{3,7},{7,3},{8,12},{12,8},{9,1... | collective-permute-start | bytes 1769480 | tf_op jit(solution)/shard_map/ppermute | solution.py:22
  18.7 23.1 %collective-permute-start = (bf16[144,2048]{1,0:T(8,128)(2,1)S(1)}, bf16[144,2048]{1,0:T(8,128)(2,1)S(1)}, u32[]{:S(2)}, u32[]{:S(2)}) collective-permute-start(bf16[144,2048]{1,0:T(8,128)(2,1)S(1)} %copy-done.1), channel_id=1, source_target_pairs={{0,4},{4,0},{1,5},{5,1},{2,6},{6,2},{3,7},{7,3},{8,12},{12,8},{9,1... | collective-permute-start | bytes 1769480 | tf_op jit(solution)/shard_map/ppermute | solution.py:22
  42.3 14.1 %copy-start.2 = (bf16[144,2048]{1,0:T(8,128)(2,1)S(1)}, bf16[144,2048]{1,0:T(8,128)(2,1)}, u32[]{:S(2)}) copy-start(bf16[144,2048]{1,0:T(8,128)(2,1)} %param.7) | copy-start | bytes 1769476
  43.1 27.3 %all-to-all-start.1 = ((bf16[4,72,384]{2,1,0:T(8,128)(2,1)}), bf16[4,72,384]{2,1,0:T(8,128)(2,1)S(1)}, u32[]{:S(2)}, u32[]{:S(2)}) async-start(bf16[4,72,384]{2,1,0:T(8,128)(2,1)} %bitcast), calls=%async_computation.1 | async-start | bytes 442368 | tf_op jit(solution)/shard_map/all_to_all | solution.py:35
  56.4 29.8 %collective-permute-start.2 = (bf16[144,2048]{1,0:T(8,128)(2,1)S(1)}, bf16[144,2048]{1,0:T(8,128)(2,1)S(1)}, u32[]{:S(2)}, u32[]{:S(2)}) collective-permute-start(bf16[144,2048]{1,0:T(8,128)(2,1)S(1)} %copy-done.2), channel_id=1, source_target_pairs={{0,4},{4,0},{1,5},{5,1},{2,6},{6,2},{3,7},{7,3},{8,12},{12,8},{9,1... | collective-permute-start | bytes 1769480 | tf_op jit(solution)/shard_map/ppermute | solution.py:22

commit v3 on v2

v3 whole, which is shorter than its diff:
```python
import jax
import jax.numpy as jnp
from jax import lax
from jax.sharding import Mesh
from jax.sharding import PartitionSpec as P

X = "x"
PLANE = "plane"
CORE = "core"
TP = "tp"


def exchange(chunks, axes):
    return lax.all_to_all(chunks, axes, split_axis=0, concat_axis=0, tiled=True)


def body(tokens, gate_weight, up_weight, down_weight):
    line, plane, tp = lax.axis_size(X), lax.axis_size(PLANE), lax.axis_size(TP)
    mine, width = tokens.shape
    hidden_width = 2 * gate_weight.shape[0]
    share = hidden_width // tp
    column = plane * mine
    rows = line * column
    swap = [(0, 1), (1, 0)]

    gate_weight, up_weight, down_weight = (
        jnp.concatenate([part, lax.ppermute(part, CORE, swap)], axis=0)
        for part in (gate_weight, up_weight, down_weight)
    )
    block = exchange(jnp.broadcast_to(tokens[None], (plane, mine, width)), PLANE)
    block = block.reshape(column, width)
    block = exchange(jnp.broadcast_to(block[None], (line, column, width)), X)
    block = block.reshape(rows, width)

    contract = (((1,), (1,)), ((), ()))
    gate_part = lax.dot_general(gate_weight, block, contract, preferred_element_type=jnp.float32)
    up_part = lax.dot_general(up_weight, block, contract, preferred_element_type=jnp.float32)
    parts = jnp.concatenate([gate_part, up_part], axis=1).reshape(tp, share, 2 * rows)
    parts = parts.astype(jnp.bfloat16)

    parts, down_weight = lax.optimization_barrier((parts, down_weight))
    down_weights = [down_weight] + [
        lax.ppermute(down_weight, X, [((i + step) % line, i) for i in range(line)])
        for step in range(1, line)
    ]
    parts = exchange(parts, TP)
    sums = jnp.sum(parts.astype(jnp.float32), axis=0)
    quarter = (jax.nn.silu(sums[:, :rows]) * sums[:, rows:]).astype(jnp.bfloat16)
    quarter = quarter.reshape(share, line, column).transpose(1, 0, 2)
    spread = jnp.broadcast_to(quarter[:, None], (line, tp, share, column))
    hidden = exchange(spread.reshape(line * tp, share, column), (X, TP))
    hidden = hidden.reshape(line, hidden_width, column)

    here = lax.axis_index(X)
    hidden = jnp.concatenate(
        [
            lax.dynamic_index_in_dim(hidden, lax.rem(here + step, line), 0, keepdims=False)
            for step in range(line)
        ],
        axis=0,
    )
    terms = lax.dot_general(
        hidden,
        jnp.concatenate(down_weights, axis=0),
        (((0,), (0,)), ((), ())),
        preferred_element_type=jnp.float32,
    ).astype(jnp.bfloat16)
    terms = exchange(terms.reshape(plane, mine, width), PLANE)
    return jnp.sum(terms.astype(jnp.float32), axis=0).astype(jnp.bfloat16)


def solution(mesh):
    line, cores = 4, 2
    fsdp, tp = mesh.devices.shape
    fine = Mesh(
        mesh.devices.reshape(line, fsdp // (line * cores), cores, tp), (X, PLANE, CORE, TP)
    )
    placed = P((X, PLANE, CORE), TP)
    return jax.shard_map(
        body, mesh=fine, in_specs=(placed,) * 4, out_specs=placed, check_vma=False
    )
```

time: 117 us -> 137 us (1.17)
  the two profiles are of different devices: /device:TPU:8 before, /device:TPU:1 now
where the time goes in v3:
time: 137 us; the launch traced here: 134 us
  starting transfers between devices  60.2 us (44%)
  waiting for transfers between devices  46.6 us (34%)
  blocking collectives  14.9 us (11%)
  matrix products  6.03 us (4%)
  local copies, waits for them, and re-layouts  4.2 us (3%)
  other arithmetic  1.79 us (1%)
    all_to_all x4, waiting for transfers between devices, exchange(): return lax.all_to_all(chunks, axes, split_axis=0, concat_axis=0, tiled=True)  46.6 us
    all_to_all x4, starting transfers between devices, exchange(): return lax.all_to_all(chunks, axes, split_axis=0, concat_axis=0, tiled=True)  40 us
    all_to_all x1, blocking collectives, exchange(): return lax.all_to_all(chunks, axes, split_axis=0, concat_axis=0, tiled=True)  14.9 us
    ppermute x3, starting transfers between devices, body(): lax.ppermute(part, CORE, swap)  11.8 us
    ppermute x3, starting transfers between devices, body(): lax.ppermute(down_weight, X, [((i + step) % line, i) for i in range(line)])  8.41 us
  transfers between devices with their start and end apart: 10, of which 4 were waited for; matrix products, arithmetic and copies ran while one was open for 3% of the time, Pallas kernels for 0%

profile of v3, /device:TPU:1, one launch (start us, length us, event | category | flops | bytes accessed | tf_op | source)
XLA Modules:
  0.0 134.0 jit_solution(4355744282437103813)
XLA Ops:
  0.0 1.5 %broadcast_in_dim.8 = bf16[24,2,2048]{2,1,0:T(2,128)(2,1)} broadcast(bf16[2,2048]{1,0:T(2,128)(2,1)} %param.4), dimensions={1,2} | broadcast | bytes 204800 | tf_op jit(solution)/shard_map/broadcast_in_dim | solution.py:30
  1.5 11.5 %all-to-all-start = ((bf16[24,2,2048]{2,1,0:T(2,128)(2,1)}), bf16[24,2,2048]{2,1,0:T(2,128)(2,1)S(1)}, u32[]{:S(2)}, u32[]{:S(2)}) async-start(bf16[24,2,2048]{2,1,0:T(2,128)(2,1)} %broadcast_in_dim.8), calls=%async_computation | async-start | bytes 393216 | tf_op jit(solution)/shard_map/all_to_all | solution.py:14
  13.0 4.7 %collective-permute-start.2 = (bf16[144,2048]{1,0:T(8,128)(2,1)}, bf16[144,2048]{1,0:T(8,128)(2,1)S(1)}, u32[]{:S(2)}, u32[]{:S(2)}) collective-permute-start(bf16[144,2048]{1,0:T(8,128)(2,1)} %param.7), channel_id=1, source_target_pairs={{0,4},{4,0},{1,5},{5,1},{2,6},{6,2},{3,7},{7,3},{8,12},{12,8},{9,1... | collective-permute-start | bytes 1769480 | tf_op jit(solution)/shard_map/ppermute | solution.py:27
  17.8 1.9 %collective-permute-start = (bf16[144,2048]{1,0:T(8,128)(2,1)}, bf16[144,2048]{1,0:T(8,128)(2,1)}, u32[]{:S(2)}, u32[]{:S(2)}) collective-permute-start(bf16[144,2048]{1,0:T(8,128)(2,1)} %param.5), channel_id=1, source_target_pairs={{0,4},{4,0},{1,5},{5,1},{2,6},{6,2},{3,7},{7,3},{8,12},{12,8},{9,1... | collective-permute-start | bytes 1769480 | tf_op jit(solution)/shard_map/ppermute | solution.py:27
  19.7 2.3 %all-to-all-done = bf16[24,2,2048]{2,1,0:T(2,128)(2,1)S(1)} async-done(((bf16[24,2,2048]{2,1,0:T(2,128)(2,1)}), bf16[24,2,2048]{2,1,0:T(2,128)(2,1)S(1)}, u32[]{:S(2)}, u32[]{:S(2)}) %all-to-all-start) | async-done | bytes 196640 | tf_op jit(solution)/shard_map/all_to_all | solution.py:14
  22.0 0.1 broadcast_in_dim.9
  22.1 0.0 copy-start
  22.1 1.0 broadcast_in_dim.10
  23.1 4.1 %all-to-all-start.1 = ((bf16[4,48,2048]{2,1,0:T(8,128)(2,1)}), bf16[4,48,2048]{2,1,0:T(8,128)(2,1)S(1)}, u32[]{:S(2)}, u32[]{:S(2)}) async-start(bf16[4,48,2048]{2,1,0:T(8,128)(2,1)} %broadcast_in_dim.10), calls=%async_computation.1 | async-start | bytes 1572864 | tf_op jit(solution)/shard_map/all_to_all | solution.py:14
  27.2 5.1 %collective-permute-start.1 = (bf16[144,2048]{1,0:T(8,128)(2,1)}, bf16[144,2048]{1,0:T(8,128)(2,1)}, u32[]{:S(2)}, u32[]{:S(2)}) collective-permute-start(bf16[144,2048]{1,0:T(8,128)(2,1)} %param.6), channel_id=1, source_target_pairs={{0,4},{4,0},{1,5},{5,1},{2,6},{6,2},{3,7},{7,3},{8,12},{12,8},{9,1... | collective-permute-start | bytes 1769480 | tf_op jit(solution)/shard_map/ppermute | solution.py:27
  32.4 0.0 collective-permute-done.2
  32.4 0.0 copy-done
  32.4 0.1 pad_maximum_fusion
  32.5 0.0 collective-permute-done
  32.5 3.5 %all-to-all-done.1 = bf16[4,48,2048]{2,1,0:T(8,128)(2,1)S(1)} async-done(((bf16[4,48,2048]{2,1,0:T(8,128)(2,1)}), bf16[4,48,2048]{2,1,0:T(8,128)(2,1)S(1)}, u32[]{:S(2)}, u32[]{:S(2)}) %all-to-all-start.1) | async-done | bytes 786464 | tf_op jit(solution)/shard_map/all_to_all | solution.py:14
  36.1 1.7 %fusion.22 = bf16[288,192]{1,0:T(8,128)(2,1)S(1)} fusion(bf16[192,2048]{1,0:T(8,128)(2,1)S(1)} %bitcast.19, bf16[144,2048]{1,0:T(8,128)(2,1)} %collective-permute-done, bf16[144,2048]{1,0:T(8,128)(2,1)} %param.5), kind=kOutput, calls=%fused_computation.19 | convolution fusion | flops 228907008 | bytes 2076672 | tf_op jit(solution)/shard_map/dot_general | solution.py:36
  37.8 0.0 collective-permute-done.1
  37.8 1.7 %fusion.19 = bf16[288,192]{1,0:T(8,128)(2,1)S(1)} fusion(bf16[192,2048]{1,0:T(8,128)(2,1)S(1)} %bitcast.20, bf16[144,2048]{1,0:T(8,128)(2,1)} %collective-permute-done.1, bf16[144,2048]{1,0:T(8,128)(2,1)} %param.6), kind=kOutput, calls=%fused_computation.18 | convolution fusion | flops 228907008 | bytes 2076672 | tf_op jit(solution)/shard_map/dot_general | solution.py:37
  39.5 0.8 pad_maximum_fusion.1
  40.3 14.8 %all-to-all-start.2 = ((bf16[4,72,384]{2,1,0:T(8,128)(2,1)}), bf16[4,72,384]{2,1,0:T(8,128)(2,1)S(1)}, u32[]{:S(2)}, u32[]{:S(2)}) async-start(bf16[4,72,384]{2,1,0:T(8,128)(2,1)} %bitcast.1), calls=%async_computation.2 | async-start | bytes 442368 | tf_op jit(solution)/shard_map/all_to_all | solution.py:14
  55.1 2.2 %collective-permute-start.5 = (bf16[288,2048]{1,0:T(8,128)(2,1)S(1)}, bf16[288,2048]{1,0:T(8,128)(2,1)S(1)}, u32[]{:S(2)}, u32[]{:S(2)}) collective-permute-start(bf16[288,2048]{1,0:T(8,128)(2,1)S(1)} %pad_maximum_fusion), channel_id=1, source_target_pairs={{576,0},{0,192},{192,384},{384,576},{577,1},{1,193},{193,385},{385... | collective-permute-start | bytes 3538952 | tf_op jit(solution)/shard_map/ppermute | solution.py:43
  57.3 3.7 %collective-permute-start.4 = (bf16[288,2048]{1,0:T(8,128)(2,1)S(1)}, bf16[288,2048]{1,0:T(8,128)(2,1)}, u32[]{:S(2)}, u32[]{:S(2)}) collective-permute-start(bf16[288,2048]{1,0:T(8,128)(2,1)S(1)} %pad_maximum_fusion), channel_id=1, source_target_pairs={{384,0},{576,192},{0,384},{192,576},{385,1},{577,193},{1,385},{193... | collective-permute-start | bytes 3538952 | tf_op jit(solution)/shard_map/ppermute | solution.py:43
  61.0 2.5 %collective-permute-start.3 = (bf16[288,2048]{1,0:T(8,128)(2,1)S(1)}, bf16[288,2048]{1,0:T(8,128)(2,1)}, u32[]{:S(2)}, u32[]{:S(2)}) collective-permute-start(bf16[288,2048]{1,0:T(8,128)(2,1)S(1)} %pad_maximum_fusion), channel_id=1, source_target_pairs={{192,0},{384,192},{576,384},{0,576},{193,1},{385,193},{577,385},{1... | collective-permute-start | bytes 3538952 | tf_op jit(solution)/shard_map/ppermute | solution.py:43
  63.6 1.7 %all-to-all-done.2 = bf16[4,72,384]{2,1,0:T(8,128)(2,1)S(1)} async-done(((bf16[4,72,384]{2,1,0:T(8,128)(2,1)}), bf16[4,72,384]{2,1,0:T(8,128)(2,1)S(1)}, u32[]{:S(2)}, u32[]{:S(2)}) %all-to-all-start.2) | async-done | bytes 221216 | tf_op jit(solution)/shard_map/all_to_all | solution.py:14
  65.3 0.1 fusion.25
  65.4 0.1 copy.10
  65.5 0.7 broadcast_in_dim.22
  66.2 9.5 %all-to-all-start.3 = ((bf16[16,72,48]{1,2,0:T(8,128)(2,1)}), bf16[16,72,48]{1,2,0:T(8,128)(2,1)S(1)}, u32[]{:S(2)}, u32[]{:S(2)}) async-start(bf16[16,72,48]{1,2,0:T(8,128)(2,1)} %bitcast.4), calls=%async_computation.3 | async-start | bytes 393216 | tf_op jit(solution)/shard_map/all_to_all | solution.py:14
  75.8 39.1 %all-to-all-done.3 = bf16[16,72,48]{1,2,0:T(8,128)(2,1)S(1)} async-done(((bf16[16,72,48]{1,2,0:T(8,128)(2,1)}), bf16[16,72,48]{1,2,0:T(8,128)(2,1)S(1)}, u32[]{:S(2)}, u32[]{:S(2)}) %all-to-all-start.3) | async-done | bytes 110624 | tf_op jit(solution)/shard_map/all_to_all | solution.py:14
  114.8 0.1 copy.11
  114.9 0.2 reshape.23
  115.1 0.3 constant_dynamic-slice_fusion
  115.4 0.1 concatenate.23
  115.6 0.0 collective-permute-done.5
  115.6 0.0 collective-permute-done.4
  115.6 0.0 collective-permute-done.3
  115.6 2.6 %fusion.8 = bf16[48,2048]{1,0:T(8,128)(2,1)S(1)} fusion(bf16[1152,48]{0,1:T(8,128)(2,1)S(1)} %concatenate.23, bf16[288,2048]{1,0:T(8,128)(2,1)S(1)} %collective-permute-done.5, bf16[288,2048]{1,0:T(8,128)(2,1)} %collective-permute-done.4, bf16[288,2048]{1,0:T(8,128)(2,1)} %collective-permute-done.3, bf16[288,2048]{1,0:T(8,128)(2,1)S(1)} %pad_maximum_fusion), kind=kOutput, calls=%fused_computation.8 | convolution fusion | flops 245465088 | bytes 5025792 | tf_op jit(solution)/shard_map/dot_general | solution.py:62
  118.2 0.1 reshape.24
  118.3 14.9 %all_to_all.25 = bf16[24,2,2048]{2,1,0:T(2,128)(2,1)S(1)} all-to-all(bf16[24,2,2048]{2,1,0:T(2,128)(2,1)S(1)} %reshape.24), channel_id=1, replica_groups=mesh['x'=4,'plane'=24,'core'=2,'tp'=4] {'plane'}, dimensions={0} | all-to-all | bytes 393216 | tf_op jit(solution)/shard_map/all_to_all | solution.py:14
  133.3 0.8 reduce_sum.22
  (3 shorter events, 0.1 us)
Async XLA Ops:
  1.5 20.5 %all-to-all-start = ((bf16[24,2,2048]{2,1,0:T(2,128)(2,1)}), bf16[24,2,2048]{2,1,0:T(2,128)(2,1)S(1)}, u32[]{:S(2)}, u32[]{:S(2)}) async-start(bf16[24,2,2048]{2,1,0:T(2,128)(2,1)} %broadcast_in_dim.8), calls=%async_computation | async-start | bytes 393216 | tf_op jit(solution)/shard_map/all_to_all | solution.py:14
  13.0 19.4 %collective-permute-start.2 = (bf16[144,2048]{1,0:T(8,128)(2,1)}, bf16[144,2048]{1,0:T(8,128)(2,1)S(1)}, u32[]{:S(2)}, u32[]{:S(2)}) collective-permute-start(bf16[144,2048]{1,0:T(8,128)(2,1)} %param.7), channel_id=1, source_target_pairs={{0,4},{4,0},{1,5},{5,1},{2,6},{6,2},{3,7},{7,3},{8,12},{12,8},{9,1... | collective-permute-start | bytes 1769480 | tf_op jit(solution)/shard_map/ppermute | solution.py:27
  17.8 14.8 %collective-permute-start = (bf16[144,2048]{1,0:T(8,128)(2,1)}, bf16[144,2048]{1,0:T(8,128)(2,1)}, u32[]{:S(2)}, u32[]{:S(2)}) collective-permute-start(bf16[144,2048]{1,0:T(8,128)(2,1)} %param.5), channel_id=1, source_target_pairs={{0,4},{4,0},{1,5},{5,1},{2,6},{6,2},{3,7},{7,3},{8,12},{12,8},{9,1... | collective-permute-start | bytes 1769480 | tf_op jit(solution)/shard_map/ppermute | solution.py:27
  22.1 10.3 %copy-start = (bf16[144,2048]{1,0:T(8,128)(2,1)S(1)}, bf16[144,2048]{1,0:T(8,128)(2,1)}, u32[]{:S(2)}) copy-start(bf16[144,2048]{1,0:T(8,128)(2,1)} %param.7) | copy-start | bytes 1769476
  23.1 13.0 %all-to-all-start.1 = ((bf16[4,48,2048]{2,1,0:T(8,128)(2,1)}), bf16[4,48,2048]{2,1,0:T(8,128)(2,1)S(1)}, u32[]{:S(2)}, u32[]{:S(2)}) async-start(bf16[4,48,2048]{2,1,0:T(8,128)(2,1)} %broadcast_in_dim.10), calls=%async_computation.1 | async-start | bytes 1572864 | tf_op jit(solution)/shard_map/all_to_all | solution.py:14
  27.2 10.6 %collective-permute-start.1 = (bf16[144,2048]{1,0:T(8,128)(2,1)}, bf16[144,2048]{1,0:T(8,128)(2,1)}, u32[]{:S(2)}, u32[]{:S(2)}) collective-permute-start(bf16[144,2048]{1,0:T(8,128)(2,1)} %param.6), channel_id=1, source_target_pairs={{0,4},{4,0},{1,5},{5,1},{2,6},{6,2},{3,7},{7,3},{8,12},{12,8},{9,1... | collective-permute-start | bytes 1769480 | tf_op jit(solution)/shard_map/ppermute | solution.py:27
  40.3 24.9 %all-to-all-start.2 = ((bf16[4,72,384]{2,1,0:T(8,128)(2,1)}), bf16[4,72,384]{2,1,0:T(8,128)(2,1)S(1)}, u32[]{:S(2)}, u32[]{:S(2)}) async-start(bf16[4,72,384]{2,1,0:T(8,128)(2,1)} %bitcast.1), calls=%async_computation.2 | async-start | bytes 442368 | tf_op jit(solution)/shard_map/all_to_all | solution.py:14
  55.1 60.5 %collective-permute-start.5 = (bf16[288,2048]{1,0:T(8,128)(2,1)S(1)}, bf16[288,2048]{1,0:T(8,128)(2,1)S(1)}, u32[]{:S(2)}, u32[]{:S(2)}) collective-permute-start(bf16[288,2048]{1,0:T(8,128)(2,1)S(1)} %pad_maximum_fusion), channel_id=1, source_target_pairs={{576,0},{0,192},{192,384},{384,576},{577,1},{1,193},{193,385},{385... | collective-permute-start | bytes 3538952 | tf_op jit(solution)/shard_map/ppermute | solution.py:43
  57.3 58.3 %collective-permute-start.4 = (bf16[288,2048]{1,0:T(8,128)(2,1)S(1)}, bf16[288,2048]{1,0:T(8,128)(2,1)}, u32[]{:S(2)}, u32[]{:S(2)}) collective-permute-start(bf16[288,2048]{1,0:T(8,128)(2,1)S(1)} %pad_maximum_fusion), channel_id=1, source_target_pairs={{384,0},{576,192},{0,384},{192,576},{385,1},{577,193},{1,385},{193... | collective-permute-start | bytes 3538952 | tf_op jit(solution)/shard_map/ppermute | solution.py:43
  61.0 54.6 %collective-permute-start.3 = (bf16[288,2048]{1,0:T(8,128)(2,1)S(1)}, bf16[288,2048]{1,0:T(8,128)(2,1)}, u32[]{:S(2)}, u32[]{:S(2)}) collective-permute-start(bf16[288,2048]{1,0:T(8,128)(2,1)S(1)} %pad_maximum_fusion), channel_id=1, source_target_pairs={{192,0},{384,192},{576,384},{0,576},{193,1},{385,193},{577,385},{1... | collective-permute-start | bytes 3538952 | tf_op jit(solution)/shard_map/ppermute | solution.py:43
  66.2 48.6 %all-to-all-start.3 = ((bf16[16,72,48]{1,2,0:T(8,128)(2,1)}), bf16[16,72,48]{1,2,0:T(8,128)(2,1)S(1)}, u32[]{:S(2)}, u32[]{:S(2)}) async-start(bf16[16,72,48]{1,2,0:T(8,128)(2,1)} %bitcast.4), calls=%async_computation.3 | async-start | bytes 393216 | tf_op jit(solution)/shard_map/all_to_all | solution.py:14

commit v4 on v3

v4 whole, which is shorter than its diff:
```python
import functools

import jax
import jax.numpy as jnp
from jax import lax
from jax.experimental import pallas as pl
from jax.experimental.pallas import tpu as pltpu
from jax.sharding import Mesh
from jax.sharding import PartitionSpec as P

X = "x"
PLANE = "plane"
CORE = "core"
TP = "tp"


def exchange(chunks, axes):
    return lax.all_to_all(chunks, axes, split_axis=0, concat_axis=0, tiled=True)


def down_kernel(line, here_ref, hidden_ref, *refs):
    weights, out_ref = refs[:-1], refs[-1]
    tp = hidden_ref.shape[0] // line
    half = tp // 2
    total = jnp.zeros(out_ref.shape, jnp.float32)
    for step in range(line):
        first = lax.rem(here_ref[0] + step, line) * tp
        for part in range(2):
            units = jnp.concatenate(
                [hidden_ref[first + part * half + i] for i in range(half)], axis=1
            )
            total += jnp.dot(
                units, weights[2 * step + part][...], preferred_element_type=jnp.float32
            )
    out_ref[...] = total.astype(out_ref.dtype)


def down_product(hidden, weights, here, line):
    column, width = hidden.shape[1], weights[0].shape[1]
    units = hidden.shape[0] * hidden.shape[2]
    vmem = pl.BlockSpec(memory_space=pltpu.VMEM)
    return pl.pallas_call(
        functools.partial(down_kernel, line),
        out_shape=jax.ShapeDtypeStruct((column, width), jnp.bfloat16),
        in_specs=[pl.BlockSpec(memory_space=pltpu.SMEM)] + [vmem] * (1 + len(weights)),
        out_specs=vmem,
        cost_estimate=pl.CostEstimate(
            flops=2 * column * units * width,
            bytes_accessed=2 * (units * width + column * width + column * units),
            transcendentals=0,
        ),
        compiler_params=pltpu.CompilerParams(vmem_limit_bytes=16 * 2**20),
    )(here.reshape(1), hidden, *weights)


def body(tokens, gate_weight, up_weight, down_weight):
    line, plane, tp = lax.axis_size(X), lax.axis_size(PLANE), lax.axis_size(TP)
    mine, width = tokens.shape
    hidden_width = 2 * gate_weight.shape[0]
    share = hidden_width // tp
    column = plane * mine
    rows = line * column
    swap = [(0, 1), (1, 0)]

    block = jnp.broadcast_to(tokens[None], (plane, mine, width))
    block = exchange(block, PLANE)
    gate_weights = (gate_weight, lax.ppermute(gate_weight, CORE, swap))
    up_weights = (up_weight, lax.ppermute(up_weight, CORE, swap))

    block, down_weight, gate_other = lax.optimization_barrier((block, down_weight, gate_weights[1]))
    gate_weights = (gate_weight, gate_other)
    block = block.reshape(column, width)
    block = exchange(jnp.broadcast_to(block[None], (line, column, width)), X)
    block = block.reshape(rows, width)
    down_weights = [down_weight] + [
        lax.ppermute(down_weight, X, [((i + step) % line, i) for i in range(line)])
        for step in range(1, line)
    ]
    down_weights = [
        part for own in down_weights for part in (own, lax.ppermute(own, CORE, swap))
    ]

    contract = (((1,), (1,)), ((), ()))
    parts = jnp.concatenate(
        [
            jnp.concatenate(
                [
                    lax.dot_general(weight, block, contract, preferred_element_type=jnp.float32)
                    for weight in pair
                ],
                axis=1,
            )
            for pair in zip(gate_weights, up_weights)
        ],
        axis=0,
    )
    parts = parts.reshape(tp, share, 2 * rows).astype(jnp.bfloat16)
    parts = exchange(parts, TP)
    sums = jnp.sum(parts.astype(jnp.float32), axis=0)
    quarter = (jax.nn.silu(sums[:, :rows]) * sums[:, rows:]).astype(jnp.bfloat16)
    quarter = quarter.T.reshape(line, 1, column, share)
    spread = jnp.broadcast_to(quarter, (line, tp, column, share))
    hidden = exchange(spread.reshape(line * tp, column, share), (X, TP))
    terms = down_product(hidden, down_weights, lax.axis_index(X), line)
    terms = exchange(terms.reshape(plane, mine, width), PLANE)
    return jnp.sum(terms.astype(jnp.float32), axis=0).astype(jnp.bfloat16)


def solution(mesh):
    line, cores = 4, 2
    fsdp, tp = mesh.devices.shape
    fine = Mesh(
        mesh.devices.reshape(line, fsdp // (line * cores), cores, tp), (X, PLANE, CORE, TP)
    )
    placed = P((X, PLANE, CORE), TP)
    return jax.shard_map(
        body, mesh=fine, in_specs=(placed,) * 4, out_specs=placed, check_vma=False
    )
```

time: 137 us -> 123 us (0.90); the launches traced: 134 us -> 122 us
  waiting for transfers between devices: 46.6 us -> 14 us
  blocking collectives: 14.9 us -> 27.5 us
  starting transfers between devices: 60.2 us -> 68.2 us
  Pallas kernels: 0 us -> 2.24 us
    all_to_all x4 -> x3, waiting for transfers between devices: 46.6 us -> 14 us  [exchange(): return lax.all_to_all(chunks, axes, split_axis=0, concat_axis=0, tiled=True)]
    ppermute x3 -> x6, starting transfers between devices: 11.8 us -> 24.9 us  [the longest x1 12.4 us: body(): gate_weights = (gate_weight, lax.ppermute(gate_weight, CORE, swap))]
    all_to_all x1 -> x2, blocking collectives: 14.9 us -> 27.5 us  [exchange(): return lax.all_to_all(chunks, axes, split_axis=0, concat_axis=0, tiled=True)]
    all_to_all x4 -> x3, starting transfers between devices: 40 us -> 33.5 us  [exchange(): return lax.all_to_all(chunks, axes, split_axis=0, concat_axis=0, tiled=True)]
    pallas_call x0 -> x1, Pallas kernels: none -> 2.24 us  [down_product(): pl.pallas_call(functools.partial(down_kernel, line), out_shape=jax.ShapeD...]
    ppermute x3, starting transfers between devices: 8.41 us -> 9.79 us  [body(): lax.ppermute(down_weight, X, [((i + step) % line, i) for i in range(line)])]
    dot_general x3 -> x4, matrix products: 6.03 us -> 4.93 us  [body(): lax.dot_general(weight, block, contract, preferred_element_type=jnp.float32)]
  transfers between devices with their start and end apart: 10 -> 12, of which waited for: 4 -> 2; matrix products, arithmetic and copies ran while one was open for 3% -> 6% of each run, Pallas kernels for 0% -> 0%
where the time goes in v4:
time: 123 us; the launch traced here: 122 us
  starting transfers between devices  68.2 us (55%)
  blocking collectives  27.5 us (22%)
  waiting for transfers between devices  14 us (11%)
  matrix products  4.93 us (4%)
  local copies, waits for them, and re-layouts  3.57 us (3%)
  Pallas kernels  2.24 us (2%)
  other arithmetic  1.69 us (1%)
    all_to_all x3, starting transfers between devices, exchange(): return lax.all_to_all(chunks, axes, split_axis=0, concat_axis=0, tiled=True)  33.5 us
    all_to_all x2, blocking collectives, exchange(): return lax.all_to_all(chunks, axes, split_axis=0, concat_axis=0, tiled=True)  27.5 us
    all_to_all x3, waiting for transfers between devices, exchange(): return lax.all_to_all(chunks, axes, split_axis=0, concat_axis=0, tiled=True)  14 us
    ppermute x1, starting transfers between devices, body(): gate_weights = (gate_weight, lax.ppermute(gate_weight, CORE, swap))  12.4 us
    ppermute x3, starting transfers between devices, body(): lax.ppermute(down_weight, X, [((i + step) % line, i) for i in range(line)])  9.79 us
    ppermute x4, starting transfers between devices, body(): lax.ppermute(own, CORE, swap)  9.28 us
    dot_general x4, matrix products, body(): lax.dot_general(weight, block, contract, preferred_element_type=jnp.float32)  4.93 us
    ppermute x1, starting transfers between devices, body(): up_weights = (up_weight, lax.ppermute(up_weight, CORE, swap))  3.18 us
  transfers between devices with their start and end apart: 12, of which 2 were waited for; matrix products, arithmetic and copies ran while one was open for 6% of the time, Pallas kernels for 0%

profile of v4, /device:TPU:1, one launch (start us, length us, event | category | flops | bytes accessed | tf_op | source)
XLA Modules:
  0.0 122.4 jit_solution(4526911790129272459)
XLA Ops:
  0.0 12.4 %collective-permute-start = (bf16[144,2048]{1,0:T(8,128)(2,1)}, bf16[144,2048]{1,0:T(8,128)(2,1)S(1)}, u32[]{:S(2)}, u32[]{:S(2)}) collective-permute-start(bf16[144,2048]{1,0:T(8,128)(2,1)} %param.5), channel_id=1, source_target_pairs={{0,4},{4,0},{1,5},{5,1},{2,6},{6,2},{3,7},{7,3},{8,12},{12,8},{9,1... | collective-permute-start | bytes 1769480 | tf_op jit(solution)/shard_map/ppermute | solution.py:67
  12.4 0.8 broadcast_in_dim.20
  13.2 12.5 %all_to_all.25 = bf16[24,2,2048]{2,1,0:T(2,128)(2,1)S(1)} all-to-all(bf16[24,2,2048]{2,1,0:T(2,128)(2,1)S(1)} %broadcast_in_dim.20), channel_id=1, replica_groups=mesh['x'=4,'plane'=24,'core'=2,'tp'=4] {'plane'}, dimensions={0} | all-to-all | bytes 393216 | tf_op jit(solution)/shard_map/all_to_all | solution.py:18
  25.7 0.0 collective-permute-done
  25.7 0.0 copy-start.1
  25.7 0.1 broadcast_in_dim.21
  25.8 0.8 copy-done.1
  26.6 1.0 broadcast_in_dim.22
  27.5 0.0 copy-start
  27.5 3.6 %all-to-all-start.1 = ((bf16[4,48,2048]{2,1,0:T(8,128)(2,1)}), bf16[4,48,2048]{2,1,0:T(8,128)(2,1)S(1)}, u32[]{:S(2)}, u32[]{:S(2)}) async-start(bf16[4,48,2048]{2,1,0:T(8,128)(2,1)} %broadcast_in_dim.22), calls=%async_computation.1 | async-start | bytes 1572864 | tf_op jit(solution)/shard_map/all_to_all | solution.py:18
  31.2 3.2 %collective-permute-start.1 = (bf16[144,2048]{1,0:T(8,128)(2,1)}, bf16[144,2048]{1,0:T(8,128)(2,1)}, u32[]{:S(2)}, u32[]{:S(2)}) collective-permute-start(bf16[144,2048]{1,0:T(8,128)(2,1)} %param.6), channel_id=1, source_target_pairs={{0,4},{4,0},{1,5},{5,1},{2,6},{6,2},{3,7},{7,3},{8,12},{12,8},{9,1... | collective-permute-start | bytes 1769480 | tf_op jit(solution)/shard_map/ppermute | solution.py:68
  34.3 0.0 copy-done
  34.4 4.8 %collective-permute-start.3 = (bf16[144,2048]{1,0:T(8,128)(2,1)S(1)}, bf16[144,2048]{1,0:T(8,128)(2,1)S(1)}, u32[]{:S(2)}, u32[]{:S(2)}) collective-permute-start(bf16[144,2048]{1,0:T(8,128)(2,1)S(1)} %copy-done), channel_id=1, source_target_pairs={{192,0},{384,192},{576,384},{0,576},{193,1},{385,193},{577,385},{1... | collective-permute-start | bytes 1769480 | tf_op jit(solution)/shard_map/ppermute | solution.py:76
  39.2 2.5 %collective-permute-start.5 = (bf16[144,2048]{1,0:T(8,128)(2,1)S(1)}, bf16[144,2048]{1,0:T(8,128)(2,1)S(1)}, u32[]{:S(2)}, u32[]{:S(2)}) collective-permute-start(bf16[144,2048]{1,0:T(8,128)(2,1)S(1)} %copy-done), channel_id=1, source_target_pairs={{384,0},{576,192},{0,384},{192,576},{385,1},{577,193},{1,385},{193... | collective-permute-start | bytes 1769480 | tf_op jit(solution)/shard_map/ppermute | solution.py:76
  41.7 2.5 %collective-permute-start.7 = (bf16[144,2048]{1,0:T(8,128)(2,1)S(1)}, bf16[144,2048]{1,0:T(8,128)(2,1)S(1)}, u32[]{:S(2)}, u32[]{:S(2)}) collective-permute-start(bf16[144,2048]{1,0:T(8,128)(2,1)S(1)} %copy-done), channel_id=1, source_target_pairs={{576,0},{0,192},{192,384},{384,576},{577,1},{1,193},{193,385},{385... | collective-permute-start | bytes 1769480 | tf_op jit(solution)/shard_map/ppermute | solution.py:76
  44.2 0.0 all-to-all-done.1
  44.2 1.5 %fusion = bf16[144,192]{1,0:T(8,128)(2,1)S(1)} fusion(bf16[192,2048]{1,0:T(8,128)(2,1)S(1)} %bitcast.21, bf16[144,2048]{1,0:T(8,128)(2,1)} %param.5), kind=kOutput, calls=%fused_computation.4 | convolution fusion | flops 113273856 | bytes 1431552 | tf_op jit(solution)/shard_map/dot_general | solution.py:88
  45.7 0.0 copy-start.2
  45.7 1.5 %fusion.1 = bf16[144,192]{1,0:T(8,128)(2,1)S(1)} fusion(bf16[192,2048]{1,0:T(8,128)(2,1)S(1)} %bitcast.22, bf16[144,2048]{1,0:T(8,128)(2,1)} %param.6), kind=kOutput, calls=%fused_computation.5 | convolution fusion | flops 113273856 | bytes 1431552 | tf_op jit(solution)/shard_map/dot_general | solution.py:88
  47.2 0.0 copy-done.2
  47.2 0.4 convolution_convert_fusion.1
  47.7 0.0 collective-permute-done.1
  47.7 1.5 %fusion.2 = bf16[144,192]{1,0:T(8,128)(2,1)S(1)} fusion(bf16[192,2048]{1,0:T(8,128)(2,1)S(1)} %bitcast.24, bf16[144,2048]{1,0:T(8,128)(2,1)} %collective-permute-done.1), kind=kOutput, calls=%fused_computation.6 | convolution fusion | flops 113273856 | bytes 1431552 | tf_op jit(solution)/shard_map/dot_general | solution.py:88
  49.2 0.8 maximum_maximum_fusion
  50.0 13.8 %all-to-all-start.2 = ((bf16[4,72,384]{2,1,0:T(8,128)(2,1)}), bf16[4,72,384]{2,1,0:T(8,128)(2,1)S(1)}, u32[]{:S(2)}, u32[]{:S(2)}) async-start(bf16[4,72,384]{2,1,0:T(8,128)(2,1)} %bitcast.5), calls=%async_computation.2 | async-start | bytes 442368 | tf_op jit(solution)/shard_map/all_to_all | solution.py:18
  63.7 3.0 %collective-permute-start.2 = (bf16[144,2048]{1,0:T(8,128)(2,1)S(1)}, bf16[144,2048]{1,0:T(8,128)(2,1)S(1)}, u32[]{:S(2)}, u32[]{:S(2)}) collective-permute-start(bf16[144,2048]{1,0:T(8,128)(2,1)S(1)} %copy-done), channel_id=1, source_target_pairs={{0,4},{4,0},{1,5},{5,1},{2,6},{6,2},{3,7},{7,3},{8,12},{12,8},{9,1... | collective-permute-start | bytes 1769480 | tf_op jit(solution)/shard_map/ppermute | solution.py:80
  66.8 0.0 collective-permute-done.3.refs_2_
  66.8 1.9 %collective-permute-start.4 = (bf16[144,2048]{1,0:T(8,128)(2,1)S(1)}, bf16[144,2048]{1,0:T(8,128)(2,1)}, u32[]{:S(2)}, u32[]{:S(2)}) collective-permute-start(bf16[144,2048]{1,0:T(8,128)(2,1)S(1)} %collective-permute-done.3.refs_2_), channel_id=1, source_target_pairs={{0,4},{4,0},{1,5},{5,1},{2,6},{6,2},{3,7},{7,3},{8,12},{12,8},{9,1... | collective-permute-start | bytes 1769480 | tf_op jit(solution)/shard_map/ppermute | solution.py:80
  68.7 0.0 collective-permute-done.5.refs_4_
  68.7 2.4 %collective-permute-start.6 = (bf16[144,2048]{1,0:T(8,128)(2,1)S(1)}, bf16[144,2048]{1,0:T(8,128)(2,1)}, u32[]{:S(2)}, u32[]{:S(2)}) collective-permute-start(bf16[144,2048]{1,0:T(8,128)(2,1)S(1)} %collective-permute-done.5.refs_4_), channel_id=1, source_target_pairs={{0,4},{4,0},{1,5},{5,1},{2,6},{6,2},{3,7},{7,3},{8,12},{12,8},{9,1... | collective-permute-start | bytes 1769480 | tf_op jit(solution)/shard_map/ppermute | solution.py:80
  71.1 0.0 collective-permute-done.7.refs_6_
  71.1 1.9 %collective-permute-start.8 = (bf16[144,2048]{1,0:T(8,128)(2,1)S(1)}, bf16[144,2048]{1,0:T(8,128)(2,1)}, u32[]{:S(2)}, u32[]{:S(2)}) collective-permute-start(bf16[144,2048]{1,0:T(8,128)(2,1)S(1)} %collective-permute-done.7.refs_6_), channel_id=1, source_target_pairs={{0,4},{4,0},{1,5},{5,1},{2,6},{6,2},{3,7},{7,3},{8,12},{12,8},{9,1... | collective-permute-start | bytes 1769480 | tf_op jit(solution)/shard_map/ppermute | solution.py:80
  73.1 0.9 all-to-all-done.2
  74.0 0.1 fusion.4
  74.1 0.1 copy.6
  74.2 0.7 broadcast_in_dim.24
  74.9 16.1 %all-to-all-start.3 = ((bf16[16,48,72]{2,1,0:T(8,128)(2,1)}), bf16[16,48,72]{2,1,0:T(8,128)(2,1)S(1)}, u32[]{:S(2)}, u32[]{:S(2)}) async-start(bf16[16,48,72]{2,1,0:T(8,128)(2,1)} %bitcast.8), calls=%async_computation.3 | async-start | bytes 393216 | tf_op jit(solution)/shard_map/all_to_all | solution.py:18
  91.1 0.0 collective-permute-done.2.refs_1_
  91.1 0.0 collective-permute-done.4.refs_3_
  91.1 0.0 collective-permute-done.6.refs_5_
  91.1 0.0 collective-permute-done.8.refs_7_
  91.1 13.0 %all-to-all-done.3.hidden_ref = bf16[16,48,72]{2,1,0:T(8,128)(2,1)S(1)} async-done(((bf16[16,48,72]{2,1,0:T(8,128)(2,1)}), bf16[16,48,72]{2,1,0:T(8,128)(2,1)S(1)}, u32[]{:S(2)}, u32[]{:S(2)}) %all-to-all-start.3) | async-done | bytes 110624 | tf_op jit(solution)/shard_map/all_to_all | solution.py:18
  104.2 2.2 %shard_map.46 = bf16[48,2048]{1,0:T(8,128)(2,1)S(1)} custom-call(s32[1]{0:T(128)} %bitcast.here_ref, bf16[16,48,72]{2,1,0:T(8,128)(2,1)S(1)} %all-to-all-done.3.hidden_ref, bf16[144,2048]{1,0:T(8,128)(2,1)S(1)} %copy-done, bf16[144,2048]{1,0:T(8,128)(2,1)S(1)} %collective-permute-done.2.refs_1_, bf16[144,2048]{1,0:T(8,128)(2,1)S(1)} %collective-permute-done.3.refs_2_, ...), custom_call_target="tpu_custom_call" | custom-call | flops 226492416 | bytes 5025792 | tf_op jit(solution)/shard_map/pallas_call | solution.py:42
  106.4 0.1 reshape.21
  106.6 15.0 %all_to_all.26 = bf16[24,2,2048]{2,1,0:T(2,128)(2,1)S(1)} all-to-all(bf16[24,2,2048]{2,1,0:T(2,128)(2,1)S(1)} %reshape.21), channel_id=1, replica_groups=mesh['x'=4,'plane'=24,'core'=2,'tp'=4] {'plane'}, dimensions={0} | all-to-all | bytes 393216 | tf_op jit(solution)/shard_map/all_to_all | solution.py:18
  121.6 0.8 reduce_sum.22
  (1 shorter events, 0.0 us)
Async XLA Ops:
  0.0 25.7 %collective-permute-start = (bf16[144,2048]{1,0:T(8,128)(2,1)}, bf16[144,2048]{1,0:T(8,128)(2,1)S(1)}, u32[]{:S(2)}, u32[]{:S(2)}) collective-permute-start(bf16[144,2048]{1,0:T(8,128)(2,1)} %param.5), channel_id=1, source_target_pairs={{0,4},{4,0},{1,5},{5,1},{2,6},{6,2},{3,7},{7,3},{8,12},{12,8},{9,1... | collective-permute-start | bytes 1769480 | tf_op jit(solution)/shard_map/ppermute | solution.py:67
  25.7 0.8 copy-start.1
  27.5 6.8 %copy-start = (bf16[144,2048]{1,0:T(8,128)(2,1)S(1)}, bf16[144,2048]{1,0:T(8,128)(2,1)}, u32[]{:S(2)}) copy-start(bf16[144,2048]{1,0:T(8,128)(2,1)} %refs_0_) | copy-start | bytes 1769476
  27.5 16.6 %all-to-all-start.1 = ((bf16[4,48,2048]{2,1,0:T(8,128)(2,1)}), bf16[4,48,2048]{2,1,0:T(8,128)(2,1)S(1)}, u32[]{:S(2)}, u32[]{:S(2)}) async-start(bf16[4,48,2048]{2,1,0:T(8,128)(2,1)} %broadcast_in_dim.22), calls=%async_computation.1 | async-start | bytes 1572864 | tf_op jit(solution)/shard_map/all_to_all | solution.py:18
  31.2 16.5 %collective-permute-start.1 = (bf16[144,2048]{1,0:T(8,128)(2,1)}, bf16[144,2048]{1,0:T(8,128)(2,1)}, u32[]{:S(2)}, u32[]{:S(2)}) collective-permute-start(bf16[144,2048]{1,0:T(8,128)(2,1)} %param.6), channel_id=1, source_target_pairs={{0,4},{4,0},{1,5},{5,1},{2,6},{6,2},{3,7},{7,3},{8,12},{12,8},{9,1... | collective-permute-start | bytes 1769480 | tf_op jit(solution)/shard_map/ppermute | solution.py:68
  34.4 32.4 %collective-permute-start.3 = (bf16[144,2048]{1,0:T(8,128)(2,1)S(1)}, bf16[144,2048]{1,0:T(8,128)(2,1)S(1)}, u32[]{:S(2)}, u32[]{:S(2)}) collective-permute-start(bf16[144,2048]{1,0:T(8,128)(2,1)S(1)} %copy-done), channel_id=1, source_target_pairs={{192,0},{384,192},{576,384},{0,576},{193,1},{385,193},{577,385},{1... | collective-permute-start | bytes 1769480 | tf_op jit(solution)/shard_map/ppermute | solution.py:76
  39.2 29.5 %collective-permute-start.5 = (bf16[144,2048]{1,0:T(8,128)(2,1)S(1)}, bf16[144,2048]{1,0:T(8,128)(2,1)S(1)}, u32[]{:S(2)}, u32[]{:S(2)}) collective-permute-start(bf16[144,2048]{1,0:T(8,128)(2,1)S(1)} %copy-done), channel_id=1, source_target_pairs={{384,0},{576,192},{0,384},{192,576},{385,1},{577,193},{1,385},{193... | collective-permute-start | bytes 1769480 | tf_op jit(solution)/shard_map/ppermute | solution.py:76
  41.7 29.5 %collective-permute-start.7 = (bf16[144,2048]{1,0:T(8,128)(2,1)S(1)}, bf16[144,2048]{1,0:T(8,128)(2,1)S(1)}, u32[]{:S(2)}, u32[]{:S(2)}) collective-permute-start(bf16[144,2048]{1,0:T(8,128)(2,1)S(1)} %copy-done), channel_id=1, source_target_pairs={{576,0},{0,192},{192,384},{384,576},{577,1},{1,193},{193,385},{385... | collective-permute-start | bytes 1769480 | tf_op jit(solution)/shard_map/ppermute | solution.py:76
  45.7 1.6 %copy-start.2 = (bf16[144,2048]{1,0:T(8,128)(2,1)S(1)}, bf16[144,2048]{1,0:T(8,128)(2,1)}, u32[]{:S(2)}) copy-start(bf16[144,2048]{1,0:T(8,128)(2,1)} %copy-done.1) | copy-start | bytes 1769476
  50.0 24.0 %all-to-all-start.2 = ((bf16[4,72,384]{2,1,0:T(8,128)(2,1)}), bf16[4,72,384]{2,1,0:T(8,128)(2,1)S(1)}, u32[]{:S(2)}, u32[]{:S(2)}) async-start(bf16[4,72,384]{2,1,0:T(8,128)(2,1)} %bitcast.5), calls=%async_computation.2 | async-start | bytes 442368 | tf_op jit(solution)/shard_map/all_to_all | solution.py:18
  63.7 27.3 %collective-permute-start.2 = (bf16[144,2048]{1,0:T(8,128)(2,1)S(1)}, bf16[144,2048]{1,0:T(8,128)(2,1)S(1)}, u32[]{:S(2)}, u32[]{:S(2)}) collective-permute-start(bf16[144,2048]{1,0:T(8,128)(2,1)S(1)} %copy-done), channel_id=1, source_target_pairs={{0,4},{4,0},{1,5},{5,1},{2,6},{6,2},{3,7},{7,3},{8,12},{12,8},{9,1... | collective-permute-start | bytes 1769480 | tf_op jit(solution)/shard_map/ppermute | solution.py:80
  66.8 24.3 %collective-permute-start.4 = (bf16[144,2048]{1,0:T(8,128)(2,1)S(1)}, bf16[144,2048]{1,0:T(8,128)(2,1)}, u32[]{:S(2)}, u32[]{:S(2)}) collective-permute-start(bf16[144,2048]{1,0:T(8,128)(2,1)S(1)} %collective-permute-done.3.refs_2_), channel_id=1, source_target_pairs={{0,4},{4,0},{1,5},{5,1},{2,6},{6,2},{3,7},{7,3},{8,12},{12,8},{9,1... | collective-permute-start | bytes 1769480 | tf_op jit(solution)/shard_map/ppermute | solution.py:80
  68.7 22.4 %collective-permute-start.6 = (bf16[144,2048]{1,0:T(8,128)(2,1)S(1)}, bf16[144,2048]{1,0:T(8,128)(2,1)}, u32[]{:S(2)}, u32[]{:S(2)}) collective-permute-start(bf16[144,2048]{1,0:T(8,128)(2,1)S(1)} %collective-permute-done.5.refs_4_), channel_id=1, source_target_pairs={{0,4},{4,0},{1,5},{5,1},{2,6},{6,2},{3,7},{7,3},{8,12},{12,8},{9,1... | collective-permute-start | bytes 1769480 | tf_op jit(solution)/shard_map/ppermute | solution.py:80
  71.1 20.0 %collective-permute-start.8 = (bf16[144,2048]{1,0:T(8,128)(2,1)S(1)}, bf16[144,2048]{1,0:T(8,128)(2,1)}, u32[]{:S(2)}, u32[]{:S(2)}) collective-permute-start(bf16[144,2048]{1,0:T(8,128)(2,1)S(1)} %collective-permute-done.7.refs_6_), channel_id=1, source_target_pairs={{0,4},{4,0},{1,5},{5,1},{2,6},{6,2},{3,7},{7,3},{8,12},{12,8},{9,1... | collective-permute-start | bytes 1769480 | tf_op jit(solution)/shard_map/ppermute | solution.py:80
  74.9 29.2 %all-to-all-start.3 = ((bf16[16,48,72]{2,1,0:T(8,128)(2,1)}), bf16[16,48,72]{2,1,0:T(8,128)(2,1)S(1)}, u32[]{:S(2)}, u32[]{:S(2)}) async-start(bf16[16,48,72]{2,1,0:T(8,128)(2,1)} %bitcast.8), calls=%async_computation.3 | async-start | bytes 393216 | tf_op jit(solution)/shard_map/all_to_all | solution.py:18

commit v5 on v4

--- a/solution.py
+++ b/solution.py
@@ -16,6 +16,40 @@
 
 def exchange(chunks, axes):
     return lax.all_to_all(chunks, axes, split_axis=0, concat_axis=0, tiled=True)
+
+
+def up_kernel(block_ref, *refs):
+    stacks, out_ref = refs[:-1], refs[-1]
+    share, each = out_ref.shape[1], out_ref.shape[0] // len(stacks)
+    for at, stack_ref in enumerate(stacks):
+        terms = lax.dot_general(
+            stack_ref[...],
+            block_ref[...],
+            (((1,), (1,)), ((), ())),
+            preferred_element_type=jnp.float32,
+        )
+        for i in range(each):
+            gate = terms[i * share : (i + 1) * share]
+            up = terms[(each + i) * share : (each + i + 1) * share]
+            out_ref[at * each + i] = jnp.concatenate([gate, up], axis=1).astype(out_ref.dtype)
+
+
+def up_product(block, stacks, tp):
+    rows, width = block.shape
+    units = sum(stack.shape[0] for stack in stacks)
+    vmem = pl.BlockSpec(memory_space=pltpu.VMEM)
+    return pl.pallas_call(
+        up_kernel,
+        out_shape=jax.ShapeDtypeStruct((tp, units // 2 // tp, 2 * rows), jnp.bfloat16),
+        in_specs=[vmem] * (1 + len(stacks)),
+        out_specs=vmem,
+        cost_estimate=pl.CostEstimate(
+            flops=2 * rows * units * width,
+            bytes_accessed=2 * (units * width + rows * width + rows * units),
+            transcendentals=0,
+        ),
+        compiler_params=pltpu.CompilerParams(vmem_limit_bytes=16 * 2**20),
+    )(block, *stacks)
 
 
 def down_kernel(line, here_ref, hidden_ref, *refs):
@@ -62,40 +96,23 @@
     rows = line * column
     swap = [(0, 1), (1, 0)]
 
-    block = jnp.broadcast_to(tokens[None], (plane, mine, width))
-    block = exchange(block, PLANE)
-    gate_weights = (gate_weight, lax.ppermute(gate_weight, CORE, swap))
-    up_weights = (up_weight, lax.ppermute(up_weight, CORE, swap))
+    stack = jnp.concatenate([gate_weight, up_weight], axis=0)
+    other_stack = lax.ppermute(stack, CORE, swap)
+    block = exchange(jnp.broadcast_to(tokens[None], (plane, mine, width)), PLANE)
 
-    block, down_weight, gate_other = lax.optimization_barrier((block, down_weight, gate_weights[1]))
-    gate_weights = (gate_weight, gate_other)
     block = block.reshape(column, width)
     block = exchange(jnp.broadcast_to(block[None], (line, column, width)), X)
     block = block.reshape(rows, width)
-    down_weights = [down_weight] + [
+    gathered = [
         lax.ppermute(down_weight, X, [((i + step) % line, i) for i in range(line)])
         for step in range(1, line)
     ]
+
+    block, *gathered = lax.optimization_barrier((block, *gathered))
+    parts = exchange(up_product(block, (stack, other_stack), tp), TP)
     down_weights = [
-        part for own in down_weights for part in (own, lax.ppermute(own, CORE, swap))
+        part for own in (down_weight, *gathered) for part in (own, lax.ppermute(own, CORE, swap))
     ]
-
-    contract = (((1,), (1,)), ((), ()))
-    parts = jnp.concatenate(
-        [
-            jnp.concatenate(
-                [
-                    lax.dot_general(weight, block, contract, preferred_element_type=jnp.float32)
-                    for weight in pair
-                ],
-                axis=1,
-            )
-            for pair in zip(gate_weights, up_weights)
-        ],
-        axis=0,
-    )
-    parts = parts.reshape(tp, share, 2 * rows).astype(jnp.bfloat16)
-    parts = exchange(parts, TP)
     sums = jnp.sum(parts.astype(jnp.float32), axis=0)
     quarter = (jax.nn.silu(sums[:, :rows]) * sums[:, rows:]).astype(jnp.bfloat16)
     quarter = quarter.T.reshape(line, 1, column, share)

time: 123 us -> 133 us (1.081)
  waiting for transfers between devices: 14 us -> 42.6 us
  starting transfers between devices: 68.2 us -> 59.1 us
  blocking collectives: 27.5 us -> 20.6 us
  matrix products: 4.93 us -> 0 us
  Pallas kernels: 2.24 us -> 3.99 us
    ppermute x3, waiting for transfers between devices: 0.01 us -> 19.8 us  [body(): lax.ppermute(down_weight, X, [((i + step) % line, i) for i in range(line)])]
    all_to_all x3 -> x4, waiting for transfers between devices: 14 us -> 22.8 us  [exchange(): return lax.all_to_all(chunks, axes, split_axis=0, concat_axis=0, tiled=True)]
    all_to_all x2 -> x1, blocking collectives: 27.5 us -> 20.6 us  [exchange(): return lax.all_to_all(chunks, axes, split_axis=0, concat_axis=0, tiled=True)]
    dot_general x4 -> x0, matrix products: 4.93 us -> none  [body(): lax.dot_general(weight, block, contract, preferred_element_type=jnp.float32)]
    all_to_all x3 -> x4, starting transfers between devices: 33.5 us -> 29.6 us  [exchange(): return lax.all_to_all(chunks, axes, split_axis=0, concat_axis=0, tiled=True)]
    ppermute x2 -> x1, starting transfers between devices: 15.6 us -> 12.4 us  [body(): other_stack = lax.ppermute(stack, CORE, swap)]
    ppermute x3, starting transfers between devices: 9.79 us -> 7.21 us  [body(): lax.ppermute(down_weight, X, [((i + step) % line, i) for i in range(line)])]
    pallas_call x0 -> x1, Pallas kernels: none -> 1.57 us  [up_product(): pl.pallas_call(up_kernel, out_shape=jax.ShapeDtypeStruct((tp, units // 2...]
  transfers between devices with their start and end apart: 12 -> 12, of which waited for: 2 -> 7; matrix products, arithmetic and copies ran while one was open for 6% -> 2% of each run, Pallas kernels for 0% -> 0%
where the time goes in v5:
time: 133 us; the launch traced here: 131 us
  starting transfers between devices  59.1 us (44%)
  waiting for transfers between devices  42.6 us (32%)
  blocking collectives  20.6 us (15%)
  local copies, waits for them, and re-layouts  4.07 us (3%)
  Pallas kernels  3.99 us (3%)
    all_to_all x4, starting transfers between devices, exchange(): return lax.all_to_all(chunks, axes, split_axis=0, concat_axis=0, tiled=True)  29.6 us
    all_to_all x4, waiting for transfers between devices, exchange(): return lax.all_to_all(chunks, axes, split_axis=0, concat_axis=0, tiled=True)  22.8 us
    all_to_all x1, blocking collectives, exchange(): return lax.all_to_all(chunks, axes, split_axis=0, concat_axis=0, tiled=True)  20.6 us
    ppermute x3, waiting for transfers between devices, body(): lax.ppermute(down_weight, X, [((i + step) % line, i) for i in range(line)])  19.8 us
    ppermute x1, starting transfers between devices, body(): other_stack = lax.ppermute(stack, CORE, swap)  12.4 us
    ppermute x4, starting transfers between devices, body(): lax.ppermute(own, CORE, swap)  9.86 us
    ppermute x3, starting transfers between devices, body(): lax.ppermute(down_weight, X, [((i + step) % line, i) for i in range(line)])  7.21 us
  transfers between devices with their start and end apart: 12, of which 7 were waited for; matrix products, arithmetic and copies ran while one was open for 2% of the time, Pallas kernels for 0%

profile of v5, /device:TPU:1, one launch (start us, length us, event | category | flops | bytes accessed | tf_op | source)
XLA Modules:
  0.0 131.5 jit_solution(5629070532908795855)
XLA Ops:
  0.0 0.0 copy-start
  0.0 0.0 copy-start.1
  0.0 1.2 constant_dynamic-update-slice_fusion.1
  1.2 0.1 copy-done
  1.3 12.4 %collective-permute-start.3 = (bf16[288,2048]{1,0:T(8,128)(2,1)S(1)}, bf16[288,2048]{1,0:T(8,128)(2,1)S(1)}, u32[]{:S(2)}, u32[]{:S(2)}) collective-permute-start(bf16[288,2048]{1,0:T(8,128)(2,1)S(1)} %constant_dynamic-update-slice_fusion.refs_0_), channel_id=1, source_target_pairs={{0,4},{4,0},{1,5},{5,1},{2,6},{6,2},{3,7},{7,3},{8,12},{12,8},{9,1... | collective-permute-start | bytes 3538952 | tf_op jit(solution)/shard_map/ppermute | solution.py:100
  13.7 0.0 copy-done.1
  13.7 0.8 broadcast_in_dim.20
  14.5 3.8 %all-to-all-start = ((bf16[24,2,2048]{2,1,0:T(2,128)(2,1)}), bf16[24,2,2048]{2,1,0:T(2,128)(2,1)S(1)}, u32[]{:S(2)}, u32[]{:S(2)}) async-start(bf16[24,2,2048]{2,1,0:T(2,128)(2,1)} %broadcast_in_dim.20), calls=%async_computation | async-start | bytes 393216 | tf_op jit(solution)/shard_map/all_to_all | solution.py:18
  18.4 2.2 %collective-permute-start = (bf16[144,2048]{1,0:T(8,128)(2,1)}, bf16[144,2048]{1,0:T(8,128)(2,1)}, u32[]{:S(2)}, u32[]{:S(2)}) collective-permute-start(bf16[144,2048]{1,0:T(8,128)(2,1)} %refs_0_.1), channel_id=1, source_target_pairs={{192,0},{384,192},{576,384},{0,576},{193,1},{385,193},{577,385},{1... | collective-permute-start | bytes 1769480 | tf_op jit(solution)/shard_map/ppermute | solution.py:107
  20.6 2.4 %collective-permute-start.1 = (bf16[144,2048]{1,0:T(8,128)(2,1)}, bf16[144,2048]{1,0:T(8,128)(2,1)}, u32[]{:S(2)}, u32[]{:S(2)}) collective-permute-start(bf16[144,2048]{1,0:T(8,128)(2,1)} %refs_0_.1), channel_id=1, source_target_pairs={{384,0},{576,192},{0,384},{192,576},{385,1},{577,193},{1,385},{193... | collective-permute-start | bytes 1769480 | tf_op jit(solution)/shard_map/ppermute | solution.py:107
  23.0 2.5 %collective-permute-start.2 = (bf16[144,2048]{1,0:T(8,128)(2,1)}, bf16[144,2048]{1,0:T(8,128)(2,1)}, u32[]{:S(2)}, u32[]{:S(2)}) collective-permute-start(bf16[144,2048]{1,0:T(8,128)(2,1)} %refs_0_.1), channel_id=1, source_target_pairs={{576,0},{0,192},{192,384},{384,576},{577,1},{1,193},{193,385},{385... | collective-permute-start | bytes 1769480 | tf_op jit(solution)/shard_map/ppermute | solution.py:107
  25.6 2.3 %all-to-all-done = bf16[24,2,2048]{2,1,0:T(2,128)(2,1)S(1)} async-done(((bf16[24,2,2048]{2,1,0:T(2,128)(2,1)}), bf16[24,2,2048]{2,1,0:T(2,128)(2,1)S(1)}, u32[]{:S(2)}, u32[]{:S(2)}) %all-to-all-start) | async-done | bytes 196640 | tf_op jit(solution)/shard_map/all_to_all | solution.py:18
  27.9 0.1 broadcast_in_dim.21
  27.9 1.0 broadcast_in_dim.22
  28.9 3.5 %all-to-all-start.1 = ((bf16[4,48,2048]{2,1,0:T(8,128)(2,1)}), bf16[4,48,2048]{2,1,0:T(8,128)(2,1)S(1)}, u32[]{:S(2)}, u32[]{:S(2)}) async-start(bf16[4,48,2048]{2,1,0:T(8,128)(2,1)} %broadcast_in_dim.22), calls=%async_computation.1 | async-start | bytes 1572864 | tf_op jit(solution)/shard_map/all_to_all | solution.py:18
  32.4 3.1 %collective-permute-done.refs_2_ = bf16[144,2048]{1,0:T(8,128)(2,1)} collective-permute-done((bf16[144,2048]{1,0:T(8,128)(2,1)}, bf16[144,2048]{1,0:T(8,128)(2,1)}, u32[]{:S(2)}, u32[]{:S(2)}) %collective-permute-start) | collective-permute-done | bytes 589856 | tf_op jit(solution)/shard_map/ppermute | solution.py:107
  35.5 3.2 %collective-permute-done.1.refs_4_ = bf16[144,2048]{1,0:T(8,128)(2,1)} collective-permute-done((bf16[144,2048]{1,0:T(8,128)(2,1)}, bf16[144,2048]{1,0:T(8,128)(2,1)}, u32[]{:S(2)}, u32[]{:S(2)}) %collective-permute-start.1) | collective-permute-done | bytes 589856 | tf_op jit(solution)/shard_map/ppermute | solution.py:107
  38.7 13.5 %collective-permute-done.2.refs_6_ = bf16[144,2048]{1,0:T(8,128)(2,1)} collective-permute-done((bf16[144,2048]{1,0:T(8,128)(2,1)}, bf16[144,2048]{1,0:T(8,128)(2,1)}, u32[]{:S(2)}, u32[]{:S(2)}) %collective-permute-start.2) | collective-permute-done | bytes 589856 | tf_op jit(solution)/shard_map/ppermute | solution.py:107
  52.2 7.4 %all-to-all-done.1 = bf16[4,48,2048]{2,1,0:T(8,128)(2,1)S(1)} async-done(((bf16[4,48,2048]{2,1,0:T(8,128)(2,1)}), bf16[4,48,2048]{2,1,0:T(8,128)(2,1)S(1)}, u32[]{:S(2)}, u32[]{:S(2)}) %all-to-all-start.1) | async-done | bytes 786464 | tf_op jit(solution)/shard_map/all_to_all | solution.py:18
  59.6 0.0 collective-permute-done.3.refs_1_
  59.6 1.6 %shard_map.46 = bf16[4,72,384]{2,1,0:T(8,128)(2,1)} custom-call(bf16[192,2048]{1,0:T(8,128)(2,1)S(1)} %bitcast.6, bf16[288,2048]{1,0:T(8,128)(2,1)S(1)} %constant_dynamic-update-slice_fusion.refs_0_, bf16[288,2048]{1,0:T(8,128)(2,1)S(1)} %collective-permute-done.3.refs_1_), custom_call_target="tpu_custom_call" | custom-call | flops 452984832 | bytes 3366912 | tf_op jit(solution)/shard_map/pallas_call | solution.py:41
  61.2 13.0 %all-to-all-start.2 = ((bf16[4,72,384]{2,1,0:T(8,128)(2,1)}), bf16[4,72,384]{2,1,0:T(8,128)(2,1)S(1)}, u32[]{:S(2)}, u32[]{:S(2)}) async-start(bf16[4,72,384]{2,1,0:T(8,128)(2,1)} %shard_map.46), calls=%async_computation.2 | async-start | bytes 442368 | tf_op jit(solution)/shard_map/all_to_all | solution.py:18
  74.2 3.6 %collective-permute-start.4 = (bf16[144,2048]{1,0:T(8,128)(2,1)}, bf16[144,2048]{1,0:T(8,128)(2,1)S(1)}, u32[]{:S(2)}, u32[]{:S(2)}) collective-permute-start(bf16[144,2048]{1,0:T(8,128)(2,1)} %refs_0_.1), channel_id=1, source_target_pairs={{0,4},{4,0},{1,5},{5,1},{2,6},{6,2},{3,7},{7,3},{8,12},{12,8},{9,1... | collective-permute-start | bytes 1769480 | tf_op jit(solution)/shard_map/ppermute | solution.py:114
  77.8 1.9 %collective-permute-start.5 = (bf16[144,2048]{1,0:T(8,128)(2,1)}, bf16[144,2048]{1,0:T(8,128)(2,1)S(1)}, u32[]{:S(2)}, u32[]{:S(2)}) collective-permute-start(bf16[144,2048]{1,0:T(8,128)(2,1)} %collective-permute-done.refs_2_), channel_id=1, source_target_pairs={{0,4},{4,0},{1,5},{5,1},{2,6},{6,2},{3,7},{7,3},{8,12},{12,8},{9,1... | collective-permute-start | bytes 1769480 | tf_op jit(solution)/shard_map/ppermute | solution.py:114
  79.8 2.4 %collective-permute-start.6 = (bf16[144,2048]{1,0:T(8,128)(2,1)}, bf16[144,2048]{1,0:T(8,128)(2,1)S(1)}, u32[]{:S(2)}, u32[]{:S(2)}) collective-permute-start(bf16[144,2048]{1,0:T(8,128)(2,1)} %collective-permute-done.1.refs_4_), channel_id=1, source_target_pairs={{0,4},{4,0},{1,5},{5,1},{2,6},{6,2},{3,7},{7,3},{8,12},{12,8},{9,1... | collective-permute-start | bytes 1769480 | tf_op jit(solution)/shard_map/ppermute | solution.py:114
  82.2 1.9 %collective-permute-start.7 = (bf16[144,2048]{1,0:T(8,128)(2,1)}, bf16[144,2048]{1,0:T(8,128)(2,1)S(1)}, u32[]{:S(2)}, u32[]{:S(2)}) collective-permute-start(bf16[144,2048]{1,0:T(8,128)(2,1)} %collective-permute-done.2.refs_6_), channel_id=1, source_target_pairs={{0,4},{4,0},{1,5},{5,1},{2,6},{6,2},{3,7},{7,3},{8,12},{12,8},{9,1... | collective-permute-start | bytes 1769480 | tf_op jit(solution)/shard_map/ppermute | solution.py:114
  84.1 0.4 all-to-all-done.2
  84.5 0.1 fusion.1
  84.6 0.1 copy.6
  84.7 0.7 broadcast_in_dim.24
  85.5 9.3 %all-to-all-start.3 = ((bf16[16,48,72]{2,1,0:T(8,128)(2,1)}), bf16[16,48,72]{2,1,0:T(8,128)(2,1)S(1)}, u32[]{:S(2)}, u32[]{:S(2)}) async-start(bf16[16,48,72]{2,1,0:T(8,128)(2,1)} %bitcast.4), calls=%async_computation.3 | async-start | bytes 393216 | tf_op jit(solution)/shard_map/all_to_all | solution.py:18
  94.8 0.0 collective-permute-done.4.refs_1_
  94.8 0.0 collective-permute-done.5.refs_3_
  94.8 0.0 collective-permute-done.6.refs_5_
  94.8 0.0 collective-permute-done.7.refs_7_
  94.8 12.7 %all-to-all-done.3.hidden_ref = bf16[16,48,72]{2,1,0:T(8,128)(2,1)S(1)} async-done(((bf16[16,48,72]{2,1,0:T(8,128)(2,1)}), bf16[16,48,72]{2,1,0:T(8,128)(2,1)S(1)}, u32[]{:S(2)}, u32[]{:S(2)}) %all-to-all-start.3) | async-done | bytes 110624 | tf_op jit(solution)/shard_map/all_to_all | solution.py:18
  107.5 2.4 %shard_map.47 = bf16[48,2048]{1,0:T(8,128)(2,1)S(1)} custom-call(s32[1]{0:T(128)} %bitcast.here_ref, bf16[16,48,72]{2,1,0:T(8,128)(2,1)S(1)} %all-to-all-done.3.hidden_ref, bf16[144,2048]{1,0:T(8,128)(2,1)} %refs_0_.1, bf16[144,2048]{1,0:T(8,128)(2,1)S(1)} %collective-permute-done.4.refs_1_, bf16[144,2048]{1,0:T(8,128)(2,1)} %collective-permute-done.refs_2_, ...), custom_call_target="tpu_custom_call" | custom-call | flops 226492416 | bytes 5025792 | tf_op jit(solution)/shard_map/pallas_call | solution.py:76
  109.9 0.1 reshape.19
  110.1 20.6 %all_to_all.25 = bf16[24,2,2048]{2,1,0:T(2,128)(2,1)S(1)} all-to-all(bf16[24,2,2048]{2,1,0:T(2,128)(2,1)S(1)} %reshape.19), channel_id=1, replica_groups=mesh['x'=4,'plane'=24,'core'=2,'tp'=4] {'plane'}, dimensions={0} | all-to-all | bytes 393216 | tf_op jit(solution)/shard_map/all_to_all | solution.py:18
  130.7 0.8 reduce_sum.22
  (2 shorter events, 0.1 us)
Async XLA Ops:
  0.0 1.2 copy-start
  0.0 13.7 %copy-start.1 = (bf16[2,2048]{1,0:T(2,128)(2,1)S(1)}, bf16[2,2048]{1,0:T(2,128)(2,1)}, u32[]{:S(2)}) copy-start(bf16[2,2048]{1,0:T(2,128)(2,1)} %param.4) | copy-start | bytes 24580
  1.3 58.3 %collective-permute-start.3 = (bf16[288,2048]{1,0:T(8,128)(2,1)S(1)}, bf16[288,2048]{1,0:T(8,128)(2,1)S(1)}, u32[]{:S(2)}, u32[]{:S(2)}) collective-permute-start(bf16[288,2048]{1,0:T(8,128)(2,1)S(1)} %constant_dynamic-update-slice_fusion.refs_0_), channel_id=1, source_target_pairs={{0,4},{4,0},{1,5},{5,1},{2,6},{6,2},{3,7},{7,3},{8,12},{12,8},{9,1... | collective-permute-start | bytes 3538952 | tf_op jit(solution)/shard_map/ppermute | solution.py:100
  14.5 13.4 %all-to-all-start = ((bf16[24,2,2048]{2,1,0:T(2,128)(2,1)}), bf16[24,2,2048]{2,1,0:T(2,128)(2,1)S(1)}, u32[]{:S(2)}, u32[]{:S(2)}) async-start(bf16[24,2,2048]{2,1,0:T(2,128)(2,1)} %broadcast_in_dim.20), calls=%async_computation | async-start | bytes 393216 | tf_op jit(solution)/shard_map/all_to_all | solution.py:18
  18.4 17.2 %collective-permute-start = (bf16[144,2048]{1,0:T(8,128)(2,1)}, bf16[144,2048]{1,0:T(8,128)(2,1)}, u32[]{:S(2)}, u32[]{:S(2)}) collective-permute-start(bf16[144,2048]{1,0:T(8,128)(2,1)} %refs_0_.1), channel_id=1, source_target_pairs={{192,0},{384,192},{576,384},{0,576},{193,1},{385,193},{577,385},{1... | collective-permute-start | bytes 1769480 | tf_op jit(solution)/shard_map/ppermute | solution.py:107
  20.6 18.1 %collective-permute-start.1 = (bf16[144,2048]{1,0:T(8,128)(2,1)}, bf16[144,2048]{1,0:T(8,128)(2,1)}, u32[]{:S(2)}, u32[]{:S(2)}) collective-permute-start(bf16[144,2048]{1,0:T(8,128)(2,1)} %refs_0_.1), channel_id=1, source_target_pairs={{384,0},{576,192},{0,384},{192,576},{385,1},{577,193},{1,385},{193... | collective-permute-start | bytes 1769480 | tf_op jit(solution)/shard_map/ppermute | solution.py:107
  23.0 29.2 %collective-permute-start.2 = (bf16[144,2048]{1,0:T(8,128)(2,1)}, bf16[144,2048]{1,0:T(8,128)(2,1)}, u32[]{:S(2)}, u32[]{:S(2)}) collective-permute-start(bf16[144,2048]{1,0:T(8,128)(2,1)} %refs_0_.1), channel_id=1, source_target_pairs={{576,0},{0,192},{192,384},{384,576},{577,1},{1,193},{193,385},{385... | collective-permute-start | bytes 1769480 | tf_op jit(solution)/shard_map/ppermute | solution.py:107
  28.9 30.7 %all-to-all-start.1 = ((bf16[4,48,2048]{2,1,0:T(8,128)(2,1)}), bf16[4,48,2048]{2,1,0:T(8,128)(2,1)S(1)}, u32[]{:S(2)}, u32[]{:S(2)}) async-start(bf16[4,48,2048]{2,1,0:T(8,128)(2,1)} %broadcast_in_dim.22), calls=%async_computation.1 | async-start | bytes 1572864 | tf_op jit(solution)/shard_map/all_to_all | solution.py:18
  61.2 23.3 %all-to-all-start.2 = ((bf16[4,72,384]{2,1,0:T(8,128)(2,1)}), bf16[4,72,384]{2,1,0:T(8,128)(2,1)S(1)}, u32[]{:S(2)}, u32[]{:S(2)}) async-start(bf16[4,72,384]{2,1,0:T(8,128)(2,1)} %shard_map.46), calls=%async_computation.2 | async-start | bytes 442368 | tf_op jit(solution)/shard_map/all_to_all | solution.py:18
  74.2 20.5 %collective-permute-start.4 = (bf16[144,2048]{1,0:T(8,128)(2,1)}, bf16[144,2048]{1,0:T(8,128)(2,1)S(1)}, u32[]{:S(2)}, u32[]{:S(2)}) collective-permute-start(bf16[144,2048]{1,0:T(8,128)(2,1)} %refs_0_.1), channel_id=1, source_target_pairs={{0,4},{4,0},{1,5},{5,1},{2,6},{6,2},{3,7},{7,3},{8,12},{12,8},{9,1... | collective-permute-start | bytes 1769480 | tf_op jit(solution)/shard_map/ppermute | solution.py:114
  77.8 16.9 %collective-permute-start.5 = (bf16[144,2048]{1,0:T(8,128)(2,1)}, bf16[144,2048]{1,0:T(8,128)(2,1)S(1)}, u32[]{:S(2)}, u32[]{:S(2)}) collective-permute-start(bf16[144,2048]{1,0:T(8,128)(2,1)} %collective-permute-done.refs_2_), channel_id=1, source_target_pairs={{0,4},{4,0},{1,5},{5,1},{2,6},{6,2},{3,7},{7,3},{8,12},{12,8},{9,1... | collective-permute-start | bytes 1769480 | tf_op jit(solution)/shard_map/ppermute | solution.py:114
  79.8 15.0 %collective-permute-start.6 = (bf16[144,2048]{1,0:T(8,128)(2,1)}, bf16[144,2048]{1,0:T(8,128)(2,1)S(1)}, u32[]{:S(2)}, u32[]{:S(2)}) collective-permute-start(bf16[144,2048]{1,0:T(8,128)(2,1)} %collective-permute-done.1.refs_4_), channel_id=1, source_target_pairs={{0,4},{4,0},{1,5},{5,1},{2,6},{6,2},{3,7},{7,3},{8,12},{12,8},{9,1... | collective-permute-start | bytes 1769480 | tf_op jit(solution)/shard_map/ppermute | solution.py:114
  82.2 12.6 %collective-permute-start.7 = (bf16[144,2048]{1,0:T(8,128)(2,1)}, bf16[144,2048]{1,0:T(8,128)(2,1)S(1)}, u32[]{:S(2)}, u32[]{:S(2)}) collective-permute-start(bf16[144,2048]{1,0:T(8,128)(2,1)} %collective-permute-done.2.refs_6_), channel_id=1, source_target_pairs={{0,4},{4,0},{1,5},{5,1},{2,6},{6,2},{3,7},{7,3},{8,12},{12,8},{9,1... | collective-permute-start | bytes 1769480 | tf_op jit(solution)/shard_map/ppermute | solution.py:114
  85.5 22.1 %all-to-all-start.3 = ((bf16[16,48,72]{2,1,0:T(8,128)(2,1)}), bf16[16,48,72]{2,1,0:T(8,128)(2,1)S(1)}, u32[]{:S(2)}, u32[]{:S(2)}) async-start(bf16[16,48,72]{2,1,0:T(8,128)(2,1)} %bitcast.4), calls=%async_computation.3 | async-start | bytes 393216 | tf_op jit(solution)/shard_map/all_to_all | solution.py:18

commit v6 on v5

--- a/solution.py
+++ b/solution.py
@@ -98,17 +98,14 @@
 
     stack = jnp.concatenate([gate_weight, up_weight], axis=0)
     other_stack = lax.ppermute(stack, CORE, swap)
-    block = exchange(jnp.broadcast_to(tokens[None], (plane, mine, width)), PLANE)
+    block = jnp.broadcast_to(tokens[None], (line * plane, mine, width))
+    block = exchange(block, (X, PLANE)).reshape(rows, width)
 
-    block = block.reshape(column, width)
-    block = exchange(jnp.broadcast_to(block[None], (line, column, width)), X)
-    block = block.reshape(rows, width)
     gathered = [
         lax.ppermute(down_weight, X, [((i + step) % line, i) for i in range(line)])
         for step in range(1, line)
     ]
 
-    block, *gathered = lax.optimization_barrier((block, *gathered))
     parts = exchange(up_product(block, (stack, other_stack), tp), TP)
     down_weights = [
         part for own in (down_weight, *gathered) for part in (own, lax.ppermute(own, CORE, swap))

time: 133 us -> 117 us (0.88)
  waiting for transfers between devices: 42.6 us -> 20.3 us
  starting transfers between devices: 59.1 us -> 65.9 us
  local copies, waits for them, and re-layouts: 4.07 us -> 5.41 us
    ppermute x3, waiting for transfers between devices: 19.8 us -> 0.01 us  [body(): lax.ppermute(down_weight, X, [((i + step) % line, i) for i in range(line)])]
    all_to_all x4 -> x3, starting transfers between devices: 29.6 us -> 40.5 us  [exchange(): return lax.all_to_all(chunks, axes, split_axis=0, concat_axis=0, tiled=True)]
    ppermute x1, starting transfers between devices: 12.4 us -> 3.63 us  [body(): other_stack = lax.ppermute(stack, CORE, swap)]
    ppermute x4, starting transfers between devices: 9.86 us -> 12.4 us  [body(): lax.ppermute(own, CORE, swap)]
    all_to_all x4 -> x3, waiting for transfers between devices: 22.8 us -> 20.2 us  [exchange(): return lax.all_to_all(chunks, axes, split_axis=0, concat_axis=0, tiled=True)]
    reshape x0 -> x1, local copies, waits for them, and re-layouts: none -> 2.26 us  [body(): block = exchange(block, (X, PLANE)).reshape(rows, width)]
    ppermute x3, starting transfers between devices: 7.21 us -> 9.31 us  [body(): lax.ppermute(down_weight, X, [((i + step) % line, i) for i in range(line)])]
  transfers between devices with their start and end apart: 12 -> 11, of which waited for: 7 -> 2; matrix products, arithmetic and copies ran while one was open for 2% -> 3% of each run, Pallas kernels for 0% -> 1%
where the time goes in v6:
time: 117 us; the launch traced here: 116 us
  starting transfers between devices  65.9 us (56%)
  waiting for transfers between devices  20.3 us (17%)
  blocking collectives  19.5 us (17%)
  local copies, waits for them, and re-layouts  5.41 us (5%)
  Pallas kernels  3.97 us (3%)
    all_to_all x3, starting transfers between devices, exchange(): return lax.all_to_all(chunks, axes, split_axis=0, concat_axis=0, tiled=True)  40.5 us
    all_to_all x3, waiting for transfers between devices, exchange(): return lax.all_to_all(chunks, axes, split_axis=0, concat_axis=0, tiled=True)  20.2 us
    all_to_all x1, blocking collectives, exchange(): return lax.all_to_all(chunks, axes, split_axis=0, concat_axis=0, tiled=True)  19.5 us
    ppermute x4, starting transfers between devices, body(): lax.ppermute(own, CORE, swap)  12.4 us
    ppermute x3, starting transfers between devices, body(): lax.ppermute(down_weight, X, [((i + step) % line, i) for i in range(line)])  9.31 us
    ppermute x1, starting transfers between devices, body(): other_stack = lax.ppermute(stack, CORE, swap)  3.63 us
    pallas_call x1, Pallas kernels, down_product(): pl.pallas_call(functools.partial(down_kernel, line), out_shape=jax.ShapeD...  2.42 us
  transfers between devices with their start and end apart: 11, of which 2 were waited for; matrix products, arithmetic and copies ran while one was open for 3% of the time, Pallas kernels for 1%

profile of v6, /device:TPU:1, one launch (start us, length us, event | category | flops | bytes accessed | tf_op | source)
XLA Modules:
  0.0 116.1 jit_solution(15343097316280464002)
XLA Ops:
  0.0 0.0 copy-start
  0.0 2.1 %broadcast_in_dim.6 = bf16[96,2,2048]{2,1,0:T(2,128)(2,1)} broadcast(bf16[2,2048]{1,0:T(2,128)(2,1)} %param.4), dimensions={1,2} | broadcast | bytes 794624 | tf_op jit(solution)/shard_map/broadcast_in_dim | solution.py:101
  2.1 0.0 copy-start.1
  2.1 15.9 %all-to-all-start = ((bf16[96,2,2048]{2,1,0:T(2,128)(2,1)}), bf16[96,2,2048]{2,1,0:T(2,128)(2,1)}, u32[]{:S(2)}, u32[]{:S(2)}) async-start(bf16[96,2,2048]{2,1,0:T(2,128)(2,1)} %broadcast_in_dim.6), calls=%async_computation | async-start | bytes 1572864 | tf_op jit(solution)/shard_map/all_to_all | solution.py:18
  18.0 0.0 copy-done
  18.0 0.0 copy-done.1
  18.1 3.6 %collective-permute-start = (bf16[288,2048]{1,0:T(8,128)(2,1)S(1)}, bf16[288,2048]{1,0:T(8,128)(2,1)S(1)}, u32[]{:S(2)}, u32[]{:S(2)}) collective-permute-start(bf16[288,2048]{1,0:T(8,128)(2,1)S(1)} %constant_dynamic-update-slice_fusion.refs_0_), channel_id=1, source_target_pairs={{0,4},{4,0},{1,5},{5,1},{2,6},{6,2},{3,7},{7,3},{8,12},{12,8},{9,1... | collective-permute-start | bytes 3538952 | tf_op jit(solution)/shard_map/ppermute | solution.py:100
  21.7 4.5 %collective-permute-start.2 = (bf16[144,2048]{1,0:T(8,128)(2,1)}, bf16[144,2048]{1,0:T(8,128)(2,1)}, u32[]{:S(2)}, u32[]{:S(2)}) collective-permute-start(bf16[144,2048]{1,0:T(8,128)(2,1)} %refs_0_.1), channel_id=1, source_target_pairs={{192,0},{384,192},{576,384},{0,576},{193,1},{385,193},{577,385},{1... | collective-permute-start | bytes 1769480 | tf_op jit(solution)/shard_map/ppermute | solution.py:105
  26.2 2.2 %collective-permute-start.4 = (bf16[144,2048]{1,0:T(8,128)(2,1)}, bf16[144,2048]{1,0:T(8,128)(2,1)}, u32[]{:S(2)}, u32[]{:S(2)}) collective-permute-start(bf16[144,2048]{1,0:T(8,128)(2,1)} %refs_0_.1), channel_id=1, source_target_pairs={{384,0},{576,192},{0,384},{192,576},{385,1},{577,193},{1,385},{193... | collective-permute-start | bytes 1769480 | tf_op jit(solution)/shard_map/ppermute | solution.py:105
  28.4 2.7 %collective-permute-start.6 = (bf16[144,2048]{1,0:T(8,128)(2,1)}, bf16[144,2048]{1,0:T(8,128)(2,1)}, u32[]{:S(2)}, u32[]{:S(2)}) collective-permute-start(bf16[144,2048]{1,0:T(8,128)(2,1)} %refs_0_.1), channel_id=1, source_target_pairs={{576,0},{0,192},{192,384},{384,576},{577,1},{1,193},{193,385},{385... | collective-permute-start | bytes 1769480 | tf_op jit(solution)/shard_map/ppermute | solution.py:105
  31.1 7.4 %all-to-all-done = bf16[96,2,2048]{2,1,0:T(2,128)(2,1)} async-done(((bf16[96,2,2048]{2,1,0:T(2,128)(2,1)}), bf16[96,2,2048]{2,1,0:T(2,128)(2,1)}, u32[]{:S(2)}, u32[]{:S(2)}) %all-to-all-start) | async-done | bytes 786464 | tf_op jit(solution)/shard_map/all_to_all | solution.py:18
  38.5 2.3 %reshape.16.block_ref = bf16[192,2048]{1,0:T(8,128)(2,1)S(1)} reshape(bf16[96,2,2048]{2,1,0:T(2,128)(2,1)} %all-to-all-done) | data formatting | bytes 1572864 | tf_op jit(solution)/shard_map/reshape | solution.py:102
  40.8 0.0 collective-permute-done.refs_1_
  40.8 1.6 %shard_map.46 = bf16[4,72,384]{2,1,0:T(8,128)(2,1)} custom-call(bf16[192,2048]{1,0:T(8,128)(2,1)S(1)} %reshape.16.block_ref, bf16[288,2048]{1,0:T(8,128)(2,1)S(1)} %constant_dynamic-update-slice_fusion.refs_0_, bf16[288,2048]{1,0:T(8,128)(2,1)S(1)} %collective-permute-done.refs_1_), custom_call_target="tpu_custom_call" | custom-call | flops 452984832 | bytes 3366912 | tf_op jit(solution)/shard_map/pallas_call | solution.py:41
  42.3 12.4 %all-to-all-start.1 = ((bf16[4,72,384]{2,1,0:T(8,128)(2,1)}), bf16[4,72,384]{2,1,0:T(8,128)(2,1)S(1)}, u32[]{:S(2)}, u32[]{:S(2)}) async-start(bf16[4,72,384]{2,1,0:T(8,128)(2,1)} %shard_map.46), calls=%async_computation.1 | async-start | bytes 442368 | tf_op jit(solution)/shard_map/all_to_all | solution.py:18
  54.8 6.2 %collective-permute-start.1 = (bf16[144,2048]{1,0:T(8,128)(2,1)}, bf16[144,2048]{1,0:T(8,128)(2,1)S(1)}, u32[]{:S(2)}, u32[]{:S(2)}) collective-permute-start(bf16[144,2048]{1,0:T(8,128)(2,1)} %refs_0_.1), channel_id=1, source_target_pairs={{0,4},{4,0},{1,5},{5,1},{2,6},{6,2},{3,7},{7,3},{8,12},{12,8},{9,1... | collective-permute-start | bytes 1769480 | tf_op jit(solution)/shard_map/ppermute | solution.py:111
  61.0 0.0 collective-permute-done.2.refs_2_
  61.0 1.9 %collective-permute-start.3 = (bf16[144,2048]{1,0:T(8,128)(2,1)}, bf16[144,2048]{1,0:T(8,128)(2,1)S(1)}, u32[]{:S(2)}, u32[]{:S(2)}) collective-permute-start(bf16[144,2048]{1,0:T(8,128)(2,1)} %collective-permute-done.2.refs_2_), channel_id=1, source_target_pairs={{0,4},{4,0},{1,5},{5,1},{2,6},{6,2},{3,7},{7,3},{8,12},{12,8},{9,1... | collective-permute-start | bytes 1769480 | tf_op jit(solution)/shard_map/ppermute | solution.py:111
  62.9 0.0 collective-permute-done.4.refs_4_
  62.9 2.4 %collective-permute-start.5 = (bf16[144,2048]{1,0:T(8,128)(2,1)}, bf16[144,2048]{1,0:T(8,128)(2,1)S(1)}, u32[]{:S(2)}, u32[]{:S(2)}) collective-permute-start(bf16[144,2048]{1,0:T(8,128)(2,1)} %collective-permute-done.4.refs_4_), channel_id=1, source_target_pairs={{0,4},{4,0},{1,5},{5,1},{2,6},{6,2},{3,7},{7,3},{8,12},{12,8},{9,1... | collective-permute-start | bytes 1769480 | tf_op jit(solution)/shard_map/ppermute | solution.py:111
  65.4 0.0 collective-permute-done.6.refs_6_
  65.4 1.9 %collective-permute-start.7 = (bf16[144,2048]{1,0:T(8,128)(2,1)}, bf16[144,2048]{1,0:T(8,128)(2,1)S(1)}, u32[]{:S(2)}, u32[]{:S(2)}) collective-permute-start(bf16[144,2048]{1,0:T(8,128)(2,1)} %collective-permute-done.6.refs_6_), channel_id=1, source_target_pairs={{0,4},{4,0},{1,5},{5,1},{2,6},{6,2},{3,7},{7,3},{8,12},{12,8},{9,1... | collective-permute-start | bytes 1769480 | tf_op jit(solution)/shard_map/ppermute | solution.py:111
  67.3 0.0 all-to-all-done.1
  67.3 0.1 fusion.1
  67.4 0.1 copy.6
  67.5 0.7 broadcast_in_dim.15
  68.3 12.2 %all-to-all-start.2 = ((bf16[16,48,72]{2,1,0:T(8,128)(2,1)}), bf16[16,48,72]{2,1,0:T(8,128)(2,1)S(1)}, u32[]{:S(2)}, u32[]{:S(2)}) async-start(bf16[16,48,72]{2,1,0:T(8,128)(2,1)} %bitcast.3), calls=%async_computation.2 | async-start | bytes 393216 | tf_op jit(solution)/shard_map/all_to_all | solution.py:18
  80.5 0.0 collective-permute-done.1.refs_1_
  80.5 0.0 collective-permute-done.3.refs_3_
  80.5 0.0 collective-permute-done.5.refs_5_
  80.5 0.0 collective-permute-done.7.refs_7_
  80.5 12.8 %all-to-all-done.2.hidden_ref = bf16[16,48,72]{2,1,0:T(8,128)(2,1)S(1)} async-done(((bf16[16,48,72]{2,1,0:T(8,128)(2,1)}), bf16[16,48,72]{2,1,0:T(8,128)(2,1)S(1)}, u32[]{:S(2)}, u32[]{:S(2)}) %all-to-all-start.2) | async-done | bytes 110624 | tf_op jit(solution)/shard_map/all_to_all | solution.py:18
  93.3 2.4 %shard_map.47 = bf16[48,2048]{1,0:T(8,128)(2,1)S(1)} custom-call(s32[1]{0:T(128)} %bitcast.here_ref, bf16[16,48,72]{2,1,0:T(8,128)(2,1)S(1)} %all-to-all-done.2.hidden_ref, bf16[144,2048]{1,0:T(8,128)(2,1)} %refs_0_.1, bf16[144,2048]{1,0:T(8,128)(2,1)S(1)} %collective-permute-done.1.refs_1_, bf16[144,2048]{1,0:T(8,128)(2,1)} %collective-permute-done.2.refs_2_, ...), custom_call_target="tpu_custom_call" | custom-call | flops 226492416 | bytes 5025792 | tf_op jit(solution)/shard_map/pallas_call | solution.py:76
  95.8 0.1 reshape.18
  95.9 19.5 %all_to_all.20 = bf16[24,2,2048]{2,1,0:T(2,128)(2,1)S(1)} all-to-all(bf16[24,2,2048]{2,1,0:T(2,128)(2,1)S(1)} %reshape.18), channel_id=1, replica_groups=mesh['x'=4,'plane'=24,'core'=2,'tp'=4] {'plane'}, dimensions={0} | all-to-all | bytes 393216 | tf_op jit(solution)/shard_map/all_to_all | solution.py:18
  115.4 0.8 reduce_sum.22
  (3 shorter events, 0.1 us)
Async XLA Ops:
  0.0 18.0 %copy-start = (bf16[144,2048]{1,0:T(8,128)(2,1)S(1)}, bf16[144,2048]{1,0:T(8,128)(2,1)}, u32[]{:S(2)}) copy-start(bf16[144,2048]{1,0:T(8,128)(2,1)} %param.5) | copy-start | bytes 1769476
  2.1 15.9 %copy-start.1 = (bf16[144,2048]{1,0:T(8,128)(2,1)S(1)}, bf16[144,2048]{1,0:T(8,128)(2,1)}, u32[]{:S(2)}) copy-start(bf16[144,2048]{1,0:T(8,128)(2,1)} %param.6) | copy-start | bytes 1769476
  2.1 36.4 %all-to-all-start = ((bf16[96,2,2048]{2,1,0:T(2,128)(2,1)}), bf16[96,2,2048]{2,1,0:T(2,128)(2,1)}, u32[]{:S(2)}, u32[]{:S(2)}) async-start(bf16[96,2,2048]{2,1,0:T(2,128)(2,1)} %broadcast_in_dim.6), calls=%async_computation | async-start | bytes 1572864 | tf_op jit(solution)/shard_map/all_to_all | solution.py:18
  18.1 22.7 %collective-permute-start = (bf16[288,2048]{1,0:T(8,128)(2,1)S(1)}, bf16[288,2048]{1,0:T(8,128)(2,1)S(1)}, u32[]{:S(2)}, u32[]{:S(2)}) collective-permute-start(bf16[288,2048]{1,0:T(8,128)(2,1)S(1)} %constant_dynamic-update-slice_fusion.refs_0_), channel_id=1, source_target_pairs={{0,4},{4,0},{1,5},{5,1},{2,6},{6,2},{3,7},{7,3},{8,12},{12,8},{9,1... | collective-permute-start | bytes 3538952 | tf_op jit(solution)/shard_map/ppermute | solution.py:100
  21.7 39.3 %collective-permute-start.2 = (bf16[144,2048]{1,0:T(8,128)(2,1)}, bf16[144,2048]{1,0:T(8,128)(2,1)}, u32[]{:S(2)}, u32[]{:S(2)}) collective-permute-start(bf16[144,2048]{1,0:T(8,128)(2,1)} %refs_0_.1), channel_id=1, source_target_pairs={{192,0},{384,192},{576,384},{0,576},{193,1},{385,193},{577,385},{1... | collective-permute-start | bytes 1769480 | tf_op jit(solution)/shard_map/ppermute | solution.py:105
  26.2 36.7 %collective-permute-start.4 = (bf16[144,2048]{1,0:T(8,128)(2,1)}, bf16[144,2048]{1,0:T(8,128)(2,1)}, u32[]{:S(2)}, u32[]{:S(2)}) collective-permute-start(bf16[144,2048]{1,0:T(8,128)(2,1)} %refs_0_.1), channel_id=1, source_target_pairs={{384,0},{576,192},{0,384},{192,576},{385,1},{577,193},{1,385},{193... | collective-permute-start | bytes 1769480 | tf_op jit(solution)/shard_map/ppermute | solution.py:105
  28.4 37.0 %collective-permute-start.6 = (bf16[144,2048]{1,0:T(8,128)(2,1)}, bf16[144,2048]{1,0:T(8,128)(2,1)}, u32[]{:S(2)}, u32[]{:S(2)}) collective-permute-start(bf16[144,2048]{1,0:T(8,128)(2,1)} %refs_0_.1), channel_id=1, source_target_pairs={{576,0},{0,192},{192,384},{384,576},{577,1},{1,193},{193,385},{385... | collective-permute-start | bytes 1769480 | tf_op jit(solution)/shard_map/ppermute | solution.py:105
  42.3 25.0 %all-to-all-start.1 = ((bf16[4,72,384]{2,1,0:T(8,128)(2,1)}), bf16[4,72,384]{2,1,0:T(8,128)(2,1)S(1)}, u32[]{:S(2)}, u32[]{:S(2)}) async-start(bf16[4,72,384]{2,1,0:T(8,128)(2,1)} %shard_map.46), calls=%async_computation.1 | async-start | bytes 442368 | tf_op jit(solution)/shard_map/all_to_all | solution.py:18
  54.8 25.7 %collective-permute-start.1 = (bf16[144,2048]{1,0:T(8,128)(2,1)}, bf16[144,2048]{1,0:T(8,128)(2,1)S(1)}, u32[]{:S(2)}, u32[]{:S(2)}) collective-permute-start(bf16[144,2048]{1,0:T(8,128)(2,1)} %refs_0_.1), channel_id=1, source_target_pairs={{0,4},{4,0},{1,5},{5,1},{2,6},{6,2},{3,7},{7,3},{8,12},{12,8},{9,1... | collective-permute-start | bytes 1769480 | tf_op jit(solution)/shard_map/ppermute | solution.py:111
  61.0 19.5 %collective-permute-start.3 = (bf16[144,2048]{1,0:T(8,128)(2,1)}, bf16[144,2048]{1,0:T(8,128)(2,1)S(1)}, u32[]{:S(2)}, u32[]{:S(2)}) collective-permute-start(bf16[144,2048]{1,0:T(8,128)(2,1)} %collective-permute-done.2.refs_2_), channel_id=1, source_target_pairs={{0,4},{4,0},{1,5},{5,1},{2,6},{6,2},{3,7},{7,3},{8,12},{12,8},{9,1... | collective-permute-start | bytes 1769480 | tf_op jit(solution)/shard_map/ppermute | solution.py:111
  62.9 17.6 %collective-permute-start.5 = (bf16[144,2048]{1,0:T(8,128)(2,1)}, bf16[144,2048]{1,0:T(8,128)(2,1)S(1)}, u32[]{:S(2)}, u32[]{:S(2)}) collective-permute-start(bf16[144,2048]{1,0:T(8,128)(2,1)} %collective-permute-done.4.refs_4_), channel_id=1, source_target_pairs={{0,4},{4,0},{1,5},{5,1},{2,6},{6,2},{3,7},{7,3},{8,12},{12,8},{9,1... | collective-permute-start | bytes 1769480 | tf_op jit(solution)/shard_map/ppermute | solution.py:111
  65.4 15.2 %collective-permute-start.7 = (bf16[144,2048]{1,0:T(8,128)(2,1)}, bf16[144,2048]{1,0:T(8,128)(2,1)S(1)}, u32[]{:S(2)}, u32[]{:S(2)}) collective-permute-start(bf16[144,2048]{1,0:T(8,128)(2,1)} %collective-permute-done.6.refs_6_), channel_id=1, source_target_pairs={{0,4},{4,0},{1,5},{5,1},{2,6},{6,2},{3,7},{7,3},{8,12},{12,8},{9,1... | collective-permute-start | bytes 1769480 | tf_op jit(solution)/shard_map/ppermute | solution.py:111
  68.3 25.1 %all-to-all-start.2 = ((bf16[16,48,72]{2,1,0:T(8,128)(2,1)}), bf16[16,48,72]{2,1,0:T(8,128)(2,1)S(1)}, u32[]{:S(2)}, u32[]{:S(2)}) async-start(bf16[16,48,72]{2,1,0:T(8,128)(2,1)} %bitcast.3), calls=%async_computation.2 | async-start | bytes 393216 | tf_op jit(solution)/shard_map/all_to_all | solution.py:18

commit v7 on v6

--- a/solution.py
+++ b/solution.py
@@ -12,6 +12,7 @@
 PLANE = "plane"
 CORE = "core"
 TP = "tp"
+STEPS = (1, 3, 2)
 
 
 def exchange(chunks, axes):
@@ -19,29 +20,36 @@
 
 
 def up_kernel(block_ref, *refs):
-    stacks, out_ref = refs[:-1], refs[-1]
-    share, each = out_ref.shape[1], out_ref.shape[0] // len(stacks)
-    for at, stack_ref in enumerate(stacks):
-        terms = lax.dot_general(
-            stack_ref[...],
-            block_ref[...],
-            (((1,), (1,)), ((), ())),
-            preferred_element_type=jnp.float32,
-        )
+    weights, out_ref = refs[:-1], refs[-1]
+    share = out_ref.shape[1]
+    each = out_ref.shape[0] // 2
+    block = block_ref[...].reshape(-1, block_ref.shape[-1])
+    for core in range(2):
+        terms = [
+            lax.dot_general(
+                weights[core + 2 * half][...],
+                block,
+                (((1,), (1,)), ((), ())),
+                preferred_element_type=jnp.float32,
+            )
+            for half in range(2)
+        ]
         for i in range(each):
-            gate = terms[i * share : (i + 1) * share]
-            up = terms[(each + i) * share : (each + i + 1) * share]
-            out_ref[at * each + i] = jnp.concatenate([gate, up], axis=1).astype(out_ref.dtype)
+            here = slice(i * share, (i + 1) * share)
+            out_ref[core * each + i] = jnp.concatenate(
+                [half[here] for half in terms], axis=1
+            ).astype(out_ref.dtype)
 
 
-def up_product(block, stacks, tp):
-    rows, width = block.shape
-    units = sum(stack.shape[0] for stack in stacks)
+def up_product(block, weights, tp):
+    chips, mine, width = block.shape
+    rows = chips * mine
+    units = sum(weight.shape[0] for weight in weights)
     vmem = pl.BlockSpec(memory_space=pltpu.VMEM)
     return pl.pallas_call(
         up_kernel,
         out_shape=jax.ShapeDtypeStruct((tp, units // 2 // tp, 2 * rows), jnp.bfloat16),
-        in_specs=[vmem] * (1 + len(stacks)),
+        in_specs=[vmem] * (1 + len(weights)),
         out_specs=vmem,
         cost_estimate=pl.CostEstimate(
             flops=2 * rows * units * width,
@@ -49,7 +57,7 @@
             transcendentals=0,
         ),
         compiler_params=pltpu.CompilerParams(vmem_limit_bytes=16 * 2**20),
-    )(block, *stacks)
+    )(block, *weights)
 
 
 def down_kernel(line, here_ref, hidden_ref, *refs):
@@ -57,14 +65,14 @@
     tp = hidden_ref.shape[0] // line
     half = tp // 2
     total = jnp.zeros(out_ref.shape, jnp.float32)
-    for step in range(line):
+    for at, step in enumerate((0, *STEPS)):
         first = lax.rem(here_ref[0] + step, line) * tp
         for part in range(2):
             units = jnp.concatenate(
                 [hidden_ref[first + part * half + i] for i in range(half)], axis=1
             )
             total += jnp.dot(
-                units, weights[2 * step + part][...], preferred_element_type=jnp.float32
+                units, weights[2 * at + part][...], preferred_element_type=jnp.float32
             )
     out_ref[...] = total.astype(out_ref.dtype)
 
@@ -96,19 +104,19 @@
     rows = line * column
     swap = [(0, 1), (1, 0)]
 
-    stack = jnp.concatenate([gate_weight, up_weight], axis=0)
-    other_stack = lax.ppermute(stack, CORE, swap)
+    stacks = [(part, lax.ppermute(part, CORE, swap)) for part in (gate_weight, up_weight)]
     block = jnp.broadcast_to(tokens[None], (line * plane, mine, width))
-    block = exchange(block, (X, PLANE)).reshape(rows, width)
+    block = exchange(block, (X, PLANE))
 
     gathered = [
         lax.ppermute(down_weight, X, [((i + step) % line, i) for i in range(line)])
-        for step in range(1, line)
+        for step in STEPS
     ]
+    block, down_other = lax.optimization_barrier((block, lax.ppermute(down_weight, CORE, swap)))
 
-    parts = exchange(up_product(block, (stack, other_stack), tp), TP)
-    down_weights = [
-        part for own in (down_weight, *gathered) for part in (own, lax.ppermute(own, CORE, swap))
+    parts = exchange(up_product(block, (*stacks[0], *stacks[1]), tp), TP)
+    down_weights = [down_weight, down_other] + [
+        part for own in gathered for part in (own, lax.ppermute(own, CORE, swap))
     ]
     sums = jnp.sum(parts.astype(jnp.float32), axis=0)
     quarter = (jax.nn.silu(sums[:, :rows]) * sums[:, rows:]).astype(jnp.bfloat16)

time: 117 us -> 119 us (1.017)
  starting transfers between devices: 65.9 us -> 71.9 us
  waiting for transfers between devices: 20.3 us -> 17.2 us
  local copies, waits for them, and re-layouts: 5.41 us -> 3.8 us
    all_to_all x3, waiting for transfers between devices: 20.2 us -> 15.6 us  [exchange(): return lax.all_to_all(chunks, axes, split_axis=0, concat_axis=0, tiled=True)]
    ppermute x1 -> x3, starting transfers between devices: 3.63 us -> 7.37 us  [the longest x2 4.33 us: body(): lax.ppermute(part, CORE, swap)]
    reshape x1 -> x0, local copies, waits for them, and re-layouts: 2.26 us -> none  [body(): block = exchange(block, (X, PLANE)).reshape(rows, width)]
    ppermute x3, waiting for transfers between devices: 0.01 us -> 1.52 us  [body(): lax.ppermute(down_weight, X, [((i + step) % line, i) for i in range(line)])]
    all_to_all x3, starting transfers between devices: 40.5 us -> 41.9 us  [exchange(): return lax.all_to_all(chunks, axes, split_axis=0, concat_axis=0, tiled=True)]
    ppermute x4 -> x3, starting transfers between devices: 12.4 us -> 12.7 us  [body(): lax.ppermute(own, CORE, swap)]
  transfers between devices with their start and end apart: 11 -> 12, of which waited for: 2 -> 3; matrix products, arithmetic and copies ran while one was open for 3% -> 1% of each run, Pallas kernels for 1% -> 2%
where the time goes in v7:
time: 119 us; the launch traced here: 118 us
  starting transfers between devices  71.9 us (60%)
  blocking collectives  19.6 us (16%)
  waiting for transfers between devices  17.2 us (14%)
  Pallas kernels  4.42 us (4%)
  local copies, waits for them, and re-layouts  3.8 us (3%)
    all_to_all x3, starting transfers between devices, exchange(): return lax.all_to_all(chunks, axes, split_axis=0, concat_axis=0, tiled=True)  41.9 us
    all_to_all x1, blocking collectives, exchange(): return lax.all_to_all(chunks, axes, split_axis=0, concat_axis=0, tiled=True)  19.6 us
    all_to_all x3, waiting for transfers between devices, exchange(): return lax.all_to_all(chunks, axes, split_axis=0, concat_axis=0, tiled=True)  15.6 us
    ppermute x3, starting transfers between devices, body(): lax.ppermute(own, CORE, swap)  12.7 us
    ppermute x3, starting transfers between devices, body(): lax.ppermute(down_weight, X, [((i + step) % line, i) for i in range(line)])  9.97 us
    ppermute x2, starting transfers between devices, body(): lax.ppermute(part, CORE, swap)  4.33 us
    ppermute x1, starting transfers between devices, body(): lax.ppermute(down_weight, CORE, swap)  3.04 us
    pallas_call x1, Pallas kernels, down_product(): pl.pallas_call(functools.partial(down_kernel, line), out_shape=jax.ShapeD...  2.42 us
  transfers between devices with their start and end apart: 12, of which 3 were waited for; matrix products, arithmetic and copies ran while one was open for 1% of the time, Pallas kernels for 2%

profile of v7, /device:TPU:1, one launch (start us, length us, event | category | flops | bytes accessed | tf_op | source)
XLA Modules:
  0.0 118.0 jit_solution(3567732358620963439)
XLA Ops:
  0.0 2.0 %broadcast_in_dim.6 = bf16[96,2,2048]{2,1,0:T(2,128)(2,1)} broadcast(bf16[2,2048]{1,0:T(2,128)(2,1)} %param.4), dimensions={1,2} | broadcast | bytes 794624 | tf_op jit(solution)/shard_map/broadcast_in_dim | solution.py:108
  2.0 0.0 copy-start
  2.0 0.0 copy-start.1
  2.0 15.5 %all-to-all-start = ((bf16[96,2,2048]{2,1,0:T(2,128)(2,1)}), bf16[96,2,2048]{2,1,0:T(2,128)(2,1)S(1)}, u32[]{:S(2)}, u32[]{:S(2)}) async-start(bf16[96,2,2048]{2,1,0:T(2,128)(2,1)} %broadcast_in_dim.6), calls=%async_computation | async-start | bytes 1572864 | tf_op jit(solution)/shard_map/all_to_all | solution.py:19
  17.5 3.0 %collective-permute-start = (bf16[144,2048]{1,0:T(8,128)(2,1)}, bf16[144,2048]{1,0:T(8,128)(2,1)S(1)}, u32[]{:S(2)}, u32[]{:S(2)}) collective-permute-start(bf16[144,2048]{1,0:T(8,128)(2,1)} %refs_0_.3), channel_id=1, source_target_pairs={{0,4},{4,0},{1,5},{5,1},{2,6},{6,2},{3,7},{7,3},{8,12},{12,8},{9,1... | collective-permute-start | bytes 1769480 | tf_op jit(solution)/shard_map/ppermute | solution.py:115
  20.5 0.0 copy-done
  20.5 1.9 %collective-permute-start.1 = (bf16[144,2048]{1,0:T(8,128)(2,1)S(1)}, bf16[144,2048]{1,0:T(8,128)(2,1)S(1)}, u32[]{:S(2)}, u32[]{:S(2)}) collective-permute-start(bf16[144,2048]{1,0:T(8,128)(2,1)S(1)} %copy-done), channel_id=1, source_target_pairs={{0,4},{4,0},{1,5},{5,1},{2,6},{6,2},{3,7},{7,3},{8,12},{12,8},{9,1... | collective-permute-start | bytes 1769480 | tf_op jit(solution)/shard_map/ppermute | solution.py:107
  22.5 0.0 copy-done.1
  22.5 2.4 %collective-permute-start.2 = (bf16[144,2048]{1,0:T(8,128)(2,1)S(1)}, bf16[144,2048]{1,0:T(8,128)(2,1)S(1)}, u32[]{:S(2)}, u32[]{:S(2)}) collective-permute-start(bf16[144,2048]{1,0:T(8,128)(2,1)S(1)} %copy-done.1), channel_id=1, source_target_pairs={{0,4},{4,0},{1,5},{5,1},{2,6},{6,2},{3,7},{7,3},{8,12},{12,8},{9,1... | collective-permute-start | bytes 1769480 | tf_op jit(solution)/shard_map/ppermute | solution.py:107
  24.9 4.6 %collective-permute-start.3 = (bf16[144,2048]{1,0:T(8,128)(2,1)}, bf16[144,2048]{1,0:T(8,128)(2,1)}, u32[]{:S(2)}, u32[]{:S(2)}) collective-permute-start(bf16[144,2048]{1,0:T(8,128)(2,1)} %refs_0_.3), channel_id=1, source_target_pairs={{192,0},{384,192},{576,384},{0,576},{193,1},{385,193},{577,385},{1... | collective-permute-start | bytes 1769480 | tf_op jit(solution)/shard_map/ppermute | solution.py:112
  29.5 1.9 %collective-permute-start.5 = (bf16[144,2048]{1,0:T(8,128)(2,1)}, bf16[144,2048]{1,0:T(8,128)(2,1)}, u32[]{:S(2)}, u32[]{:S(2)}) collective-permute-start(bf16[144,2048]{1,0:T(8,128)(2,1)} %refs_0_.3), channel_id=1, source_target_pairs={{576,0},{0,192},{192,384},{384,576},{577,1},{1,193},{193,385},{385... | collective-permute-start | bytes 1769480 | tf_op jit(solution)/shard_map/ppermute | solution.py:112
  31.4 0.0 collective-permute-done.refs_1_
  31.4 0.0 copy-start.2
  31.4 0.8 copy-done.2
  32.2 3.5 %collective-permute-start.7 = (bf16[144,2048]{1,0:T(8,128)(2,1)}, bf16[144,2048]{1,0:T(8,128)(2,1)}, u32[]{:S(2)}, u32[]{:S(2)}) collective-permute-start(bf16[144,2048]{1,0:T(8,128)(2,1)} %refs_0_.3), channel_id=1, source_target_pairs={{384,0},{576,192},{0,384},{192,576},{385,1},{577,193},{1,385},{193... | collective-permute-start | bytes 1769480 | tf_op jit(solution)/shard_map/ppermute | solution.py:112
  35.7 2.8 %all-to-all-done.block_ref = bf16[96,2,2048]{2,1,0:T(2,128)(2,1)S(1)} async-done(((bf16[96,2,2048]{2,1,0:T(2,128)(2,1)}), bf16[96,2,2048]{2,1,0:T(2,128)(2,1)S(1)}, u32[]{:S(2)}, u32[]{:S(2)}) %all-to-all-start) | async-done | bytes 786464 | tf_op jit(solution)/shard_map/all_to_all | solution.py:19
  38.5 0.0 collective-permute-done.1.refs_1_
  38.5 0.0 collective-permute-done.2.refs_3_
  38.5 2.0 %shard_map.46 = bf16[4,72,384]{2,1,0:T(8,128)(2,1)} custom-call(bf16[96,2,2048]{2,1,0:T(2,128)(2,1)S(1)} %all-to-all-done.block_ref, bf16[144,2048]{1,0:T(8,128)(2,1)S(1)} %copy-done, bf16[144,2048]{1,0:T(8,128)(2,1)S(1)} %collective-permute-done.1.refs_1_, bf16[144,2048]{1,0:T(8,128)(2,1)S(1)} %copy-done.1, bf16[144,2048]{1,0:T(8,128)(2,1)S(1)} %collective-permute-done.2.refs_3_), custom_call_target="tpu_custom_call" | custom-call | flops 452984832 | bytes 3366912 | tf_op jit(solution)/shard_map/pallas_call | solution.py:49
  40.5 12.3 %all-to-all-start.1 = ((bf16[4,72,384]{2,1,0:T(8,128)(2,1)}), bf16[4,72,384]{2,1,0:T(8,128)(2,1)S(1)}, u32[]{:S(2)}, u32[]{:S(2)}) async-start(bf16[4,72,384]{2,1,0:T(8,128)(2,1)} %shard_map.46), calls=%async_computation.1 | async-start | bytes 442368 | tf_op jit(solution)/shard_map/all_to_all | solution.py:19
  52.8 0.0 copy-start.3
  52.8 0.0 collective-permute-done.3.refs_2_
  52.8 8.0 %collective-permute-start.4 = (bf16[144,2048]{1,0:T(8,128)(2,1)}, bf16[144,2048]{1,0:T(8,128)(2,1)S(1)}, u32[]{:S(2)}, u32[]{:S(2)}) collective-permute-start(bf16[144,2048]{1,0:T(8,128)(2,1)} %collective-permute-done.3.refs_2_), channel_id=1, source_target_pairs={{0,4},{4,0},{1,5},{5,1},{2,6},{6,2},{3,7},{7,3},{8,12},{12,8},{9,1... | collective-permute-start | bytes 1769480 | tf_op jit(solution)/shard_map/ppermute | solution.py:119
  60.8 1.5 %collective-permute-done.5.refs_4_ = bf16[144,2048]{1,0:T(8,128)(2,1)} collective-permute-done((bf16[144,2048]{1,0:T(8,128)(2,1)}, bf16[144,2048]{1,0:T(8,128)(2,1)}, u32[]{:S(2)}, u32[]{:S(2)}) %collective-permute-start.5) | collective-permute-done | bytes 589856 | tf_op jit(solution)/shard_map/ppermute | solution.py:112
  62.4 2.7 %collective-permute-start.6 = (bf16[144,2048]{1,0:T(8,128)(2,1)}, bf16[144,2048]{1,0:T(8,128)(2,1)S(1)}, u32[]{:S(2)}, u32[]{:S(2)}) collective-permute-start(bf16[144,2048]{1,0:T(8,128)(2,1)} %collective-permute-done.5.refs_4_), channel_id=1, source_target_pairs={{0,4},{4,0},{1,5},{5,1},{2,6},{6,2},{3,7},{7,3},{8,12},{12,8},{9,1... | collective-permute-start | bytes 1769480 | tf_op jit(solution)/shard_map/ppermute | solution.py:119
  65.1 0.0 collective-permute-done.7.refs_6_
  65.1 1.9 %collective-permute-start.8 = (bf16[144,2048]{1,0:T(8,128)(2,1)}, bf16[144,2048]{1,0:T(8,128)(2,1)S(1)}, u32[]{:S(2)}, u32[]{:S(2)}) collective-permute-start(bf16[144,2048]{1,0:T(8,128)(2,1)} %collective-permute-done.7.refs_6_), channel_id=1, source_target_pairs={{0,4},{4,0},{1,5},{5,1},{2,6},{6,2},{3,7},{7,3},{8,12},{12,8},{9,1... | collective-permute-start | bytes 1769480 | tf_op jit(solution)/shard_map/ppermute | solution.py:119
  67.0 0.0 all-to-all-done.1
  67.0 0.1 fusion.1
  67.1 0.1 copy.6
  67.2 0.7 broadcast_in_dim.15
  68.0 14.1 %all-to-all-start.2 = ((bf16[16,48,72]{2,1,0:T(8,128)(2,1)}), bf16[16,48,72]{2,1,0:T(8,128)(2,1)S(1)}, u32[]{:S(2)}, u32[]{:S(2)}) async-start(bf16[16,48,72]{2,1,0:T(8,128)(2,1)} %bitcast.3), calls=%async_computation.2 | async-start | bytes 393216 | tf_op jit(solution)/shard_map/all_to_all | solution.py:19
  82.1 0.0 collective-permute-done.4.refs_3_
  82.1 0.0 collective-permute-done.6.refs_5_
  82.1 0.0 collective-permute-done.8.refs_7_
  82.1 12.9 %all-to-all-done.2.hidden_ref = bf16[16,48,72]{2,1,0:T(8,128)(2,1)S(1)} async-done(((bf16[16,48,72]{2,1,0:T(8,128)(2,1)}), bf16[16,48,72]{2,1,0:T(8,128)(2,1)S(1)}, u32[]{:S(2)}, u32[]{:S(2)}) %all-to-all-start.2) | async-done | bytes 110624 | tf_op jit(solution)/shard_map/all_to_all | solution.py:19
  95.0 0.0 copy-done.3
  95.0 2.4 %shard_map.47 = bf16[48,2048]{1,0:T(8,128)(2,1)S(1)} custom-call(s32[1]{0:T(128)} %bitcast.here_ref, bf16[16,48,72]{2,1,0:T(8,128)(2,1)S(1)} %all-to-all-done.2.hidden_ref, bf16[144,2048]{1,0:T(8,128)(2,1)} %refs_0_.3, bf16[144,2048]{1,0:T(8,128)(2,1)S(1)} %copy-done.3, bf16[144,2048]{1,0:T(8,128)(2,1)} %collective-permute-done.3.refs_2_, ...), custom_call_target="tpu_custom_call" | custom-call | flops 226492416 | bytes 5025792 | tf_op jit(solution)/shard_map/pallas_call | solution.py:84
  97.4 0.1 reshape.14
  97.6 19.6 %all_to_all.20 = bf16[24,2,2048]{2,1,0:T(2,128)(2,1)S(1)} all-to-all(bf16[24,2,2048]{2,1,0:T(2,128)(2,1)S(1)} %reshape.14), channel_id=1, replica_groups=mesh['x'=4,'plane'=24,'core'=2,'tp'=4] {'plane'}, dimensions={0} | all-to-all | bytes 393216 | tf_op jit(solution)/shard_map/all_to_all | solution.py:19
  117.2 0.8 reduce_sum.22
  (1 shorter events, 0.0 us)
Async XLA Ops:
  2.0 18.5 %copy-start = (bf16[144,2048]{1,0:T(8,128)(2,1)S(1)}, bf16[144,2048]{1,0:T(8,128)(2,1)}, u32[]{:S(2)}) copy-start(bf16[144,2048]{1,0:T(8,128)(2,1)} %refs_0_.2) | copy-start | bytes 1769476
  2.0 20.5 %copy-start.1 = (bf16[144,2048]{1,0:T(8,128)(2,1)S(1)}, bf16[144,2048]{1,0:T(8,128)(2,1)}, u32[]{:S(2)}) copy-start(bf16[144,2048]{1,0:T(8,128)(2,1)} %refs_2_.1) | copy-start | bytes 1769476
  2.0 36.5 %all-to-all-start = ((bf16[96,2,2048]{2,1,0:T(2,128)(2,1)}), bf16[96,2,2048]{2,1,0:T(2,128)(2,1)S(1)}, u32[]{:S(2)}, u32[]{:S(2)}) async-start(bf16[96,2,2048]{2,1,0:T(2,128)(2,1)} %broadcast_in_dim.6), calls=%async_computation | async-start | bytes 1572864 | tf_op jit(solution)/shard_map/all_to_all | solution.py:19
  17.5 13.9 %collective-permute-start = (bf16[144,2048]{1,0:T(8,128)(2,1)}, bf16[144,2048]{1,0:T(8,128)(2,1)S(1)}, u32[]{:S(2)}, u32[]{:S(2)}) collective-permute-start(bf16[144,2048]{1,0:T(8,128)(2,1)} %refs_0_.3), channel_id=1, source_target_pairs={{0,4},{4,0},{1,5},{5,1},{2,6},{6,2},{3,7},{7,3},{8,12},{12,8},{9,1... | collective-permute-start | bytes 1769480 | tf_op jit(solution)/shard_map/ppermute | solution.py:115
  20.5 17.9 %collective-permute-start.1 = (bf16[144,2048]{1,0:T(8,128)(2,1)S(1)}, bf16[144,2048]{1,0:T(8,128)(2,1)S(1)}, u32[]{:S(2)}, u32[]{:S(2)}) collective-permute-start(bf16[144,2048]{1,0:T(8,128)(2,1)S(1)} %copy-done), channel_id=1, source_target_pairs={{0,4},{4,0},{1,5},{5,1},{2,6},{6,2},{3,7},{7,3},{8,12},{12,8},{9,1... | collective-permute-start | bytes 1769480 | tf_op jit(solution)/shard_map/ppermute | solution.py:107
  22.5 16.0 %collective-permute-start.2 = (bf16[144,2048]{1,0:T(8,128)(2,1)S(1)}, bf16[144,2048]{1,0:T(8,128)(2,1)S(1)}, u32[]{:S(2)}, u32[]{:S(2)}) collective-permute-start(bf16[144,2048]{1,0:T(8,128)(2,1)S(1)} %copy-done.1), channel_id=1, source_target_pairs={{0,4},{4,0},{1,5},{5,1},{2,6},{6,2},{3,7},{7,3},{8,12},{12,8},{9,1... | collective-permute-start | bytes 1769480 | tf_op jit(solution)/shard_map/ppermute | solution.py:107
  24.9 27.9 %collective-permute-start.3 = (bf16[144,2048]{1,0:T(8,128)(2,1)}, bf16[144,2048]{1,0:T(8,128)(2,1)}, u32[]{:S(2)}, u32[]{:S(2)}) collective-permute-start(bf16[144,2048]{1,0:T(8,128)(2,1)} %refs_0_.3), channel_id=1, source_target_pairs={{192,0},{384,192},{576,384},{0,576},{193,1},{385,193},{577,385},{1... | collective-permute-start | bytes 1769480 | tf_op jit(solution)/shard_map/ppermute | solution.py:112
  29.5 32.9 %collective-permute-start.5 = (bf16[144,2048]{1,0:T(8,128)(2,1)}, bf16[144,2048]{1,0:T(8,128)(2,1)}, u32[]{:S(2)}, u32[]{:S(2)}) collective-permute-start(bf16[144,2048]{1,0:T(8,128)(2,1)} %refs_0_.3), channel_id=1, source_target_pairs={{576,0},{0,192},{192,384},{384,576},{577,1},{1,193},{193,385},{385... | collective-permute-start | bytes 1769480 | tf_op jit(solution)/shard_map/ppermute | solution.py:112
  31.4 0.8 copy-start.2
  32.2 32.8 %collective-permute-start.7 = (bf16[144,2048]{1,0:T(8,128)(2,1)}, bf16[144,2048]{1,0:T(8,128)(2,1)}, u32[]{:S(2)}, u32[]{:S(2)}) collective-permute-start(bf16[144,2048]{1,0:T(8,128)(2,1)} %refs_0_.3), channel_id=1, source_target_pairs={{384,0},{576,192},{0,384},{192,576},{385,1},{577,193},{1,385},{193... | collective-permute-start | bytes 1769480 | tf_op jit(solution)/shard_map/ppermute | solution.py:112
  40.5 26.5 %all-to-all-start.1 = ((bf16[4,72,384]{2,1,0:T(8,128)(2,1)}), bf16[4,72,384]{2,1,0:T(8,128)(2,1)S(1)}, u32[]{:S(2)}, u32[]{:S(2)}) async-start(bf16[4,72,384]{2,1,0:T(8,128)(2,1)} %shard_map.46), calls=%async_computation.1 | async-start | bytes 442368 | tf_op jit(solution)/shard_map/all_to_all | solution.py:19
  52.8 42.2 %copy-start.3 = (bf16[144,2048]{1,0:T(8,128)(2,1)S(1)}, bf16[144,2048]{1,0:T(8,128)(2,1)}, u32[]{:S(2)}) copy-start(bf16[144,2048]{1,0:T(8,128)(2,1)} %copy-done.2) | copy-start | bytes 1769476
  52.8 29.3 %collective-permute-start.4 = (bf16[144,2048]{1,0:T(8,128)(2,1)}, bf16[144,2048]{1,0:T(8,128)(2,1)S(1)}, u32[]{:S(2)}, u32[]{:S(2)}) collective-permute-start(bf16[144,2048]{1,0:T(8,128)(2,1)} %collective-permute-done.3.refs_2_), channel_id=1, source_target_pairs={{0,4},{4,0},{1,5},{5,1},{2,6},{6,2},{3,7},{7,3},{8,12},{12,8},{9,1... | collective-permute-start | bytes 1769480 | tf_op jit(solution)/shard_map/ppermute | solution.py:119
  62.4 19.8 %collective-permute-start.6 = (bf16[144,2048]{1,0:T(8,128)(2,1)}, bf16[144,2048]{1,0:T(8,128)(2,1)S(1)}, u32[]{:S(2)}, u32[]{:S(2)}) collective-permute-start(bf16[144,2048]{1,0:T(8,128)(2,1)} %collective-permute-done.5.refs_4_), channel_id=1, source_target_pairs={{0,4},{4,0},{1,5},{5,1},{2,6},{6,2},{3,7},{7,3},{8,12},{12,8},{9,1... | collective-permute-start | bytes 1769480 | tf_op jit(solution)/shard_map/ppermute | solution.py:119
  65.1 17.0 %collective-permute-start.8 = (bf16[144,2048]{1,0:T(8,128)(2,1)}, bf16[144,2048]{1,0:T(8,128)(2,1)S(1)}, u32[]{:S(2)}, u32[]{:S(2)}) collective-permute-start(bf16[144,2048]{1,0:T(8,128)(2,1)} %collective-permute-done.7.refs_6_), channel_id=1, source_target_pairs={{0,4},{4,0},{1,5},{5,1},{2,6},{6,2},{3,7},{7,3},{8,12},{12,8},{9,1... | collective-permute-start | bytes 1769480 | tf_op jit(solution)/shard_map/ppermute | solution.py:119
  68.0 27.0 %all-to-all-start.2 = ((bf16[16,48,72]{2,1,0:T(8,128)(2,1)}), bf16[16,48,72]{2,1,0:T(8,128)(2,1)S(1)}, u32[]{:S(2)}, u32[]{:S(2)}) async-start(bf16[16,48,72]{2,1,0:T(8,128)(2,1)} %bitcast.3), calls=%async_computation.2 | async-start | bytes 393216 | tf_op jit(solution)/shard_map/all_to_all | solution.py:19

commit v8 on v6

--- a/solution.py
+++ b/solution.py
@@ -12,6 +12,7 @@
 PLANE = "plane"
 CORE = "core"
 TP = "tp"
+STEPS = (1, 3, 2)
 
 
 def exchange(chunks, axes):
@@ -21,10 +22,11 @@
 def up_kernel(block_ref, *refs):
     stacks, out_ref = refs[:-1], refs[-1]
     share, each = out_ref.shape[1], out_ref.shape[0] // len(stacks)
+    block = block_ref[...].reshape(-1, block_ref.shape[-1])
     for at, stack_ref in enumerate(stacks):
         terms = lax.dot_general(
             stack_ref[...],
-            block_ref[...],
+            block,
             (((1,), (1,)), ((), ())),
             preferred_element_type=jnp.float32,
         )
@@ -35,7 +37,8 @@
 
 
 def up_product(block, stacks, tp):
-    rows, width = block.shape
+    chips, mine, width = block.shape
+    rows = chips * mine
     units = sum(stack.shape[0] for stack in stacks)
     vmem = pl.BlockSpec(memory_space=pltpu.VMEM)
     return pl.pallas_call(
@@ -52,39 +55,36 @@
     )(block, *stacks)
 
 
-def down_kernel(line, here_ref, hidden_ref, *refs):
-    weights, out_ref = refs[:-1], refs[-1]
+def down_kernel(line, places, here_ref, hidden_ref, *refs):
+    weights, out_ref = refs[: len(places)], refs[-1]
     tp = hidden_ref.shape[0] // line
     half = tp // 2
-    total = jnp.zeros(out_ref.shape, jnp.float32)
-    for step in range(line):
-        first = lax.rem(here_ref[0] + step, line) * tp
-        for part in range(2):
-            units = jnp.concatenate(
-                [hidden_ref[first + part * half + i] for i in range(half)], axis=1
-            )
-            total += jnp.dot(
-                units, weights[2 * step + part][...], preferred_element_type=jnp.float32
-            )
+    total = refs[-2][...] if len(refs) > len(places) + 1 else jnp.zeros(out_ref.shape, jnp.float32)
+    for (step, core), weight_ref in zip(places, weights):
+        first = lax.rem(here_ref[0] + step, line) * tp + core * half
+        units = jnp.concatenate([hidden_ref[first + i] for i in range(half)], axis=1)
+        total += jnp.dot(units, weight_ref[...], preferred_element_type=jnp.float32)
     out_ref[...] = total.astype(out_ref.dtype)
 
 
-def down_product(hidden, weights, here, line):
-    column, width = hidden.shape[1], weights[0].shape[1]
-    units = hidden.shape[0] * hidden.shape[2]
+def down_product(hidden, weights, here, line, dtype, *total):
+    column, width = hidden.shape[1], next(iter(weights.values())).shape[1]
+    units = sum(weight.shape[0] for weight in weights.values())
+    weight_of = 1 if total else 64
     vmem = pl.BlockSpec(memory_space=pltpu.VMEM)
     return pl.pallas_call(
-        functools.partial(down_kernel, line),
-        out_shape=jax.ShapeDtypeStruct((column, width), jnp.bfloat16),
-        in_specs=[pl.BlockSpec(memory_space=pltpu.SMEM)] + [vmem] * (1 + len(weights)),
+        functools.partial(down_kernel, line, tuple(weights)),
+        out_shape=jax.ShapeDtypeStruct((column, width), dtype),
+        in_specs=[pl.BlockSpec(memory_space=pltpu.SMEM)]
+        + [vmem] * (1 + len(weights) + len(total)),
         out_specs=vmem,
         cost_estimate=pl.CostEstimate(
-            flops=2 * column * units * width,
+            flops=weight_of * 2 * column * units * width,
             bytes_accessed=2 * (units * width + column * width + column * units),
             transcendentals=0,
         ),
         compiler_params=pltpu.CompilerParams(vmem_limit_bytes=16 * 2**20),
-    )(here.reshape(1), hidden, *weights)
+    )(here.reshape(1), hidden, *weights.values(), *total)
 
 
 def body(tokens, gate_weight, up_weight, down_weight):
@@ -99,23 +99,29 @@
     stack = jnp.concatenate([gate_weight, up_weight], axis=0)
     other_stack = lax.ppermute(stack, CORE, swap)
     block = jnp.broadcast_to(tokens[None], (line * plane, mine, width))
-    block = exchange(block, (X, PLANE)).reshape(rows, width)
+    block = exchange(block, (X, PLANE))
 
     gathered = [
         lax.ppermute(down_weight, X, [((i + step) % line, i) for i in range(line)])
-        for step in range(1, line)
+        for step in STEPS
     ]
-
+    block, down_other = lax.optimization_barrier((block, lax.ppermute(down_weight, CORE, swap)))
     parts = exchange(up_product(block, (stack, other_stack), tp), TP)
-    down_weights = [
-        part for own in (down_weight, *gathered) for part in (own, lax.ppermute(own, CORE, swap))
-    ]
     sums = jnp.sum(parts.astype(jnp.float32), axis=0)
     quarter = (jax.nn.silu(sums[:, :rows]) * sums[:, rows:]).astype(jnp.bfloat16)
     quarter = quarter.T.reshape(line, 1, column, share)
     spread = jnp.broadcast_to(quarter, (line, tp, column, share))
     hidden = exchange(spread.reshape(line * tp, column, share), (X, TP))
-    terms = down_product(hidden, down_weights, lax.axis_index(X), line)
+    here = lax.axis_index(X)
+    swapped = [lax.ppermute(weight, CORE, swap) for weight in gathered]
+    pairs = [(down_weight, down_other), *zip(gathered, swapped)]
+    places = [
+        {(step, core): weight for core, weight in enumerate(pair)}
+        for step, pair in zip((0, *STEPS), pairs)
+    ]
+    near = places[0] | places[1] | places[2]
+    terms = down_product(hidden, near, here, line, jnp.float32)
+    terms = down_product(hidden, places[3], here, line, jnp.bfloat16, terms)
     terms = exchange(terms.reshape(plane, mine, width), PLANE)
     return jnp.sum(terms.astype(jnp.float32), axis=0).astype(jnp.bfloat16)
 

time: 117 us -> 110 us (0.940)
  waiting for transfers between devices: 20.3 us -> 18 us
  blocking collectives: 19.5 us -> 17.3 us
  starting transfers between devices: 65.9 us -> 64.4 us
  local copies, waits for them, and re-layouts: 5.41 us -> 3.95 us
    reshape x1 -> x0, local copies, waits for them, and re-layouts: 2.26 us -> none  [body(): block = exchange(block, (X, PLANE)).reshape(rows, width)]
    all_to_all x3, waiting for transfers between devices: 20.2 us -> 18 us  [exchange(): return lax.all_to_all(chunks, axes, split_axis=0, concat_axis=0, tiled=True)]
    all_to_all x1, blocking collectives: 19.5 us -> 17.3 us  [exchange(): return lax.all_to_all(chunks, axes, split_axis=0, concat_axis=0, tiled=True)]
    all_to_all x3, starting transfers between devices: 40.5 us -> 38.9 us  [exchange(): return lax.all_to_all(chunks, axes, split_axis=0, concat_axis=0, tiled=True)]
    ppermute x3, starting transfers between devices: 9.31 us -> 10.9 us  [body(): lax.ppermute(down_weight, X, [((i + step) % line, i) for i in range(line)])]
    pallas_call x1 -> x2, Pallas kernels: 2.42 us -> 2.45 us  [down_product(): pl.pallas_call(functools.partial(down_kernel, line, tuple(weights)), out_...]
  transfers between devices with their start and end apart: 11 -> 11, of which waited for: 2 -> 2; matrix products, arithmetic and copies ran while one was open for 3% -> 1% of each run, Pallas kernels for 1% -> 3%
where the time goes in v8:
time: 110 us; the launch traced here: 109 us
  starting transfers between devices  64.4 us (59%)
  waiting for transfers between devices  18 us (16%)
  blocking collectives  17.3 us (16%)
  Pallas kernels  4.05 us (4%)
  local copies, waits for them, and re-layouts  3.95 us (4%)
    all_to_all x3, starting transfers between devices, exchange(): return lax.all_to_all(chunks, axes, split_axis=0, concat_axis=0, tiled=True)  38.9 us
    all_to_all x3, waiting for transfers between devices, exchange(): return lax.all_to_all(chunks, axes, split_axis=0, concat_axis=0, tiled=True)  18 us
    all_to_all x1, blocking collectives, exchange(): return lax.all_to_all(chunks, axes, split_axis=0, concat_axis=0, tiled=True)  17.3 us
    ppermute x3, starting transfers between devices, body(): lax.ppermute(down_weight, X, [((i + step) % line, i) for i in range(line)])  10.9 us
    ppermute x3, starting transfers between devices, body(): swapped = [lax.ppermute(weight, CORE, swap) for weight in gathered]  9.63 us
    ppermute x1, starting transfers between devices, body(): other_stack = lax.ppermute(stack, CORE, swap)  3.04 us
    pallas_call x2, Pallas kernels, down_product(): pl.pallas_call(functools.partial(down_kernel, line, tuple(weights)), out_...  2.45 us
  transfers between devices with their start and end apart: 11, of which 2 were waited for; matrix products, arithmetic and copies ran while one was open for 1% of the time, Pallas kernels for 3%

profile of v8, /device:TPU:1, one launch (start us, length us, event | category | flops | bytes accessed | tf_op | source)
XLA Modules:
  0.0 108.8 jit_solution(8649009921186362842)
XLA Ops:
  0.0 0.0 copy-start.2
  0.0 2.0 %broadcast_in_dim.6 = bf16[96,2,2048]{2,1,0:T(2,128)(2,1)} broadcast(bf16[2,2048]{1,0:T(2,128)(2,1)} %param.4), dimensions={1,2} | broadcast | bytes 794624 | tf_op jit(solution)/shard_map/broadcast_in_dim | solution.py:101
  2.1 0.0 copy-start.3
  2.1 15.5 %all-to-all-start = ((bf16[96,2,2048]{2,1,0:T(2,128)(2,1)}), bf16[96,2,2048]{2,1,0:T(2,128)(2,1)S(1)}, u32[]{:S(2)}, u32[]{:S(2)}) async-start(bf16[96,2,2048]{2,1,0:T(2,128)(2,1)} %broadcast_in_dim.6), calls=%async_computation | async-start | bytes 1572864 | tf_op jit(solution)/shard_map/all_to_all | solution.py:19
  17.5 0.0 copy-done.2
  17.6 0.0 copy-done.3
  17.7 3.0 %collective-permute-start.1 = (bf16[288,2048]{1,0:T(8,128)(2,1)S(1)}, bf16[288,2048]{1,0:T(8,128)(2,1)S(1)}, u32[]{:S(2)}, u32[]{:S(2)}) collective-permute-start(bf16[288,2048]{1,0:T(8,128)(2,1)S(1)} %constant_dynamic-update-slice_fusion.refs_0_), channel_id=1, source_target_pairs={{0,4},{4,0},{1,5},{5,1},{2,6},{6,2},{3,7},{7,3},{8,12},{12,8},{9,1... | collective-permute-start | bytes 3538952 | tf_op jit(solution)/shard_map/ppermute | solution.py:100
  20.7 1.9 %collective-permute-start = (bf16[144,2048]{1,0:T(8,128)(2,1)}, bf16[144,2048]{1,0:T(8,128)(2,1)S(1)}, u32[]{:S(2)}, u32[]{:S(2)}) collective-permute-start(bf16[144,2048]{1,0:T(8,128)(2,1)} %refs_0_.1), channel_id=1, source_target_pairs={{0,4},{4,0},{1,5},{5,1},{2,6},{6,2},{3,7},{7,3},{8,12},{12,8},{9,1... | collective-permute-start | bytes 1769480 | tf_op jit(solution)/shard_map/ppermute | solution.py:108
  22.6 4.6 %collective-permute-start.4 = (bf16[144,2048]{1,0:T(8,128)(2,1)}, bf16[144,2048]{1,0:T(8,128)(2,1)}, u32[]{:S(2)}, u32[]{:S(2)}) collective-permute-start(bf16[144,2048]{1,0:T(8,128)(2,1)} %refs_0_.1), channel_id=1, source_target_pairs={{192,0},{384,192},{576,384},{0,576},{193,1},{385,193},{577,385},{1... | collective-permute-start | bytes 1769480 | tf_op jit(solution)/shard_map/ppermute | solution.py:105
  27.2 1.9 %collective-permute-start.6 = (bf16[144,2048]{1,0:T(8,128)(2,1)}, bf16[144,2048]{1,0:T(8,128)(2,1)}, u32[]{:S(2)}, u32[]{:S(2)}) collective-permute-start(bf16[144,2048]{1,0:T(8,128)(2,1)} %refs_0_.1), channel_id=1, source_target_pairs={{576,0},{0,192},{192,384},{384,576},{577,1},{1,193},{193,385},{385... | collective-permute-start | bytes 1769480 | tf_op jit(solution)/shard_map/ppermute | solution.py:105
  29.1 0.0 collective-permute-done.refs_1_
  29.2 0.0 copy-start
  29.2 0.8 copy-done
  30.0 8.5 %all-to-all-done.block_ref = bf16[96,2,2048]{2,1,0:T(2,128)(2,1)S(1)} async-done(((bf16[96,2,2048]{2,1,0:T(2,128)(2,1)}), bf16[96,2,2048]{2,1,0:T(2,128)(2,1)S(1)}, u32[]{:S(2)}, u32[]{:S(2)}) %all-to-all-start) | async-done | bytes 786464 | tf_op jit(solution)/shard_map/all_to_all | solution.py:19
  38.5 0.0 collective-permute-done.1.refs_1_
  38.5 1.6 %shard_map.46 = bf16[4,72,384]{2,1,0:T(8,128)(2,1)} custom-call(bf16[96,2,2048]{2,1,0:T(2,128)(2,1)S(1)} %all-to-all-done.block_ref, bf16[288,2048]{1,0:T(8,128)(2,1)S(1)} %constant_dynamic-update-slice_fusion.refs_0_, bf16[288,2048]{1,0:T(8,128)(2,1)S(1)} %collective-permute-done.1.refs_1_), custom_call_target="tpu_custom_call" | custom-call | flops 452984832 | bytes 3366912 | tf_op jit(solution)/shard_map/pallas_call | solution.py:44
  40.1 0.0 copy-start.1
  40.1 12.4 %all-to-all-start.1 = ((bf16[4,72,384]{2,1,0:T(8,128)(2,1)}), bf16[4,72,384]{2,1,0:T(8,128)(2,1)S(1)}, u32[]{:S(2)}, u32[]{:S(2)}) async-start(bf16[4,72,384]{2,1,0:T(8,128)(2,1)} %shard_map.46), calls=%async_computation.1 | async-start | bytes 442368 | tf_op jit(solution)/shard_map/all_to_all | solution.py:19
  52.5 4.5 %collective-permute-start.2 = (bf16[144,2048]{1,0:T(8,128)(2,1)}, bf16[144,2048]{1,0:T(8,128)(2,1)S(1)}, u32[]{:S(2)}, u32[]{:S(2)}) collective-permute-start(bf16[144,2048]{1,0:T(8,128)(2,1)} %refs_0_.1), channel_id=1, source_target_pairs={{384,0},{576,192},{0,384},{192,576},{385,1},{577,193},{1,385},{193... | collective-permute-start | bytes 1769480 | tf_op jit(solution)/shard_map/ppermute | solution.py:105
  57.0 0.0 collective-permute-done.4.refs_2_
  57.0 5.0 %collective-permute-start.5 = (bf16[144,2048]{1,0:T(8,128)(2,1)}, bf16[144,2048]{1,0:T(8,128)(2,1)S(1)}, u32[]{:S(2)}, u32[]{:S(2)}) collective-permute-start(bf16[144,2048]{1,0:T(8,128)(2,1)} %collective-permute-done.4.refs_2_), channel_id=1, source_target_pairs={{0,4},{4,0},{1,5},{5,1},{2,6},{6,2},{3,7},{7,3},{8,12},{12,8},{9,1... | collective-permute-start | bytes 1769480 | tf_op jit(solution)/shard_map/ppermute | solution.py:116
  62.0 0.0 collective-permute-done.6.refs_4_
  62.0 1.9 %collective-permute-start.7 = (bf16[144,2048]{1,0:T(8,128)(2,1)}, bf16[144,2048]{1,0:T(8,128)(2,1)S(1)}, u32[]{:S(2)}, u32[]{:S(2)}) collective-permute-start(bf16[144,2048]{1,0:T(8,128)(2,1)} %collective-permute-done.6.refs_4_), channel_id=1, source_target_pairs={{0,4},{4,0},{1,5},{5,1},{2,6},{6,2},{3,7},{7,3},{8,12},{12,8},{9,1... | collective-permute-start | bytes 1769480 | tf_op jit(solution)/shard_map/ppermute | solution.py:116
  64.0 0.0 all-to-all-done.1
  64.0 0.1 fusion.1
  64.1 0.1 copy.6
  64.2 0.7 broadcast_in_dim.15
  64.9 11.0 %all-to-all-start.2 = ((bf16[16,48,72]{2,1,0:T(8,128)(2,1)}), bf16[16,48,72]{2,1,0:T(8,128)(2,1)S(1)}, u32[]{:S(2)}, u32[]{:S(2)}) async-start(bf16[16,48,72]{2,1,0:T(8,128)(2,1)} %bitcast.3), calls=%async_computation.2 | async-start | bytes 393216 | tf_op jit(solution)/shard_map/all_to_all | solution.py:19
  75.9 0.0 collective-permute-done.2.refs_0_
  76.0 2.7 %collective-permute-start.3 = (bf16[144,2048]{1,0:T(8,128)(2,1)S(1)}, bf16[144,2048]{1,0:T(8,128)(2,1)S(1)}, u32[]{:S(2)}, u32[]{:S(2)}) collective-permute-start(bf16[144,2048]{1,0:T(8,128)(2,1)S(1)} %collective-permute-done.2.refs_0_), channel_id=1, source_target_pairs={{0,4},{4,0},{1,5},{5,1},{2,6},{6,2},{3,7},{7,3},{8,12},{12,8},{9,1... | collective-permute-start | bytes 1769480 | tf_op jit(solution)/shard_map/ppermute | solution.py:116
  78.7 0.0 collective-permute-done.5.refs_3_
  78.7 0.0 collective-permute-done.7.refs_5_
  78.7 9.5 %all-to-all-done.2.hidden_ref = bf16[16,48,72]{2,1,0:T(8,128)(2,1)S(1)} async-done(((bf16[16,48,72]{2,1,0:T(8,128)(2,1)}), bf16[16,48,72]{2,1,0:T(8,128)(2,1)S(1)}, u32[]{:S(2)}, u32[]{:S(2)}) %all-to-all-start.2) | async-done | bytes 110624 | tf_op jit(solution)/shard_map/all_to_all | solution.py:19
  88.1 0.0 copy-done.1
  88.1 2.1 %shard_map.47.refs_2_ = f32[48,2048]{1,0:T(8,128)S(1)} custom-call(s32[1]{0:T(128)} %bitcast.here_ref, bf16[16,48,72]{2,1,0:T(8,128)(2,1)S(1)} %all-to-all-done.2.hidden_ref, bf16[144,2048]{1,0:T(8,128)(2,1)} %refs_0_.1, bf16[144,2048]{1,0:T(8,128)(2,1)S(1)} %copy-done.1, bf16[144,2048]{1,0:T(8,128)(2,1)} %collective-permute-done.4.refs_2_, ...), custom_call_target="tpu_custom_call" | custom-call | flops 10871635968 | bytes 3818496 | tf_op jit(solution)/shard_map/pallas_call | solution.py:75
  90.2 0.0 collective-permute-done.3.refs_1_
  90.2 0.4 shard_map.48
  90.6 0.1 reshape.15
  90.8 17.3 %all_to_all.20 = bf16[24,2,2048]{2,1,0:T(2,128)(2,1)S(1)} all-to-all(bf16[24,2,2048]{2,1,0:T(2,128)(2,1)S(1)} %reshape.15), channel_id=1, replica_groups=mesh['x'=4,'plane'=24,'core'=2,'tp'=4] {'plane'}, dimensions={0} | all-to-all | bytes 393216 | tf_op jit(solution)/shard_map/all_to_all | solution.py:19
  108.0 0.8 reduce_sum.22
  (3 shorter events, 0.1 us)
Async XLA Ops:
  0.0 17.5 %copy-start.2 = (bf16[144,2048]{1,0:T(8,128)(2,1)S(1)}, bf16[144,2048]{1,0:T(8,128)(2,1)}, u32[]{:S(2)}) copy-start(bf16[144,2048]{1,0:T(8,128)(2,1)} %param.5) | copy-start | bytes 1769476
  2.1 15.5 %copy-start.3 = (bf16[144,2048]{1,0:T(8,128)(2,1)S(1)}, bf16[144,2048]{1,0:T(8,128)(2,1)}, u32[]{:S(2)}) copy-start(bf16[144,2048]{1,0:T(8,128)(2,1)} %param.6) | copy-start | bytes 1769476
  2.1 36.5 %all-to-all-start = ((bf16[96,2,2048]{2,1,0:T(2,128)(2,1)}), bf16[96,2,2048]{2,1,0:T(2,128)(2,1)S(1)}, u32[]{:S(2)}, u32[]{:S(2)}) async-start(bf16[96,2,2048]{2,1,0:T(2,128)(2,1)} %broadcast_in_dim.6), calls=%async_computation | async-start | bytes 1572864 | tf_op jit(solution)/shard_map/all_to_all | solution.py:19
  17.7 20.9 %collective-permute-start.1 = (bf16[288,2048]{1,0:T(8,128)(2,1)S(1)}, bf16[288,2048]{1,0:T(8,128)(2,1)S(1)}, u32[]{:S(2)}, u32[]{:S(2)}) collective-permute-start(bf16[288,2048]{1,0:T(8,128)(2,1)S(1)} %constant_dynamic-update-slice_fusion.refs_0_), channel_id=1, source_target_pairs={{0,4},{4,0},{1,5},{5,1},{2,6},{6,2},{3,7},{7,3},{8,12},{12,8},{9,1... | collective-permute-start | bytes 3538952 | tf_op jit(solution)/shard_map/ppermute | solution.py:100
  20.7 8.4 %collective-permute-start = (bf16[144,2048]{1,0:T(8,128)(2,1)}, bf16[144,2048]{1,0:T(8,128)(2,1)S(1)}, u32[]{:S(2)}, u32[]{:S(2)}) collective-permute-start(bf16[144,2048]{1,0:T(8,128)(2,1)} %refs_0_.1), channel_id=1, source_target_pairs={{0,4},{4,0},{1,5},{5,1},{2,6},{6,2},{3,7},{7,3},{8,12},{12,8},{9,1... | collective-permute-start | bytes 1769480 | tf_op jit(solution)/shard_map/ppermute | solution.py:108
  22.6 34.4 %collective-permute-start.4 = (bf16[144,2048]{1,0:T(8,128)(2,1)}, bf16[144,2048]{1,0:T(8,128)(2,1)}, u32[]{:S(2)}, u32[]{:S(2)}) collective-permute-start(bf16[144,2048]{1,0:T(8,128)(2,1)} %refs_0_.1), channel_id=1, source_target_pairs={{192,0},{384,192},{576,384},{0,576},{193,1},{385,193},{577,385},{1... | collective-permute-start | bytes 1769480 | tf_op jit(solution)/shard_map/ppermute | solution.py:105
  27.2 34.8 %collective-permute-start.6 = (bf16[144,2048]{1,0:T(8,128)(2,1)}, bf16[144,2048]{1,0:T(8,128)(2,1)}, u32[]{:S(2)}, u32[]{:S(2)}) collective-permute-start(bf16[144,2048]{1,0:T(8,128)(2,1)} %refs_0_.1), channel_id=1, source_target_pairs={{576,0},{0,192},{192,384},{384,576},{577,1},{1,193},{193,385},{385... | collective-permute-start | bytes 1769480 | tf_op jit(solution)/shard_map/ppermute | solution.py:105
  29.2 0.8 copy-start
  40.1 48.0 %copy-start.1 = (bf16[144,2048]{1,0:T(8,128)(2,1)S(1)}, bf16[144,2048]{1,0:T(8,128)(2,1)}, u32[]{:S(2)}) copy-start(bf16[144,2048]{1,0:T(8,128)(2,1)} %copy-done) | copy-start | bytes 1769476
  40.1 23.8 %all-to-all-start.1 = ((bf16[4,72,384]{2,1,0:T(8,128)(2,1)}), bf16[4,72,384]{2,1,0:T(8,128)(2,1)S(1)}, u32[]{:S(2)}, u32[]{:S(2)}) async-start(bf16[4,72,384]{2,1,0:T(8,128)(2,1)} %shard_map.46), calls=%async_computation.1 | async-start | bytes 442368 | tf_op jit(solution)/shard_map/all_to_all | solution.py:19
  52.5 23.4 %collective-permute-start.2 = (bf16[144,2048]{1,0:T(8,128)(2,1)}, bf16[144,2048]{1,0:T(8,128)(2,1)S(1)}, u32[]{:S(2)}, u32[]{:S(2)}) collective-permute-start(bf16[144,2048]{1,0:T(8,128)(2,1)} %refs_0_.1), channel_id=1, source_target_pairs={{384,0},{576,192},{0,384},{192,576},{385,1},{577,193},{1,385},{193... | collective-permute-start | bytes 1769480 | tf_op jit(solution)/shard_map/ppermute | solution.py:105
  57.0 21.7 %collective-permute-start.5 = (bf16[144,2048]{1,0:T(8,128)(2,1)}, bf16[144,2048]{1,0:T(8,128)(2,1)S(1)}, u32[]{:S(2)}, u32[]{:S(2)}) collective-permute-start(bf16[144,2048]{1,0:T(8,128)(2,1)} %collective-permute-done.4.refs_2_), channel_id=1, source_target_pairs={{0,4},{4,0},{1,5},{5,1},{2,6},{6,2},{3,7},{7,3},{8,12},{12,8},{9,1... | collective-permute-start | bytes 1769480 | tf_op jit(solution)/shard_map/ppermute | solution.py:116
  62.0 16.6 %collective-permute-start.7 = (bf16[144,2048]{1,0:T(8,128)(2,1)}, bf16[144,2048]{1,0:T(8,128)(2,1)S(1)}, u32[]{:S(2)}, u32[]{:S(2)}) collective-permute-start(bf16[144,2048]{1,0:T(8,128)(2,1)} %collective-permute-done.6.refs_4_), channel_id=1, source_target_pairs={{0,4},{4,0},{1,5},{5,1},{2,6},{6,2},{3,7},{7,3},{8,12},{12,8},{9,1... | collective-permute-start | bytes 1769480 | tf_op jit(solution)/shard_map/ppermute | solution.py:116
  64.9 23.2 %all-to-all-start.2 = ((bf16[16,48,72]{2,1,0:T(8,128)(2,1)}), bf16[16,48,72]{2,1,0:T(8,128)(2,1)S(1)}, u32[]{:S(2)}, u32[]{:S(2)}) async-start(bf16[16,48,72]{2,1,0:T(8,128)(2,1)} %bitcast.3), calls=%async_computation.2 | async-start | bytes 393216 | tf_op jit(solution)/shard_map/all_to_all | solution.py:19
  76.0 14.3 %collective-permute-start.3 = (bf16[144,2048]{1,0:T(8,128)(2,1)S(1)}, bf16[144,2048]{1,0:T(8,128)(2,1)S(1)}, u32[]{:S(2)}, u32[]{:S(2)}) collective-permute-start(bf16[144,2048]{1,0:T(8,128)(2,1)S(1)} %collective-permute-done.2.refs_0_), channel_id=1, source_target_pairs={{0,4},{4,0},{1,5},{5,1},{2,6},{6,2},{3,7},{7,3},{8,12},{12,8},{9,1... | collective-permute-start | bytes 1769480 | tf_op jit(solution)/shard_map/ppermute | solution.py:116

commit v9 on v8

--- a/solution.py
+++ b/solution.py
@@ -17,6 +17,33 @@
 
 def exchange(chunks, axes):
     return lax.all_to_all(chunks, axes, split_axis=0, concat_axis=0, tiled=True)
+
+
+def spread_kernel(rows_ref, out_ref, held, sems):
+    held[...] = jnp.broadcast_to(rows_ref[...][None], held.shape)
+    size = held.shape[0]
+    copies = [
+        pltpu.make_async_copy(held, out_ref.at[pl.ds(i * size, size)], sems.at[i])
+        for i in range(out_ref.shape[0] // size)
+    ]
+    for copy in copies:
+        copy.start()
+    for copy in copies:
+        copy.wait()
+
+
+def spread_rows(rows, copies, blocks):
+    return pl.pallas_call(
+        spread_kernel,
+        out_shape=jax.ShapeDtypeStruct((copies, *rows.shape), rows.dtype),
+        in_specs=[pl.BlockSpec(memory_space=pltpu.VMEM)],
+        out_specs=pl.BlockSpec(memory_space=pl.ANY),
+        scratch_shapes=[
+            pltpu.VMEM((copies // blocks, *rows.shape), rows.dtype),
+            pltpu.SemaphoreType.DMA((blocks,)),
+        ],
+        compiler_params=pltpu.CompilerParams(vmem_limit_bytes=8 * 2**20),
+    )(rows)
 
 
 def up_kernel(block_ref, *refs):
@@ -53,6 +80,29 @@
         ),
         compiler_params=pltpu.CompilerParams(vmem_limit_bytes=16 * 2**20),
     )(block, *stacks)
+
+
+def hidden_kernel(parts_ref, out_ref):
+    line, tp, column, _ = out_ref.shape
+    rows = line * column
+    sums = jnp.sum(parts_ref[...].astype(jnp.float32), axis=0)
+    hidden = (jax.nn.silu(sums[:, :rows]) * sums[:, rows:]).T.astype(out_ref.dtype)
+    for x in range(line):
+        block = hidden[x * column : (x + 1) * column]
+        for i in range(tp):
+            out_ref[x, i] = block
+
+
+def hidden_spread(parts, line, column):
+    tp, share, _ = parts.shape
+    vmem = pl.BlockSpec(memory_space=pltpu.VMEM)
+    return pl.pallas_call(
+        hidden_kernel,
+        out_shape=jax.ShapeDtypeStruct((line, tp, column, share), parts.dtype),
+        in_specs=[vmem],
+        out_specs=vmem,
+        compiler_params=pltpu.CompilerParams(vmem_limit_bytes=8 * 2**20),
+    )(parts)
 
 
 def down_kernel(line, places, here_ref, hidden_ref, *refs):
@@ -98,7 +148,7 @@
 
     stack = jnp.concatenate([gate_weight, up_weight], axis=0)
     other_stack = lax.ppermute(stack, CORE, swap)
-    block = jnp.broadcast_to(tokens[None], (line * plane, mine, width))
+    block = spread_rows(tokens, line * plane, 2 * line)
     block = exchange(block, (X, PLANE))
 
     gathered = [
@@ -107,10 +157,7 @@
     ]
     block, down_other = lax.optimization_barrier((block, lax.ppermute(down_weight, CORE, swap)))
     parts = exchange(up_product(block, (stack, other_stack), tp), TP)
-    sums = jnp.sum(parts.astype(jnp.float32), axis=0)
-    quarter = (jax.nn.silu(sums[:, :rows]) * sums[:, rows:]).astype(jnp.bfloat16)
-    quarter = quarter.T.reshape(line, 1, column, share)
-    spread = jnp.broadcast_to(quarter, (line, tp, column, share))
+    spread = hidden_spread(parts, line, column)
     hidden = exchange(spread.reshape(line * tp, column, share), (X, TP))
     here = lax.axis_index(X)
     swapped = [lax.ppermute(weight, CORE, swap) for weight in gathered]

time: 110 us -> 109 us (level)
  local copies, waits for them, and re-layouts: 3.95 us -> 1.76 us
  Pallas kernels: 4.05 us -> 5.86 us
    broadcast_in_dim x2 -> x0, local copies, waits for them, and re-layouts: 2.76 us -> none  [the longest x1 2.05 us: body(): block = jnp.broadcast_to(tokens[None], (line * plane, mine, width))]
    pallas_call x0 -> x2, Pallas kernels: none -> 1.83 us  [the longest x1 0.98 us: spread_rows(): pl.pallas_call(spread_kernel, out_shape=jax.ShapeDtypeStruct((copies, *ro...]
  transfers between devices with their start and end apart: 11 -> 11, of which waited for: 2 -> 2; matrix products, arithmetic and copies ran while one was open for 1% -> 0% of each run, Pallas kernels for 3% -> 4%
where the time goes in v9:
time: 109 us; the launch traced here: 108 us
  starting transfers between devices  64.4 us (59%)
  waiting for transfers between devices  18 us (17%)
  blocking collectives  17.3 us (16%)
  Pallas kernels  5.86 us (5%)
  local copies, waits for them, and re-layouts  1.76 us (2%)
    all_to_all x3, starting transfers between devices, exchange(): return lax.all_to_all(chunks, axes, split_axis=0, concat_axis=0, tiled=True)  38.9 us
    all_to_all x3, waiting for transfers between devices, exchange(): return lax.all_to_all(chunks, axes, split_axis=0, concat_axis=0, tiled=True)  18 us
    all_to_all x1, blocking collectives, exchange(): return lax.all_to_all(chunks, axes, split_axis=0, concat_axis=0, tiled=True)  17.3 us
    ppermute x3, starting transfers between devices, body(): lax.ppermute(down_weight, X, [((i + step) % line, i) for i in range(line)])  10.9 us
    ppermute x3, starting transfers between devices, body(): swapped = [lax.ppermute(weight, CORE, swap) for weight in gathered]  9.62 us
    ppermute x1, starting transfers between devices, body(): other_stack = lax.ppermute(stack, CORE, swap)  3.04 us
    pallas_call x2, Pallas kernels, down_product(): pl.pallas_call(functools.partial(down_kernel, line, tuple(weights)), out_...  2.45 us
  transfers between devices with their start and end apart: 11, of which 2 were waited for; matrix products, arithmetic and copies ran while one was open for 0% of the time, Pallas kernels for 4%

profile of v9, /device:TPU:1, one launch (start us, length us, event | category | flops | bytes accessed | tf_op | source)
XLA Modules:
  0.0 108.4 jit_solution(5279611749023460779)
XLA Ops:
  0.0 0.0 copy-start
  0.0 0.7 copy-done
  0.7 0.0 copy-start.3
  0.7 1.0 shard_map.46
  1.7 0.0 copy-start.4
  1.7 15.5 %all-to-all-start = ((bf16[96,2,2048]{2,1,0:T(2,128)(2,1)}), bf16[96,2,2048]{2,1,0:T(2,128)(2,1)S(1)}, u32[]{:S(2)}, u32[]{:S(2)}) async-start(bf16[96,2,2048]{2,1,0:T(2,128)(2,1)} %shard_map.46), calls=%async_computation | async-start | bytes 1572864 | tf_op jit(solution)/shard_map/all_to_all | solution.py:19
  17.2 0.0 copy-done.3
  17.3 0.0 copy-done.4
  17.3 3.0 %collective-permute-start.1 = (bf16[288,2048]{1,0:T(8,128)(2,1)S(1)}, bf16[288,2048]{1,0:T(8,128)(2,1)S(1)}, u32[]{:S(2)}, u32[]{:S(2)}) collective-permute-start(bf16[288,2048]{1,0:T(8,128)(2,1)S(1)} %constant_dynamic-update-slice_fusion.refs_0_), channel_id=1, source_target_pairs={{0,4},{4,0},{1,5},{5,1},{2,6},{6,2},{3,7},{7,3},{8,12},{12,8},{9,1... | collective-permute-start | bytes 3538952 | tf_op jit(solution)/shard_map/ppermute | solution.py:150
  20.4 1.9 %collective-permute-start = (bf16[144,2048]{1,0:T(8,128)(2,1)}, bf16[144,2048]{1,0:T(8,128)(2,1)S(1)}, u32[]{:S(2)}, u32[]{:S(2)}) collective-permute-start(bf16[144,2048]{1,0:T(8,128)(2,1)} %refs_0_.1), channel_id=1, source_target_pairs={{0,4},{4,0},{1,5},{5,1},{2,6},{6,2},{3,7},{7,3},{8,12},{12,8},{9,1... | collective-permute-start | bytes 1769480 | tf_op jit(solution)/shard_map/ppermute | solution.py:158
  22.3 4.6 %collective-permute-start.4 = (bf16[144,2048]{1,0:T(8,128)(2,1)}, bf16[144,2048]{1,0:T(8,128)(2,1)}, u32[]{:S(2)}, u32[]{:S(2)}) collective-permute-start(bf16[144,2048]{1,0:T(8,128)(2,1)} %refs_0_.1), channel_id=1, source_target_pairs={{192,0},{384,192},{576,384},{0,576},{193,1},{385,193},{577,385},{1... | collective-permute-start | bytes 1769480 | tf_op jit(solution)/shard_map/ppermute | solution.py:155
  26.9 1.9 %collective-permute-start.6 = (bf16[144,2048]{1,0:T(8,128)(2,1)}, bf16[144,2048]{1,0:T(8,128)(2,1)}, u32[]{:S(2)}, u32[]{:S(2)}) collective-permute-start(bf16[144,2048]{1,0:T(8,128)(2,1)} %refs_0_.1), channel_id=1, source_target_pairs={{576,0},{0,192},{192,384},{384,576},{577,1},{1,193},{193,385},{385... | collective-permute-start | bytes 1769480 | tf_op jit(solution)/shard_map/ppermute | solution.py:155
  28.8 0.0 collective-permute-done.refs_1_
  28.8 0.0 copy-start.1
  28.8 0.8 copy-done.1
  29.6 8.5 %all-to-all-done.block_ref = bf16[96,2,2048]{2,1,0:T(2,128)(2,1)S(1)} async-done(((bf16[96,2,2048]{2,1,0:T(2,128)(2,1)}), bf16[96,2,2048]{2,1,0:T(2,128)(2,1)S(1)}, u32[]{:S(2)}, u32[]{:S(2)}) %all-to-all-start) | async-done | bytes 786464 | tf_op jit(solution)/shard_map/all_to_all | solution.py:19
  38.2 0.0 collective-permute-done.1.refs_1_
  38.2 1.6 %shard_map.47 = bf16[4,72,384]{2,1,0:T(8,128)(2,1)} custom-call(bf16[96,2,2048]{2,1,0:T(2,128)(2,1)S(1)} %all-to-all-done.block_ref, bf16[288,2048]{1,0:T(8,128)(2,1)S(1)} %constant_dynamic-update-slice_fusion.refs_0_, bf16[288,2048]{1,0:T(8,128)(2,1)S(1)} %collective-permute-done.1.refs_1_), custom_call_target="tpu_custom_call" | custom-call | flops 452984832 | bytes 3366912 | tf_op jit(solution)/shard_map/pallas_call | solution.py:71
  39.8 0.0 copy-start.2
  39.8 12.4 %all-to-all-start.1 = ((bf16[4,72,384]{2,1,0:T(8,128)(2,1)}), bf16[4,72,384]{2,1,0:T(8,128)(2,1)S(1)}, u32[]{:S(2)}, u32[]{:S(2)}) async-start(bf16[4,72,384]{2,1,0:T(8,128)(2,1)} %shard_map.47), calls=%async_computation.1 | async-start | bytes 442368 | tf_op jit(solution)/shard_map/all_to_all | solution.py:19
  52.2 4.5 %collective-permute-start.2 = (bf16[144,2048]{1,0:T(8,128)(2,1)}, bf16[144,2048]{1,0:T(8,128)(2,1)S(1)}, u32[]{:S(2)}, u32[]{:S(2)}) collective-permute-start(bf16[144,2048]{1,0:T(8,128)(2,1)} %refs_0_.1), channel_id=1, source_target_pairs={{384,0},{576,192},{0,384},{192,576},{385,1},{577,193},{1,385},{193... | collective-permute-start | bytes 1769480 | tf_op jit(solution)/shard_map/ppermute | solution.py:155
  56.7 0.0 collective-permute-done.4.refs_2_
  56.7 5.0 %collective-permute-start.5 = (bf16[144,2048]{1,0:T(8,128)(2,1)}, bf16[144,2048]{1,0:T(8,128)(2,1)S(1)}, u32[]{:S(2)}, u32[]{:S(2)}) collective-permute-start(bf16[144,2048]{1,0:T(8,128)(2,1)} %collective-permute-done.4.refs_2_), channel_id=1, source_target_pairs={{0,4},{4,0},{1,5},{5,1},{2,6},{6,2},{3,7},{7,3},{8,12},{12,8},{9,1... | collective-permute-start | bytes 1769480 | tf_op jit(solution)/shard_map/ppermute | solution.py:163
  61.7 0.0 collective-permute-done.6.refs_4_
  61.7 1.9 %collective-permute-start.7 = (bf16[144,2048]{1,0:T(8,128)(2,1)}, bf16[144,2048]{1,0:T(8,128)(2,1)S(1)}, u32[]{:S(2)}, u32[]{:S(2)}) collective-permute-start(bf16[144,2048]{1,0:T(8,128)(2,1)} %collective-permute-done.6.refs_4_), channel_id=1, source_target_pairs={{0,4},{4,0},{1,5},{5,1},{2,6},{6,2},{3,7},{7,3},{8,12},{12,8},{9,1... | collective-permute-start | bytes 1769480 | tf_op jit(solution)/shard_map/ppermute | solution.py:163
  63.6 0.0 all-to-all-done.1.parts_ref
  63.6 0.9 shard_map.48
  64.5 11.0 %all-to-all-start.2 = ((bf16[16,48,72]{2,1,0:T(8,128)(2,1)}), bf16[16,48,72]{2,1,0:T(8,128)(2,1)S(1)}, u32[]{:S(2)}, u32[]{:S(2)}) async-start(bf16[16,48,72]{2,1,0:T(8,128)(2,1)} %bitcast.1), calls=%async_computation.2 | async-start | bytes 393216 | tf_op jit(solution)/shard_map/all_to_all | solution.py:19
  75.5 0.0 collective-permute-done.2.refs_0_
  75.5 2.7 %collective-permute-start.3 = (bf16[144,2048]{1,0:T(8,128)(2,1)S(1)}, bf16[144,2048]{1,0:T(8,128)(2,1)S(1)}, u32[]{:S(2)}, u32[]{:S(2)}) collective-permute-start(bf16[144,2048]{1,0:T(8,128)(2,1)S(1)} %collective-permute-done.2.refs_0_), channel_id=1, source_target_pairs={{0,4},{4,0},{1,5},{5,1},{2,6},{6,2},{3,7},{7,3},{8,12},{12,8},{9,1... | collective-permute-start | bytes 1769480 | tf_op jit(solution)/shard_map/ppermute | solution.py:163
  78.2 0.0 collective-permute-done.5.refs_3_
  78.2 0.0 collective-permute-done.7.refs_5_
  78.2 9.4 %all-to-all-done.2.hidden_ref = bf16[16,48,72]{2,1,0:T(8,128)(2,1)S(1)} async-done(((bf16[16,48,72]{2,1,0:T(8,128)(2,1)}), bf16[16,48,72]{2,1,0:T(8,128)(2,1)S(1)}, u32[]{:S(2)}, u32[]{:S(2)}) %all-to-all-start.2) | async-done | bytes 110624 | tf_op jit(solution)/shard_map/all_to_all | solution.py:19
  87.7 0.0 copy-done.2
  87.7 2.1 %shard_map.49.refs_2_ = f32[48,2048]{1,0:T(8,128)S(1)} custom-call(s32[1]{0:T(128)} %bitcast.here_ref, bf16[16,48,72]{2,1,0:T(8,128)(2,1)S(1)} %all-to-all-done.2.hidden_ref, bf16[144,2048]{1,0:T(8,128)(2,1)} %refs_0_.1, bf16[144,2048]{1,0:T(8,128)(2,1)S(1)} %copy-done.2, bf16[144,2048]{1,0:T(8,128)(2,1)} %collective-permute-done.4.refs_2_, ...), custom_call_target="tpu_custom_call" | custom-call | flops 10871635968 | bytes 3818496 | tf_op jit(solution)/shard_map/pallas_call | solution.py:125
  89.8 0.0 collective-permute-done.3.refs_1_
  89.8 0.4 shard_map.50
  90.2 0.1 reshape.12
  90.3 17.3 %all_to_all.20 = bf16[24,2,2048]{2,1,0:T(2,128)(2,1)S(1)} all-to-all(bf16[24,2,2048]{2,1,0:T(2,128)(2,1)S(1)} %reshape.12), channel_id=1, replica_groups=mesh['x'=4,'plane'=24,'core'=2,'tp'=4] {'plane'}, dimensions={0} | all-to-all | bytes 393216 | tf_op jit(solution)/shard_map/all_to_all | solution.py:19
  107.6 0.8 reduce_sum.12
  (2 shorter events, 0.1 us)
Async XLA Ops:
  0.0 0.7 copy-start
  0.7 16.5 %copy-start.3 = (bf16[144,2048]{1,0:T(8,128)(2,1)S(1)}, bf16[144,2048]{1,0:T(8,128)(2,1)}, u32[]{:S(2)}) copy-start(bf16[144,2048]{1,0:T(8,128)(2,1)} %param.5) | copy-start | bytes 1769476
  1.7 15.6 %copy-start.4 = (bf16[144,2048]{1,0:T(8,128)(2,1)S(1)}, bf16[144,2048]{1,0:T(8,128)(2,1)}, u32[]{:S(2)}) copy-start(bf16[144,2048]{1,0:T(8,128)(2,1)} %param.6) | copy-start | bytes 1769476
  1.7 36.5 %all-to-all-start = ((bf16[96,2,2048]{2,1,0:T(2,128)(2,1)}), bf16[96,2,2048]{2,1,0:T(2,128)(2,1)S(1)}, u32[]{:S(2)}, u32[]{:S(2)}) async-start(bf16[96,2,2048]{2,1,0:T(2,128)(2,1)} %shard_map.46), calls=%async_computation | async-start | bytes 1572864 | tf_op jit(solution)/shard_map/all_to_all | solution.py:19
  17.3 20.9 %collective-permute-start.1 = (bf16[288,2048]{1,0:T(8,128)(2,1)S(1)}, bf16[288,2048]{1,0:T(8,128)(2,1)S(1)}, u32[]{:S(2)}, u32[]{:S(2)}) collective-permute-start(bf16[288,2048]{1,0:T(8,128)(2,1)S(1)} %constant_dynamic-update-slice_fusion.refs_0_), channel_id=1, source_target_pairs={{0,4},{4,0},{1,5},{5,1},{2,6},{6,2},{3,7},{7,3},{8,12},{12,8},{9,1... | collective-permute-start | bytes 3538952 | tf_op jit(solution)/shard_map/ppermute | solution.py:150
  20.4 8.4 %collective-permute-start = (bf16[144,2048]{1,0:T(8,128)(2,1)}, bf16[144,2048]{1,0:T(8,128)(2,1)S(1)}, u32[]{:S(2)}, u32[]{:S(2)}) collective-permute-start(bf16[144,2048]{1,0:T(8,128)(2,1)} %refs_0_.1), channel_id=1, source_target_pairs={{0,4},{4,0},{1,5},{5,1},{2,6},{6,2},{3,7},{7,3},{8,12},{12,8},{9,1... | collective-permute-start | bytes 1769480 | tf_op jit(solution)/shard_map/ppermute | solution.py:158
  22.3 34.4 %collective-permute-start.4 = (bf16[144,2048]{1,0:T(8,128)(2,1)}, bf16[144,2048]{1,0:T(8,128)(2,1)}, u32[]{:S(2)}, u32[]{:S(2)}) collective-permute-start(bf16[144,2048]{1,0:T(8,128)(2,1)} %refs_0_.1), channel_id=1, source_target_pairs={{192,0},{384,192},{576,384},{0,576},{193,1},{385,193},{577,385},{1... | collective-permute-start | bytes 1769480 | tf_op jit(solution)/shard_map/ppermute | solution.py:155
  26.9 34.8 %collective-permute-start.6 = (bf16[144,2048]{1,0:T(8,128)(2,1)}, bf16[144,2048]{1,0:T(8,128)(2,1)}, u32[]{:S(2)}, u32[]{:S(2)}) collective-permute-start(bf16[144,2048]{1,0:T(8,128)(2,1)} %refs_0_.1), channel_id=1, source_target_pairs={{576,0},{0,192},{192,384},{384,576},{577,1},{1,193},{193,385},{385... | collective-permute-start | bytes 1769480 | tf_op jit(solution)/shard_map/ppermute | solution.py:155
  28.8 0.8 copy-start.1
  39.8 47.9 %copy-start.2 = (bf16[144,2048]{1,0:T(8,128)(2,1)S(1)}, bf16[144,2048]{1,0:T(8,128)(2,1)}, u32[]{:S(2)}) copy-start(bf16[144,2048]{1,0:T(8,128)(2,1)} %copy-done.1) | copy-start | bytes 1769476
  39.8 23.9 %all-to-all-start.1 = ((bf16[4,72,384]{2,1,0:T(8,128)(2,1)}), bf16[4,72,384]{2,1,0:T(8,128)(2,1)S(1)}, u32[]{:S(2)}, u32[]{:S(2)}) async-start(bf16[4,72,384]{2,1,0:T(8,128)(2,1)} %shard_map.47), calls=%async_computation.1 | async-start | bytes 442368 | tf_op jit(solution)/shard_map/all_to_all | solution.py:19
  52.2 23.3 %collective-permute-start.2 = (bf16[144,2048]{1,0:T(8,128)(2,1)}, bf16[144,2048]{1,0:T(8,128)(2,1)S(1)}, u32[]{:S(2)}, u32[]{:S(2)}) collective-permute-start(bf16[144,2048]{1,0:T(8,128)(2,1)} %refs_0_.1), channel_id=1, source_target_pairs={{384,0},{576,192},{0,384},{192,576},{385,1},{577,193},{1,385},{193... | collective-permute-start | bytes 1769480 | tf_op jit(solution)/shard_map/ppermute | solution.py:155
  56.7 21.5 %collective-permute-start.5 = (bf16[144,2048]{1,0:T(8,128)(2,1)}, bf16[144,2048]{1,0:T(8,128)(2,1)S(1)}, u32[]{:S(2)}, u32[]{:S(2)}) collective-permute-start(bf16[144,2048]{1,0:T(8,128)(2,1)} %collective-permute-done.4.refs_2_), channel_id=1, source_target_pairs={{0,4},{4,0},{1,5},{5,1},{2,6},{6,2},{3,7},{7,3},{8,12},{12,8},{9,1... | collective-permute-start | bytes 1769480 | tf_op jit(solution)/shard_map/ppermute | solution.py:163
  61.7 16.5 %collective-permute-start.7 = (bf16[144,2048]{1,0:T(8,128)(2,1)}, bf16[144,2048]{1,0:T(8,128)(2,1)S(1)}, u32[]{:S(2)}, u32[]{:S(2)}) collective-permute-start(bf16[144,2048]{1,0:T(8,128)(2,1)} %collective-permute-done.6.refs_4_), channel_id=1, source_target_pairs={{0,4},{4,0},{1,5},{5,1},{2,6},{6,2},{3,7},{7,3},{8,12},{12,8},{9,1... | collective-permute-start | bytes 1769480 | tf_op jit(solution)/shard_map/ppermute | solution.py:163
  64.5 23.2 %all-to-all-start.2 = ((bf16[16,48,72]{2,1,0:T(8,128)(2,1)}), bf16[16,48,72]{2,1,0:T(8,128)(2,1)S(1)}, u32[]{:S(2)}, u32[]{:S(2)}) async-start(bf16[16,48,72]{2,1,0:T(8,128)(2,1)} %bitcast.1), calls=%async_computation.2 | async-start | bytes 393216 | tf_op jit(solution)/shard_map/all_to_all | solution.py:19
  75.5 14.3 %collective-permute-start.3 = (bf16[144,2048]{1,0:T(8,128)(2,1)S(1)}, bf16[144,2048]{1,0:T(8,128)(2,1)S(1)}, u32[]{:S(2)}, u32[]{:S(2)}) collective-permute-start(bf16[144,2048]{1,0:T(8,128)(2,1)S(1)} %collective-permute-done.2.refs_0_), channel_id=1, source_target_pairs={{0,4},{4,0},{1,5},{5,1},{2,6},{6,2},{3,7},{7,3},{8,12},{12,8},{9,1... | collective-permute-start | bytes 1769480 | tf_op jit(solution)/shard_map/ppermute | solution.py:163

commit v10 on v9

--- a/solution.py
+++ b/solution.py
@@ -19,8 +19,11 @@
     return lax.all_to_all(chunks, axes, split_axis=0, concat_axis=0, tiled=True)
 
 
-def spread_kernel(rows_ref, out_ref, held, sems):
-    held[...] = jnp.broadcast_to(rows_ref[...][None], held.shape)
+def spread_kernel(rows_ref, out_ref, rows, held, row_sem, sems):
+    load = pltpu.make_async_copy(rows_ref, rows, row_sem)
+    load.start()
+    load.wait()
+    held[...] = jnp.broadcast_to(rows[...][None], held.shape)
     size = held.shape[0]
     copies = [
         pltpu.make_async_copy(held, out_ref.at[pl.ds(i * size, size)], sems.at[i])
@@ -36,10 +39,12 @@
     return pl.pallas_call(
         spread_kernel,
         out_shape=jax.ShapeDtypeStruct((copies, *rows.shape), rows.dtype),
-        in_specs=[pl.BlockSpec(memory_space=pltpu.VMEM)],
+        in_specs=[pl.BlockSpec(memory_space=pltpu.HBM)],
         out_specs=pl.BlockSpec(memory_space=pl.ANY),
         scratch_shapes=[
+            pltpu.VMEM(rows.shape, rows.dtype),
             pltpu.VMEM((copies // blocks, *rows.shape), rows.dtype),
+            pltpu.SemaphoreType.DMA,
             pltpu.SemaphoreType.DMA((blocks,)),
         ],
         compiler_params=pltpu.CompilerParams(vmem_limit_bytes=8 * 2**20),
@@ -105,29 +110,54 @@
     )(parts)
 
 
-def down_kernel(line, places, here_ref, hidden_ref, *refs):
-    weights, out_ref = refs[: len(places)], refs[-1]
+def down_kernel(line, places, totals, moved, here_ref, hidden_ref, *refs):
+    weights, more = refs[: len(places)], refs[len(places) :]
+    total_refs, out_ref, room = more[:totals], more[totals], more[totals + 1 :]
     tp = hidden_ref.shape[0] // line
     half = tp // 2
-    total = refs[-2][...] if len(refs) > len(places) + 1 else jnp.zeros(out_ref.shape, jnp.float32)
-    for (step, core), weight_ref in zip(places, weights):
+    copies = [
+        pltpu.make_async_copy(weights[at], room[0].at[slot], room[1].at[slot])
+        for slot, at in enumerate(moved)
+    ]
+    for copy in copies:
+        copy.start()
+
+    def terms(at, weight):
+        step, core = places[at]
         first = lax.rem(here_ref[0] + step, line) * tp + core * half
         units = jnp.concatenate([hidden_ref[first + i] for i in range(half)], axis=1)
-        total += jnp.dot(units, weight_ref[...], preferred_element_type=jnp.float32)
+        return jnp.dot(units, weight, preferred_element_type=jnp.float32)
+
+    total = sum((ref[...] for ref in total_refs), jnp.zeros(out_ref.shape, jnp.float32))
+    for at in range(len(places)):
+        if at not in moved:
+            total += terms(at, weights[at][...])
+    for slot, at in enumerate(moved):
+        copies[slot].wait()
+        total += terms(at, room[0][slot])
     out_ref[...] = total.astype(out_ref.dtype)
 
 
 def down_product(hidden, weights, here, line, dtype, *total):
-    column, width = hidden.shape[1], next(iter(weights.values())).shape[1]
-    units = sum(weight.shape[0] for weight in weights.values())
+    depth, width = next(iter(weights.values())).shape
+    column = hidden.shape[1]
+    units = depth * len(weights)
     weight_of = 1 if total else 64
+    moved = [at for at, (step, core) in enumerate(weights) if step and not core and not total]
     vmem = pl.BlockSpec(memory_space=pltpu.VMEM)
     return pl.pallas_call(
-        functools.partial(down_kernel, line, tuple(weights)),
+        functools.partial(down_kernel, line, tuple(weights), len(total), moved),
         out_shape=jax.ShapeDtypeStruct((column, width), dtype),
-        in_specs=[pl.BlockSpec(memory_space=pltpu.SMEM)]
-        + [vmem] * (1 + len(weights) + len(total)),
+        in_specs=[pl.BlockSpec(memory_space=pltpu.SMEM), vmem]
+        + [pl.BlockSpec(memory_space=pl.ANY) if at in moved else vmem for at in range(len(weights))]
+        + [vmem] * len(total),
         out_specs=vmem,
+        scratch_shapes=[
+            pltpu.VMEM((len(moved), depth, width), hidden.dtype),
+            pltpu.SemaphoreType.DMA((len(moved),)),
+        ]
+        if moved
+        else [],
         cost_estimate=pl.CostEstimate(
             flops=weight_of * 2 * column * units * width,
             bytes_accessed=2 * (units * width + column * width + column * units),
@@ -148,7 +178,7 @@
 
     stack = jnp.concatenate([gate_weight, up_weight], axis=0)
     other_stack = lax.ppermute(stack, CORE, swap)
-    block = spread_rows(tokens, line * plane, 2 * line)
+    block = spread_rows(pltpu.with_memory_space_constraint(tokens, pltpu.HBM), line * plane, 2 * line)
     block = exchange(block, (X, PLANE))
 
     gathered = [

time: 109 us -> 110 us (level)
  Pallas kernels: 5.86 us -> 7.15 us
  transfers between devices with their start and end apart: 11 -> 11, of which waited for: 2 -> 2; matrix products, arithmetic and copies ran while one was open for 0% -> 0% of each run, Pallas kernels for 4% -> 5%
where the time goes in v10:
time: 110 us; the launch traced here: 109 us
  starting transfers between devices  64.4 us (59%)
  waiting for transfers between devices  18 us (16%)
  blocking collectives  17.3 us (16%)
  Pallas kernels  7.15 us (6%)
    all_to_all x3, starting transfers between devices, exchange(): return lax.all_to_all(chunks, axes, split_axis=0, concat_axis=0, tiled=True)  38.9 us
    all_to_all x3, waiting for transfers between devices, exchange(): return lax.all_to_all(chunks, axes, split_axis=0, concat_axis=0, tiled=True)  18 us
    all_to_all x1, blocking collectives, exchange(): return lax.all_to_all(chunks, axes, split_axis=0, concat_axis=0, tiled=True)  17.3 us
    ppermute x3, starting transfers between devices, body(): lax.ppermute(down_weight, X, [((i + step) % line, i) for i in range(line)])  10.9 us
    ppermute x3, starting transfers between devices, body(): swapped = [lax.ppermute(weight, CORE, swap) for weight in gathered]  9.63 us
    ppermute x1, starting transfers between devices, body(): other_stack = lax.ppermute(stack, CORE, swap)  3.04 us
    pallas_call x2, Pallas kernels, down_product(): pl.pallas_call(functools.partial(down_kernel, line, tuple(weights), len(t...  2.97 us
  transfers between devices with their start and end apart: 11, of which 2 were waited for; matrix products, arithmetic and copies ran while one was open for 0% of the time, Pallas kernels for 5%

profile of v10, /device:TPU:1, one launch (start us, length us, event | category | flops | bytes accessed | tf_op | source)
XLA Modules:
  0.0 109.0 jit_solution(12479907204777989179)
XLA Ops:
  0.0 0.0 copy-start.2
  0.0 1.7 %shard_map.46 = bf16[96,2,2048]{2,1,0:T(2,128)(2,1)} custom-call(bf16[2,2048]{1,0:T(2,128)(2,1)} %rows_ref.1), custom_call_target="tpu_custom_call" | custom-call | tf_op jit(solution)/shard_map/pallas_call | solution.py:39
  1.8 0.0 copy-start.3
  1.8 15.5 %all-to-all-start = ((bf16[96,2,2048]{2,1,0:T(2,128)(2,1)}), bf16[96,2,2048]{2,1,0:T(2,128)(2,1)S(1)}, u32[]{:S(2)}, u32[]{:S(2)}) async-start(bf16[96,2,2048]{2,1,0:T(2,128)(2,1)} %shard_map.46), calls=%async_computation | async-start | bytes 1572864 | tf_op jit(solution)/shard_map/all_to_all | solution.py:19
  17.3 0.0 copy-done.2
  17.3 0.0 copy-done.3
  17.4 3.0 %collective-permute-start.1 = (bf16[288,2048]{1,0:T(8,128)(2,1)S(1)}, bf16[288,2048]{1,0:T(8,128)(2,1)S(1)}, u32[]{:S(2)}, u32[]{:S(2)}) collective-permute-start(bf16[288,2048]{1,0:T(8,128)(2,1)S(1)} %constant_dynamic-update-slice_fusion.refs_0_), channel_id=1, source_target_pairs={{0,4},{4,0},{1,5},{5,1},{2,6},{6,2},{3,7},{7,3},{8,12},{12,8},{9,1... | collective-permute-start | bytes 3538952 | tf_op jit(solution)/shard_map/ppermute | solution.py:180
  20.4 1.9 %collective-permute-start = (bf16[144,2048]{1,0:T(8,128)(2,1)}, bf16[144,2048]{1,0:T(8,128)(2,1)S(1)}, u32[]{:S(2)}, u32[]{:S(2)}) collective-permute-start(bf16[144,2048]{1,0:T(8,128)(2,1)} %refs_0_.1), channel_id=1, source_target_pairs={{0,4},{4,0},{1,5},{5,1},{2,6},{6,2},{3,7},{7,3},{8,12},{12,8},{9,1... | collective-permute-start | bytes 1769480 | tf_op jit(solution)/shard_map/ppermute | solution.py:188
  22.4 4.6 %collective-permute-start.4 = (bf16[144,2048]{1,0:T(8,128)(2,1)}, bf16[144,2048]{1,0:T(8,128)(2,1)}, u32[]{:S(2)}, u32[]{:S(2)}) collective-permute-start(bf16[144,2048]{1,0:T(8,128)(2,1)} %refs_0_.1), channel_id=1, source_target_pairs={{192,0},{384,192},{576,384},{0,576},{193,1},{385,193},{577,385},{1... | collective-permute-start | bytes 1769480 | tf_op jit(solution)/shard_map/ppermute | solution.py:185
  26.9 1.9 %collective-permute-start.6 = (bf16[144,2048]{1,0:T(8,128)(2,1)}, bf16[144,2048]{1,0:T(8,128)(2,1)}, u32[]{:S(2)}, u32[]{:S(2)}) collective-permute-start(bf16[144,2048]{1,0:T(8,128)(2,1)} %refs_0_.1), channel_id=1, source_target_pairs={{576,0},{0,192},{192,384},{384,576},{577,1},{1,193},{193,385},{385... | collective-permute-start | bytes 1769480 | tf_op jit(solution)/shard_map/ppermute | solution.py:185
  28.9 0.0 collective-permute-done.refs_1_
  28.9 0.0 copy-start
  28.9 0.8 copy-done
  29.7 8.6 %all-to-all-done.block_ref = bf16[96,2,2048]{2,1,0:T(2,128)(2,1)S(1)} async-done(((bf16[96,2,2048]{2,1,0:T(2,128)(2,1)}), bf16[96,2,2048]{2,1,0:T(2,128)(2,1)S(1)}, u32[]{:S(2)}, u32[]{:S(2)}) %all-to-all-start) | async-done | bytes 786464 | tf_op jit(solution)/shard_map/all_to_all | solution.py:19
  38.3 0.0 collective-permute-done.1.refs_1_
  38.3 1.6 %shard_map.47 = bf16[4,72,384]{2,1,0:T(8,128)(2,1)} custom-call(bf16[96,2,2048]{2,1,0:T(2,128)(2,1)S(1)} %all-to-all-done.block_ref, bf16[288,2048]{1,0:T(8,128)(2,1)S(1)} %constant_dynamic-update-slice_fusion.refs_0_, bf16[288,2048]{1,0:T(8,128)(2,1)S(1)} %collective-permute-done.1.refs_1_), custom_call_target="tpu_custom_call" | custom-call | flops 452984832 | bytes 3366912 | tf_op jit(solution)/shard_map/pallas_call | solution.py:76
  39.8 0.0 copy-start.1
  39.8 12.4 %all-to-all-start.1 = ((bf16[4,72,384]{2,1,0:T(8,128)(2,1)}), bf16[4,72,384]{2,1,0:T(8,128)(2,1)S(1)}, u32[]{:S(2)}, u32[]{:S(2)}) async-start(bf16[4,72,384]{2,1,0:T(8,128)(2,1)} %shard_map.47), calls=%async_computation.1 | async-start | bytes 442368 | tf_op jit(solution)/shard_map/all_to_all | solution.py:19
  52.2 4.5 %collective-permute-start.2 = (bf16[144,2048]{1,0:T(8,128)(2,1)}, bf16[144,2048]{1,0:T(8,128)(2,1)S(1)}, u32[]{:S(2)}, u32[]{:S(2)}) collective-permute-start(bf16[144,2048]{1,0:T(8,128)(2,1)} %refs_0_.1), channel_id=1, source_target_pairs={{384,0},{576,192},{0,384},{192,576},{385,1},{577,193},{1,385},{193... | collective-permute-start | bytes 1769480 | tf_op jit(solution)/shard_map/ppermute | solution.py:185
  56.7 0.0 collective-permute-done.4.refs_2_
  56.7 5.0 %collective-permute-start.5 = (bf16[144,2048]{1,0:T(8,128)(2,1)}, bf16[144,2048]{1,0:T(8,128)(2,1)S(1)}, u32[]{:S(2)}, u32[]{:S(2)}) collective-permute-start(bf16[144,2048]{1,0:T(8,128)(2,1)} %collective-permute-done.4.refs_2_), channel_id=1, source_target_pairs={{0,4},{4,0},{1,5},{5,1},{2,6},{6,2},{3,7},{7,3},{8,12},{12,8},{9,1... | collective-permute-start | bytes 1769480 | tf_op jit(solution)/shard_map/ppermute | solution.py:193
  61.8 0.0 collective-permute-done.6.refs_4_
  61.8 1.9 %collective-permute-start.7 = (bf16[144,2048]{1,0:T(8,128)(2,1)}, bf16[144,2048]{1,0:T(8,128)(2,1)S(1)}, u32[]{:S(2)}, u32[]{:S(2)}) collective-permute-start(bf16[144,2048]{1,0:T(8,128)(2,1)} %collective-permute-done.6.refs_4_), channel_id=1, source_target_pairs={{0,4},{4,0},{1,5},{5,1},{2,6},{6,2},{3,7},{7,3},{8,12},{12,8},{9,1... | collective-permute-start | bytes 1769480 | tf_op jit(solution)/shard_map/ppermute | solution.py:193
  63.7 0.0 all-to-all-done.1.parts_ref
  63.7 0.9 shard_map.48
  64.6 11.0 %all-to-all-start.2 = ((bf16[16,48,72]{2,1,0:T(8,128)(2,1)}), bf16[16,48,72]{2,1,0:T(8,128)(2,1)S(1)}, u32[]{:S(2)}, u32[]{:S(2)}) async-start(bf16[16,48,72]{2,1,0:T(8,128)(2,1)} %bitcast.1), calls=%async_computation.2 | async-start | bytes 393216 | tf_op jit(solution)/shard_map/all_to_all | solution.py:19
  75.6 0.0 collective-permute-done.2.refs_0_
  75.6 2.7 %collective-permute-start.3 = (bf16[144,2048]{1,0:T(8,128)(2,1)S(1)}, bf16[144,2048]{1,0:T(8,128)(2,1)S(1)}, u32[]{:S(2)}, u32[]{:S(2)}) collective-permute-start(bf16[144,2048]{1,0:T(8,128)(2,1)S(1)} %collective-permute-done.2.refs_0_), channel_id=1, source_target_pairs={{0,4},{4,0},{1,5},{5,1},{2,6},{6,2},{3,7},{7,3},{8,12},{12,8},{9,1... | collective-permute-start | bytes 1769480 | tf_op jit(solution)/shard_map/ppermute | solution.py:193
  78.3 0.0 collective-permute-done.5.refs_3_
  78.3 0.0 collective-permute-done.7.refs_5_
  78.3 9.5 %all-to-all-done.2.hidden_ref = bf16[16,48,72]{2,1,0:T(8,128)(2,1)S(1)} async-done(((bf16[16,48,72]{2,1,0:T(8,128)(2,1)}), bf16[16,48,72]{2,1,0:T(8,128)(2,1)S(1)}, u32[]{:S(2)}, u32[]{:S(2)}) %all-to-all-start.2) | async-done | bytes 110624 | tf_op jit(solution)/shard_map/all_to_all | solution.py:19
  87.7 0.0 copy-done.1
  87.7 2.6 %shard_map.49.refs_2_ = f32[48,2048]{1,0:T(8,128)S(1)} custom-call(s32[1]{0:T(128)} %bitcast.here_ref, bf16[16,48,72]{2,1,0:T(8,128)(2,1)S(1)} %all-to-all-done.2.hidden_ref, bf16[144,2048]{1,0:T(8,128)(2,1)} %refs_0_.1, bf16[144,2048]{1,0:T(8,128)(2,1)S(1)} %copy-done.1, bf16[144,2048]{1,0:T(8,128)(2,1)} %collective-permute-done.4.refs_2_, ...), custom_call_target="tpu_custom_call" | custom-call | flops 10871635968 | bytes 3818496 | tf_op jit(solution)/shard_map/pallas_call | solution.py:148
  90.4 0.0 collective-permute-done.3.refs_1_
  90.4 0.4 shard_map.50
  90.7 0.1 reshape.12
  90.9 17.3 %all_to_all.20 = bf16[24,2,2048]{2,1,0:T(2,128)(2,1)S(1)} all-to-all(bf16[24,2,2048]{2,1,0:T(2,128)(2,1)S(1)} %reshape.12), channel_id=1, replica_groups=mesh['x'=4,'plane'=24,'core'=2,'tp'=4] {'plane'}, dimensions={0} | all-to-all | bytes 393216 | tf_op jit(solution)/shard_map/all_to_all | solution.py:19
  108.2 0.8 reduce_sum.12
  (2 shorter events, 0.1 us)
Async XLA Ops:
  0.0 17.3 %copy-start.2 = (bf16[144,2048]{1,0:T(8,128)(2,1)S(1)}, bf16[144,2048]{1,0:T(8,128)(2,1)}, u32[]{:S(2)}) copy-start(bf16[144,2048]{1,0:T(8,128)(2,1)} %param.5) | copy-start | bytes 1769476
  1.8 15.6 %copy-start.3 = (bf16[144,2048]{1,0:T(8,128)(2,1)S(1)}, bf16[144,2048]{1,0:T(8,128)(2,1)}, u32[]{:S(2)}) copy-start(bf16[144,2048]{1,0:T(8,128)(2,1)} %param.6) | copy-start | bytes 1769476
  1.8 36.5 %all-to-all-start = ((bf16[96,2,2048]{2,1,0:T(2,128)(2,1)}), bf16[96,2,2048]{2,1,0:T(2,128)(2,1)S(1)}, u32[]{:S(2)}, u32[]{:S(2)}) async-start(bf16[96,2,2048]{2,1,0:T(2,128)(2,1)} %shard_map.46), calls=%async_computation | async-start | bytes 1572864 | tf_op jit(solution)/shard_map/all_to_all | solution.py:19
  17.4 20.9 %collective-permute-start.1 = (bf16[288,2048]{1,0:T(8,128)(2,1)S(1)}, bf16[288,2048]{1,0:T(8,128)(2,1)S(1)}, u32[]{:S(2)}, u32[]{:S(2)}) collective-permute-start(bf16[288,2048]{1,0:T(8,128)(2,1)S(1)} %constant_dynamic-update-slice_fusion.refs_0_), channel_id=1, source_target_pairs={{0,4},{4,0},{1,5},{5,1},{2,6},{6,2},{3,7},{7,3},{8,12},{12,8},{9,1... | collective-permute-start | bytes 3538952 | tf_op jit(solution)/shard_map/ppermute | solution.py:180
  20.4 8.4 %collective-permute-start = (bf16[144,2048]{1,0:T(8,128)(2,1)}, bf16[144,2048]{1,0:T(8,128)(2,1)S(1)}, u32[]{:S(2)}, u32[]{:S(2)}) collective-permute-start(bf16[144,2048]{1,0:T(8,128)(2,1)} %refs_0_.1), channel_id=1, source_target_pairs={{0,4},{4,0},{1,5},{5,1},{2,6},{6,2},{3,7},{7,3},{8,12},{12,8},{9,1... | collective-permute-start | bytes 1769480 | tf_op jit(solution)/shard_map/ppermute | solution.py:188
  22.4 34.3 %collective-permute-start.4 = (bf16[144,2048]{1,0:T(8,128)(2,1)}, bf16[144,2048]{1,0:T(8,128)(2,1)}, u32[]{:S(2)}, u32[]{:S(2)}) collective-permute-start(bf16[144,2048]{1,0:T(8,128)(2,1)} %refs_0_.1), channel_id=1, source_target_pairs={{192,0},{384,192},{576,384},{0,576},{193,1},{385,193},{577,385},{1... | collective-permute-start | bytes 1769480 | tf_op jit(solution)/shard_map/ppermute | solution.py:185
  26.9 34.8 %collective-permute-start.6 = (bf16[144,2048]{1,0:T(8,128)(2,1)}, bf16[144,2048]{1,0:T(8,128)(2,1)}, u32[]{:S(2)}, u32[]{:S(2)}) collective-permute-start(bf16[144,2048]{1,0:T(8,128)(2,1)} %refs_0_.1), channel_id=1, source_target_pairs={{576,0},{0,192},{192,384},{384,576},{577,1},{1,193},{193,385},{385... | collective-permute-start | bytes 1769480 | tf_op jit(solution)/shard_map/ppermute | solution.py:185
  28.9 0.8 copy-start
  39.8 47.9 %copy-start.1 = (bf16[144,2048]{1,0:T(8,128)(2,1)S(1)}, bf16[144,2048]{1,0:T(8,128)(2,1)}, u32[]{:S(2)}) copy-start(bf16[144,2048]{1,0:T(8,128)(2,1)} %copy-done) | copy-start | bytes 1769476
  39.8 23.9 %all-to-all-start.1 = ((bf16[4,72,384]{2,1,0:T(8,128)(2,1)}), bf16[4,72,384]{2,1,0:T(8,128)(2,1)S(1)}, u32[]{:S(2)}, u32[]{:S(2)}) async-start(bf16[4,72,384]{2,1,0:T(8,128)(2,1)} %shard_map.47), calls=%async_computation.1 | async-start | bytes 442368 | tf_op jit(solution)/shard_map/all_to_all | solution.py:19
  52.2 23.3 %collective-permute-start.2 = (bf16[144,2048]{1,0:T(8,128)(2,1)}, bf16[144,2048]{1,0:T(8,128)(2,1)S(1)}, u32[]{:S(2)}, u32[]{:S(2)}) collective-permute-start(bf16[144,2048]{1,0:T(8,128)(2,1)} %refs_0_.1), channel_id=1, source_target_pairs={{384,0},{576,192},{0,384},{192,576},{385,1},{577,193},{1,385},{193... | collective-permute-start | bytes 1769480 | tf_op jit(solution)/shard_map/ppermute | solution.py:185
  56.7 21.6 %collective-permute-start.5 = (bf16[144,2048]{1,0:T(8,128)(2,1)}, bf16[144,2048]{1,0:T(8,128)(2,1)S(1)}, u32[]{:S(2)}, u32[]{:S(2)}) collective-permute-start(bf16[144,2048]{1,0:T(8,128)(2,1)} %collective-permute-done.4.refs_2_), channel_id=1, source_target_pairs={{0,4},{4,0},{1,5},{5,1},{2,6},{6,2},{3,7},{7,3},{8,12},{12,8},{9,1... | collective-permute-start | bytes 1769480 | tf_op jit(solution)/shard_map/ppermute | solution.py:193
  61.8 16.5 %collective-permute-start.7 = (bf16[144,2048]{1,0:T(8,128)(2,1)}, bf16[144,2048]{1,0:T(8,128)(2,1)S(1)}, u32[]{:S(2)}, u32[]{:S(2)}) collective-permute-start(bf16[144,2048]{1,0:T(8,128)(2,1)} %collective-permute-done.6.refs_4_), channel_id=1, source_target_pairs={{0,4},{4,0},{1,5},{5,1},{2,6},{6,2},{3,7},{7,3},{8,12},{12,8},{9,1... | collective-permute-start | bytes 1769480 | tf_op jit(solution)/shard_map/ppermute | solution.py:193
  64.6 23.2 %all-to-all-start.2 = ((bf16[16,48,72]{2,1,0:T(8,128)(2,1)}), bf16[16,48,72]{2,1,0:T(8,128)(2,1)S(1)}, u32[]{:S(2)}, u32[]{:S(2)}) async-start(bf16[16,48,72]{2,1,0:T(8,128)(2,1)} %bitcast.1), calls=%async_computation.2 | async-start | bytes 393216 | tf_op jit(solution)/shard_map/all_to_all | solution.py:19
  75.6 14.8 %collective-permute-start.3 = (bf16[144,2048]{1,0:T(8,128)(2,1)S(1)}, bf16[144,2048]{1,0:T(8,128)(2,1)S(1)}, u32[]{:S(2)}, u32[]{:S(2)}) collective-permute-start(bf16[144,2048]{1,0:T(8,128)(2,1)S(1)} %collective-permute-done.2.refs_0_), channel_id=1, source_target_pairs={{0,4},{4,0},{1,5},{5,1},{2,6},{6,2},{3,7},{7,3},{8,12},{12,8},{9,1... | collective-permute-start | bytes 1769480 | tf_op jit(solution)/shard_map/ppermute | solution.py:193

commit v11 on v9

--- a/solution.py
+++ b/solution.py
@@ -83,14 +83,14 @@
 
 
 def hidden_kernel(parts_ref, out_ref):
-    line, tp, column, _ = out_ref.shape
+    tp, line, column, _ = out_ref.shape
     rows = line * column
     sums = jnp.sum(parts_ref[...].astype(jnp.float32), axis=0)
     hidden = (jax.nn.silu(sums[:, :rows]) * sums[:, rows:]).T.astype(out_ref.dtype)
     for x in range(line):
         block = hidden[x * column : (x + 1) * column]
         for i in range(tp):
-            out_ref[x, i] = block
+            out_ref[i, x] = block
 
 
 def hidden_spread(parts, line, column):
@@ -98,7 +98,7 @@
     vmem = pl.BlockSpec(memory_space=pltpu.VMEM)
     return pl.pallas_call(
         hidden_kernel,
-        out_shape=jax.ShapeDtypeStruct((line, tp, column, share), parts.dtype),
+        out_shape=jax.ShapeDtypeStruct((tp, line, column, share), parts.dtype),
         in_specs=[vmem],
         out_specs=vmem,
         compiler_params=pltpu.CompilerParams(vmem_limit_bytes=8 * 2**20),
@@ -111,8 +111,8 @@
     half = tp // 2
     total = refs[-2][...] if len(refs) > len(places) + 1 else jnp.zeros(out_ref.shape, jnp.float32)
     for (step, core), weight_ref in zip(places, weights):
-        first = lax.rem(here_ref[0] + step, line) * tp + core * half
-        units = jnp.concatenate([hidden_ref[first + i] for i in range(half)], axis=1)
+        first = lax.rem(here_ref[0] + step, line) + core * half * line
+        units = jnp.concatenate([hidden_ref[first + i * line] for i in range(half)], axis=1)
         total += jnp.dot(units, weight_ref[...], preferred_element_type=jnp.float32)
     out_ref[...] = total.astype(out_ref.dtype)
 
@@ -158,7 +158,7 @@
     block, down_other = lax.optimization_barrier((block, lax.ppermute(down_weight, CORE, swap)))
     parts = exchange(up_product(block, (stack, other_stack), tp), TP)
     spread = hidden_spread(parts, line, column)
-    hidden = exchange(spread.reshape(line * tp, column, share), (X, TP))
+    hidden = exchange(spread.reshape(tp * line, column, share), (TP, X))
     here = lax.axis_index(X)
     swapped = [lax.ppermute(weight, CORE, swap) for weight in gathered]
     pairs = [(down_weight, down_other), *zip(gathered, swapped)]

time: 109 us -> 109 us (level)
  no operation moved by 1% of the time
where the time goes in v11:
time: 109 us; the launch traced here: 108 us
  starting transfers between devices  64.4 us (59%)
  waiting for transfers between devices  17.8 us (16%)
  blocking collectives  17.3 us (16%)
  Pallas kernels  5.87 us (5%)
  local copies, waits for them, and re-layouts  1.76 us (2%)
    all_to_all x3, starting transfers between devices, exchange(): return lax.all_to_all(chunks, axes, split_axis=0, concat_axis=0, tiled=True)  38.9 us
    all_to_all x3, waiting for transfers between devices, exchange(): return lax.all_to_all(chunks, axes, split_axis=0, concat_axis=0, tiled=True)  17.8 us
    all_to_all x1, blocking collectives, exchange(): return lax.all_to_all(chunks, axes, split_axis=0, concat_axis=0, tiled=True)  17.3 us
    ppermute x3, starting transfers between devices, body(): lax.ppermute(down_weight, X, [((i + step) % line, i) for i in range(line)])  10.9 us
    ppermute x3, starting transfers between devices, body(): swapped = [lax.ppermute(weight, CORE, swap) for weight in gathered]  9.62 us
    ppermute x1, starting transfers between devices, body(): other_stack = lax.ppermute(stack, CORE, swap)  3.04 us
    pallas_call x2, Pallas kernels, down_product(): pl.pallas_call(functools.partial(down_kernel, line, tuple(weights)), out_...  2.46 us
  transfers between devices with their start and end apart: 11, of which 2 were waited for; matrix products, arithmetic and copies ran while one was open for 0% of the time, Pallas kernels for 4%

profile of v11, /device:TPU:1, one launch (start us, length us, event | category | flops | bytes accessed | tf_op | source)
XLA Modules:
  0.0 108.2 jit_solution(4023561986810800772)
XLA Ops:
  0.0 0.0 copy-start
  0.0 0.7 copy-done
  0.7 0.0 copy-start.3
  0.7 1.0 shard_map.46
  1.7 0.0 copy-start.4
  1.7 15.5 %all-to-all-start = ((bf16[96,2,2048]{2,1,0:T(2,128)(2,1)}), bf16[96,2,2048]{2,1,0:T(2,128)(2,1)S(1)}, u32[]{:S(2)}, u32[]{:S(2)}) async-start(bf16[96,2,2048]{2,1,0:T(2,128)(2,1)} %shard_map.46), calls=%async_computation | async-start | bytes 1572864 | tf_op jit(solution)/shard_map/all_to_all | solution.py:19
  17.2 0.0 copy-done.3
  17.3 0.0 copy-done.4
  17.3 3.0 %collective-permute-start.1 = (bf16[288,2048]{1,0:T(8,128)(2,1)S(1)}, bf16[288,2048]{1,0:T(8,128)(2,1)S(1)}, u32[]{:S(2)}, u32[]{:S(2)}) collective-permute-start(bf16[288,2048]{1,0:T(8,128)(2,1)S(1)} %constant_dynamic-update-slice_fusion.refs_0_), channel_id=1, source_target_pairs={{0,4},{4,0},{1,5},{5,1},{2,6},{6,2},{3,7},{7,3},{8,12},{12,8},{9,1... | collective-permute-start | bytes 3538952 | tf_op jit(solution)/shard_map/ppermute | solution.py:150
  20.4 1.9 %collective-permute-start = (bf16[144,2048]{1,0:T(8,128)(2,1)}, bf16[144,2048]{1,0:T(8,128)(2,1)S(1)}, u32[]{:S(2)}, u32[]{:S(2)}) collective-permute-start(bf16[144,2048]{1,0:T(8,128)(2,1)} %refs_0_.1), channel_id=1, source_target_pairs={{0,4},{4,0},{1,5},{5,1},{2,6},{6,2},{3,7},{7,3},{8,12},{12,8},{9,1... | collective-permute-start | bytes 1769480 | tf_op jit(solution)/shard_map/ppermute | solution.py:158
  22.3 4.6 %collective-permute-start.4 = (bf16[144,2048]{1,0:T(8,128)(2,1)}, bf16[144,2048]{1,0:T(8,128)(2,1)}, u32[]{:S(2)}, u32[]{:S(2)}) collective-permute-start(bf16[144,2048]{1,0:T(8,128)(2,1)} %refs_0_.1), channel_id=1, source_target_pairs={{192,0},{384,192},{576,384},{0,576},{193,1},{385,193},{577,385},{1... | collective-permute-start | bytes 1769480 | tf_op jit(solution)/shard_map/ppermute | solution.py:155
  26.9 1.9 %collective-permute-start.6 = (bf16[144,2048]{1,0:T(8,128)(2,1)}, bf16[144,2048]{1,0:T(8,128)(2,1)}, u32[]{:S(2)}, u32[]{:S(2)}) collective-permute-start(bf16[144,2048]{1,0:T(8,128)(2,1)} %refs_0_.1), channel_id=1, source_target_pairs={{576,0},{0,192},{192,384},{384,576},{577,1},{1,193},{193,385},{385... | collective-permute-start | bytes 1769480 | tf_op jit(solution)/shard_map/ppermute | solution.py:155
  28.8 0.0 collective-permute-done.refs_1_
  28.8 0.0 copy-start.1
  28.8 0.8 copy-done.1
  29.6 8.5 %all-to-all-done.block_ref = bf16[96,2,2048]{2,1,0:T(2,128)(2,1)S(1)} async-done(((bf16[96,2,2048]{2,1,0:T(2,128)(2,1)}), bf16[96,2,2048]{2,1,0:T(2,128)(2,1)S(1)}, u32[]{:S(2)}, u32[]{:S(2)}) %all-to-all-start) | async-done | bytes 786464 | tf_op jit(solution)/shard_map/all_to_all | solution.py:19
  38.2 0.0 collective-permute-done.1.refs_1_
  38.2 1.6 %shard_map.47 = bf16[4,72,384]{2,1,0:T(8,128)(2,1)} custom-call(bf16[96,2,2048]{2,1,0:T(2,128)(2,1)S(1)} %all-to-all-done.block_ref, bf16[288,2048]{1,0:T(8,128)(2,1)S(1)} %constant_dynamic-update-slice_fusion.refs_0_, bf16[288,2048]{1,0:T(8,128)(2,1)S(1)} %collective-permute-done.1.refs_1_), custom_call_target="tpu_custom_call" | custom-call | flops 452984832 | bytes 3366912 | tf_op jit(solution)/shard_map/pallas_call | solution.py:71
  39.8 0.0 copy-start.2
  39.8 12.4 %all-to-all-start.1 = ((bf16[4,72,384]{2,1,0:T(8,128)(2,1)}), bf16[4,72,384]{2,1,0:T(8,128)(2,1)S(1)}, u32[]{:S(2)}, u32[]{:S(2)}) async-start(bf16[4,72,384]{2,1,0:T(8,128)(2,1)} %shard_map.47), calls=%async_computation.1 | async-start | bytes 442368 | tf_op jit(solution)/shard_map/all_to_all | solution.py:19
  52.2 4.5 %collective-permute-start.2 = (bf16[144,2048]{1,0:T(8,128)(2,1)}, bf16[144,2048]{1,0:T(8,128)(2,1)S(1)}, u32[]{:S(2)}, u32[]{:S(2)}) collective-permute-start(bf16[144,2048]{1,0:T(8,128)(2,1)} %refs_0_.1), channel_id=1, source_target_pairs={{384,0},{576,192},{0,384},{192,576},{385,1},{577,193},{1,385},{193... | collective-permute-start | bytes 1769480 | tf_op jit(solution)/shard_map/ppermute | solution.py:155
  56.7 0.0 collective-permute-done.4.refs_2_
  56.7 5.0 %collective-permute-start.5 = (bf16[144,2048]{1,0:T(8,128)(2,1)}, bf16[144,2048]{1,0:T(8,128)(2,1)S(1)}, u32[]{:S(2)}, u32[]{:S(2)}) collective-permute-start(bf16[144,2048]{1,0:T(8,128)(2,1)} %collective-permute-done.4.refs_2_), channel_id=1, source_target_pairs={{0,4},{4,0},{1,5},{5,1},{2,6},{6,2},{3,7},{7,3},{8,12},{12,8},{9,1... | collective-permute-start | bytes 1769480 | tf_op jit(solution)/shard_map/ppermute | solution.py:163
  61.7 0.0 collective-permute-done.6.refs_4_
  61.7 1.9 %collective-permute-start.7 = (bf16[144,2048]{1,0:T(8,128)(2,1)}, bf16[144,2048]{1,0:T(8,128)(2,1)S(1)}, u32[]{:S(2)}, u32[]{:S(2)}) collective-permute-start(bf16[144,2048]{1,0:T(8,128)(2,1)} %collective-permute-done.6.refs_4_), channel_id=1, source_target_pairs={{0,4},{4,0},{1,5},{5,1},{2,6},{6,2},{3,7},{7,3},{8,12},{12,8},{9,1... | collective-permute-start | bytes 1769480 | tf_op jit(solution)/shard_map/ppermute | solution.py:163
  63.6 0.0 all-to-all-done.1.parts_ref
  63.6 0.9 shard_map.48
  64.5 11.0 %all-to-all-start.2 = ((bf16[16,48,72]{2,1,0:T(8,128)(2,1)}), bf16[16,48,72]{2,1,0:T(8,128)(2,1)S(1)}, u32[]{:S(2)}, u32[]{:S(2)}) async-start(bf16[16,48,72]{2,1,0:T(8,128)(2,1)} %bitcast.1), calls=%async_computation.2 | async-start | bytes 393216 | tf_op jit(solution)/shard_map/all_to_all | solution.py:19
  75.5 0.0 collective-permute-done.2.refs_0_
  75.5 2.7 %collective-permute-start.3 = (bf16[144,2048]{1,0:T(8,128)(2,1)S(1)}, bf16[144,2048]{1,0:T(8,128)(2,1)S(1)}, u32[]{:S(2)}, u32[]{:S(2)}) collective-permute-start(bf16[144,2048]{1,0:T(8,128)(2,1)S(1)} %collective-permute-done.2.refs_0_), channel_id=1, source_target_pairs={{0,4},{4,0},{1,5},{5,1},{2,6},{6,2},{3,7},{7,3},{8,12},{12,8},{9,1... | collective-permute-start | bytes 1769480 | tf_op jit(solution)/shard_map/ppermute | solution.py:163
  78.2 0.0 collective-permute-done.5.refs_3_
  78.2 0.0 collective-permute-done.7.refs_5_
  78.2 9.2 %all-to-all-done.2.hidden_ref = bf16[16,48,72]{2,1,0:T(8,128)(2,1)S(1)} async-done(((bf16[16,48,72]{2,1,0:T(8,128)(2,1)}), bf16[16,48,72]{2,1,0:T(8,128)(2,1)S(1)}, u32[]{:S(2)}, u32[]{:S(2)}) %all-to-all-start.2) | async-done | bytes 110624 | tf_op jit(solution)/shard_map/all_to_all | solution.py:19
  87.5 0.0 copy-done.2
  87.5 2.1 %shard_map.49.refs_2_ = f32[48,2048]{1,0:T(8,128)S(1)} custom-call(s32[1]{0:T(128)} %bitcast.here_ref, bf16[16,48,72]{2,1,0:T(8,128)(2,1)S(1)} %all-to-all-done.2.hidden_ref, bf16[144,2048]{1,0:T(8,128)(2,1)} %refs_0_.1, bf16[144,2048]{1,0:T(8,128)(2,1)S(1)} %copy-done.2, bf16[144,2048]{1,0:T(8,128)(2,1)} %collective-permute-done.4.refs_2_, ...), custom_call_target="tpu_custom_call" | custom-call | flops 10871635968 | bytes 3818496 | tf_op jit(solution)/shard_map/pallas_call | solution.py:125
  89.6 0.0 collective-permute-done.3.refs_1_
  89.6 0.4 shard_map.50
  89.9 0.1 reshape.12
  90.1 17.3 %all_to_all.20 = bf16[24,2,2048]{2,1,0:T(2,128)(2,1)S(1)} all-to-all(bf16[24,2,2048]{2,1,0:T(2,128)(2,1)S(1)} %reshape.12), channel_id=1, replica_groups=mesh['x'=4,'plane'=24,'core'=2,'tp'=4] {'plane'}, dimensions={0} | all-to-all | bytes 393216 | tf_op jit(solution)/shard_map/all_to_all | solution.py:19
  107.4 0.8 reduce_sum.12
  (2 shorter events, 0.1 us)
Async XLA Ops:
  0.0 0.7 copy-start
  0.7 16.5 %copy-start.3 = (bf16[144,2048]{1,0:T(8,128)(2,1)S(1)}, bf16[144,2048]{1,0:T(8,128)(2,1)}, u32[]{:S(2)}) copy-start(bf16[144,2048]{1,0:T(8,128)(2,1)} %param.5) | copy-start | bytes 1769476
  1.7 15.6 %copy-start.4 = (bf16[144,2048]{1,0:T(8,128)(2,1)S(1)}, bf16[144,2048]{1,0:T(8,128)(2,1)}, u32[]{:S(2)}) copy-start(bf16[144,2048]{1,0:T(8,128)(2,1)} %param.6) | copy-start | bytes 1769476
  1.7 36.5 %all-to-all-start = ((bf16[96,2,2048]{2,1,0:T(2,128)(2,1)}), bf16[96,2,2048]{2,1,0:T(2,128)(2,1)S(1)}, u32[]{:S(2)}, u32[]{:S(2)}) async-start(bf16[96,2,2048]{2,1,0:T(2,128)(2,1)} %shard_map.46), calls=%async_computation | async-start | bytes 1572864 | tf_op jit(solution)/shard_map/all_to_all | solution.py:19
  17.3 20.9 %collective-permute-start.1 = (bf16[288,2048]{1,0:T(8,128)(2,1)S(1)}, bf16[288,2048]{1,0:T(8,128)(2,1)S(1)}, u32[]{:S(2)}, u32[]{:S(2)}) collective-permute-start(bf16[288,2048]{1,0:T(8,128)(2,1)S(1)} %constant_dynamic-update-slice_fusion.refs_0_), channel_id=1, source_target_pairs={{0,4},{4,0},{1,5},{5,1},{2,6},{6,2},{3,7},{7,3},{8,12},{12,8},{9,1... | collective-permute-start | bytes 3538952 | tf_op jit(solution)/shard_map/ppermute | solution.py:150
  20.4 8.4 %collective-permute-start = (bf16[144,2048]{1,0:T(8,128)(2,1)}, bf16[144,2048]{1,0:T(8,128)(2,1)S(1)}, u32[]{:S(2)}, u32[]{:S(2)}) collective-permute-start(bf16[144,2048]{1,0:T(8,128)(2,1)} %refs_0_.1), channel_id=1, source_target_pairs={{0,4},{4,0},{1,5},{5,1},{2,6},{6,2},{3,7},{7,3},{8,12},{12,8},{9,1... | collective-permute-start | bytes 1769480 | tf_op jit(solution)/shard_map/ppermute | solution.py:158
  22.3 34.4 %collective-permute-start.4 = (bf16[144,2048]{1,0:T(8,128)(2,1)}, bf16[144,2048]{1,0:T(8,128)(2,1)}, u32[]{:S(2)}, u32[]{:S(2)}) collective-permute-start(bf16[144,2048]{1,0:T(8,128)(2,1)} %refs_0_.1), channel_id=1, source_target_pairs={{192,0},{384,192},{576,384},{0,576},{193,1},{385,193},{577,385},{1... | collective-permute-start | bytes 1769480 | tf_op jit(solution)/shard_map/ppermute | solution.py:155
  26.9 34.8 %collective-permute-start.6 = (bf16[144,2048]{1,0:T(8,128)(2,1)}, bf16[144,2048]{1,0:T(8,128)(2,1)}, u32[]{:S(2)}, u32[]{:S(2)}) collective-permute-start(bf16[144,2048]{1,0:T(8,128)(2,1)} %refs_0_.1), channel_id=1, source_target_pairs={{576,0},{0,192},{192,384},{384,576},{577,1},{1,193},{193,385},{385... | collective-permute-start | bytes 1769480 | tf_op jit(solution)/shard_map/ppermute | solution.py:155
  28.8 0.8 copy-start.1
  39.8 47.7 %copy-start.2 = (bf16[144,2048]{1,0:T(8,128)(2,1)S(1)}, bf16[144,2048]{1,0:T(8,128)(2,1)}, u32[]{:S(2)}) copy-start(bf16[144,2048]{1,0:T(8,128)(2,1)} %copy-done.1) | copy-start | bytes 1769476
  39.8 23.9 %all-to-all-start.1 = ((bf16[4,72,384]{2,1,0:T(8,128)(2,1)}), bf16[4,72,384]{2,1,0:T(8,128)(2,1)S(1)}, u32[]{:S(2)}, u32[]{:S(2)}) async-start(bf16[4,72,384]{2,1,0:T(8,128)(2,1)} %shard_map.47), calls=%async_computation.1 | async-start | bytes 442368 | tf_op jit(solution)/shard_map/all_to_all | solution.py:19
  52.2 23.3 %collective-permute-start.2 = (bf16[144,2048]{1,0:T(8,128)(2,1)}, bf16[144,2048]{1,0:T(8,128)(2,1)S(1)}, u32[]{:S(2)}, u32[]{:S(2)}) collective-permute-start(bf16[144,2048]{1,0:T(8,128)(2,1)} %refs_0_.1), channel_id=1, source_target_pairs={{384,0},{576,192},{0,384},{192,576},{385,1},{577,193},{1,385},{193... | collective-permute-start | bytes 1769480 | tf_op jit(solution)/shard_map/ppermute | solution.py:155
  56.7 21.5 %collective-permute-start.5 = (bf16[144,2048]{1,0:T(8,128)(2,1)}, bf16[144,2048]{1,0:T(8,128)(2,1)S(1)}, u32[]{:S(2)}, u32[]{:S(2)}) collective-permute-start(bf16[144,2048]{1,0:T(8,128)(2,1)} %collective-permute-done.4.refs_2_), channel_id=1, source_target_pairs={{0,4},{4,0},{1,5},{5,1},{2,6},{6,2},{3,7},{7,3},{8,12},{12,8},{9,1... | collective-permute-start | bytes 1769480 | tf_op jit(solution)/shard_map/ppermute | solution.py:163
  61.7 16.5 %collective-permute-start.7 = (bf16[144,2048]{1,0:T(8,128)(2,1)}, bf16[144,2048]{1,0:T(8,128)(2,1)S(1)}, u32[]{:S(2)}, u32[]{:S(2)}) collective-permute-start(bf16[144,2048]{1,0:T(8,128)(2,1)} %collective-permute-done.6.refs_4_), channel_id=1, source_target_pairs={{0,4},{4,0},{1,5},{5,1},{2,6},{6,2},{3,7},{7,3},{8,12},{12,8},{9,1... | collective-permute-start | bytes 1769480 | tf_op jit(solution)/shard_map/ppermute | solution.py:163
  64.5 23.0 %all-to-all-start.2 = ((bf16[16,48,72]{2,1,0:T(8,128)(2,1)}), bf16[16,48,72]{2,1,0:T(8,128)(2,1)S(1)}, u32[]{:S(2)}, u32[]{:S(2)}) async-start(bf16[16,48,72]{2,1,0:T(8,128)(2,1)} %bitcast.1), calls=%async_computation.2 | async-start | bytes 393216 | tf_op jit(solution)/shard_map/all_to_all | solution.py:19
  75.5 14.1 %collective-permute-start.3 = (bf16[144,2048]{1,0:T(8,128)(2,1)S(1)}, bf16[144,2048]{1,0:T(8,128)(2,1)S(1)}, u32[]{:S(2)}, u32[]{:S(2)}) collective-permute-start(bf16[144,2048]{1,0:T(8,128)(2,1)S(1)} %collective-permute-done.2.refs_0_), channel_id=1, source_target_pairs={{0,4},{4,0},{1,5},{5,1},{2,6},{6,2},{3,7},{7,3},{8,12},{12,8},{9,1... | collective-permute-start | bytes 1769480 | tf_op jit(solution)/shard_map/ppermute | solution.py:163

commit v12 on v11

--- a/solution.py
+++ b/solution.py
@@ -46,10 +46,14 @@
     )(rows)
 
 
-def up_kernel(block_ref, *refs):
+def up_kernel(line, block_ref, *refs):
     stacks, out_ref = refs[:-1], refs[-1]
     share, each = out_ref.shape[1], out_ref.shape[0] // len(stacks)
-    block = block_ref[...].reshape(-1, block_ref.shape[-1])
+    chips, mine, width = block_ref.shape
+    block = block_ref[...].reshape(chips // line, line, mine, width)
+    block = jnp.concatenate(
+        [block[:, x].reshape(chips // line * mine, width) for x in range(line)], axis=0
+    )
     for at, stack_ref in enumerate(stacks):
         terms = lax.dot_general(
             stack_ref[...],
@@ -63,13 +67,13 @@
             out_ref[at * each + i] = jnp.concatenate([gate, up], axis=1).astype(out_ref.dtype)
 
 
-def up_product(block, stacks, tp):
+def up_product(block, stacks, tp, line):
     chips, mine, width = block.shape
     rows = chips * mine
     units = sum(stack.shape[0] for stack in stacks)
     vmem = pl.BlockSpec(memory_space=pltpu.VMEM)
     return pl.pallas_call(
-        up_kernel,
+        functools.partial(up_kernel, line),
         out_shape=jax.ShapeDtypeStruct((tp, units // 2 // tp, 2 * rows), jnp.bfloat16),
         in_specs=[vmem] * (1 + len(stacks)),
         out_specs=vmem,
@@ -149,14 +153,14 @@
     stack = jnp.concatenate([gate_weight, up_weight], axis=0)
     other_stack = lax.ppermute(stack, CORE, swap)
     block = spread_rows(tokens, line * plane, 2 * line)
-    block = exchange(block, (X, PLANE))
+    block = exchange(block, (PLANE, X))
 
     gathered = [
         lax.ppermute(down_weight, X, [((i + step) % line, i) for i in range(line)])
         for step in STEPS
     ]
     block, down_other = lax.optimization_barrier((block, lax.ppermute(down_weight, CORE, swap)))
-    parts = exchange(up_product(block, (stack, other_stack), tp), TP)
+    parts = exchange(up_product(block, (stack, other_stack), tp, line), TP)
     spread = hidden_spread(parts, line, column)
     hidden = exchange(spread.reshape(tp * line, column, share), (TP, X))
     here = lax.axis_index(X)

time: 109 us -> 109 us (level)
  no operation moved by 1% of the time
where the time goes in v12:
time: 109 us; the launch traced here: 108 us
  starting transfers between devices  63.6 us (58%)
  waiting for transfers between devices  18.7 us (17%)
  blocking collectives  17.1 us (16%)
  Pallas kernels  5.86 us (5%)
  local copies, waits for them, and re-layouts  1.76 us (2%)
    all_to_all x3, starting transfers between devices, exchange(): return lax.all_to_all(chunks, axes, split_axis=0, concat_axis=0, tiled=True)  38.9 us
    all_to_all x3, waiting for transfers between devices, exchange(): return lax.all_to_all(chunks, axes, split_axis=0, concat_axis=0, tiled=True)  18.7 us
    all_to_all x1, blocking collectives, exchange(): return lax.all_to_all(chunks, axes, split_axis=0, concat_axis=0, tiled=True)  17.1 us
    ppermute x3, starting transfers between devices, body(): lax.ppermute(down_weight, X, [((i + step) % line, i) for i in range(line)])  10.3 us
    ppermute x3, starting transfers between devices, body(): swapped = [lax.ppermute(weight, CORE, swap) for weight in gathered]  9.37 us
    ppermute x1, starting transfers between devices, body(): other_stack = lax.ppermute(stack, CORE, swap)  3.04 us
    pallas_call x2, Pallas kernels, down_product(): pl.pallas_call(functools.partial(down_kernel, line, tuple(weights)), out_...  2.46 us
  transfers between devices with their start and end apart: 11, of which 2 were waited for; matrix products, arithmetic and copies ran while one was open for 0% of the time, Pallas kernels for 4%

profile of v12, /device:TPU:1, one launch (start us, length us, event | category | flops | bytes accessed | tf_op | source)
XLA Modules:
  0.0 108.0 jit_solution(7201996577336898649)
XLA Ops:
  0.0 0.0 copy-start
  0.0 0.7 copy-done
  0.7 0.0 copy-start.3
  0.7 1.0 shard_map.46
  1.7 0.0 copy-start.4
  1.7 15.5 %all-to-all-start = ((bf16[96,2,2048]{2,1,0:T(2,128)(2,1)}), bf16[96,2,2048]{2,1,0:T(2,128)(2,1)S(1)}, u32[]{:S(2)}, u32[]{:S(2)}) async-start(bf16[96,2,2048]{2,1,0:T(2,128)(2,1)} %shard_map.46), calls=%async_computation | async-start | bytes 1572864 | tf_op jit(solution)/shard_map/all_to_all | solution.py:19
  17.2 0.0 copy-done.3
  17.3 0.0 copy-done.4
  17.3 3.0 %collective-permute-start.1 = (bf16[288,2048]{1,0:T(8,128)(2,1)S(1)}, bf16[288,2048]{1,0:T(8,128)(2,1)S(1)}, u32[]{:S(2)}, u32[]{:S(2)}) collective-permute-start(bf16[288,2048]{1,0:T(8,128)(2,1)S(1)} %constant_dynamic-update-slice_fusion.refs_0_), channel_id=1, source_target_pairs={{0,4},{4,0},{1,5},{5,1},{2,6},{6,2},{3,7},{7,3},{8,12},{12,8},{9,1... | collective-permute-start | bytes 3538952 | tf_op jit(solution)/shard_map/ppermute | solution.py:154
  20.4 1.9 %collective-permute-start = (bf16[144,2048]{1,0:T(8,128)(2,1)}, bf16[144,2048]{1,0:T(8,128)(2,1)S(1)}, u32[]{:S(2)}, u32[]{:S(2)}) collective-permute-start(bf16[144,2048]{1,0:T(8,128)(2,1)} %refs_0_.1), channel_id=1, source_target_pairs={{0,4},{4,0},{1,5},{5,1},{2,6},{6,2},{3,7},{7,3},{8,12},{12,8},{9,1... | collective-permute-start | bytes 1769480 | tf_op jit(solution)/shard_map/ppermute | solution.py:162
  22.3 4.1 %collective-permute-start.4 = (bf16[144,2048]{1,0:T(8,128)(2,1)}, bf16[144,2048]{1,0:T(8,128)(2,1)}, u32[]{:S(2)}, u32[]{:S(2)}) collective-permute-start(bf16[144,2048]{1,0:T(8,128)(2,1)} %refs_0_.1), channel_id=1, source_target_pairs={{192,0},{384,192},{576,384},{0,576},{193,1},{385,193},{577,385},{1... | collective-permute-start | bytes 1769480 | tf_op jit(solution)/shard_map/ppermute | solution.py:159
  26.4 1.9 %collective-permute-start.6 = (bf16[144,2048]{1,0:T(8,128)(2,1)}, bf16[144,2048]{1,0:T(8,128)(2,1)}, u32[]{:S(2)}, u32[]{:S(2)}) collective-permute-start(bf16[144,2048]{1,0:T(8,128)(2,1)} %refs_0_.1), channel_id=1, source_target_pairs={{576,0},{0,192},{192,384},{384,576},{577,1},{1,193},{193,385},{385... | collective-permute-start | bytes 1769480 | tf_op jit(solution)/shard_map/ppermute | solution.py:159
  28.3 0.0 collective-permute-done.refs_1_
  28.3 0.0 copy-start.1
  28.4 0.8 copy-done.1
  29.2 9.5 %all-to-all-done.block_ref = bf16[96,2,2048]{2,1,0:T(2,128)(2,1)S(1)} async-done(((bf16[96,2,2048]{2,1,0:T(2,128)(2,1)}), bf16[96,2,2048]{2,1,0:T(2,128)(2,1)S(1)}, u32[]{:S(2)}, u32[]{:S(2)}) %all-to-all-start) | async-done | bytes 786464 | tf_op jit(solution)/shard_map/all_to_all | solution.py:19
  38.7 0.0 collective-permute-done.1.refs_1_
  38.7 1.6 %shard_map.47 = bf16[4,72,384]{2,1,0:T(8,128)(2,1)} custom-call(bf16[96,2,2048]{2,1,0:T(2,128)(2,1)S(1)} %all-to-all-done.block_ref, bf16[288,2048]{1,0:T(8,128)(2,1)S(1)} %constant_dynamic-update-slice_fusion.refs_0_, bf16[288,2048]{1,0:T(8,128)(2,1)S(1)} %collective-permute-done.1.refs_1_), custom_call_target="tpu_custom_call" | custom-call | flops 452984832 | bytes 3366912 | tf_op jit(solution)/shard_map/pallas_call | solution.py:75
  40.2 0.0 copy-start.2
  40.2 13.1 %all-to-all-start.1 = ((bf16[4,72,384]{2,1,0:T(8,128)(2,1)}), bf16[4,72,384]{2,1,0:T(8,128)(2,1)S(1)}, u32[]{:S(2)}, u32[]{:S(2)}) async-start(bf16[4,72,384]{2,1,0:T(8,128)(2,1)} %shard_map.47), calls=%async_computation.1 | async-start | bytes 442368 | tf_op jit(solution)/shard_map/all_to_all | solution.py:19
  53.4 4.3 %collective-permute-start.2 = (bf16[144,2048]{1,0:T(8,128)(2,1)}, bf16[144,2048]{1,0:T(8,128)(2,1)S(1)}, u32[]{:S(2)}, u32[]{:S(2)}) collective-permute-start(bf16[144,2048]{1,0:T(8,128)(2,1)} %refs_0_.1), channel_id=1, source_target_pairs={{384,0},{576,192},{0,384},{192,576},{385,1},{577,193},{1,385},{193... | collective-permute-start | bytes 1769480 | tf_op jit(solution)/shard_map/ppermute | solution.py:159
  57.6 0.0 collective-permute-done.4.refs_2_
  57.7 4.8 %collective-permute-start.5 = (bf16[144,2048]{1,0:T(8,128)(2,1)}, bf16[144,2048]{1,0:T(8,128)(2,1)S(1)}, u32[]{:S(2)}, u32[]{:S(2)}) collective-permute-start(bf16[144,2048]{1,0:T(8,128)(2,1)} %collective-permute-done.4.refs_2_), channel_id=1, source_target_pairs={{0,4},{4,0},{1,5},{5,1},{2,6},{6,2},{3,7},{7,3},{8,12},{12,8},{9,1... | collective-permute-start | bytes 1769480 | tf_op jit(solution)/shard_map/ppermute | solution.py:167
  62.4 0.0 collective-permute-done.6.refs_4_
  62.4 1.9 %collective-permute-start.7 = (bf16[144,2048]{1,0:T(8,128)(2,1)}, bf16[144,2048]{1,0:T(8,128)(2,1)S(1)}, u32[]{:S(2)}, u32[]{:S(2)}) collective-permute-start(bf16[144,2048]{1,0:T(8,128)(2,1)} %collective-permute-done.6.refs_4_), channel_id=1, source_target_pairs={{0,4},{4,0},{1,5},{5,1},{2,6},{6,2},{3,7},{7,3},{8,12},{12,8},{9,1... | collective-permute-start | bytes 1769480 | tf_op jit(solution)/shard_map/ppermute | solution.py:167
  64.4 0.0 all-to-all-done.1.parts_ref
  64.4 0.9 shard_map.48
  65.2 10.3 %all-to-all-start.2 = ((bf16[16,48,72]{2,1,0:T(8,128)(2,1)}), bf16[16,48,72]{2,1,0:T(8,128)(2,1)S(1)}, u32[]{:S(2)}, u32[]{:S(2)}) async-start(bf16[16,48,72]{2,1,0:T(8,128)(2,1)} %bitcast.1), calls=%async_computation.2 | async-start | bytes 393216 | tf_op jit(solution)/shard_map/all_to_all | solution.py:19
  75.6 0.0 collective-permute-done.2.refs_0_
  75.6 2.7 %collective-permute-start.3 = (bf16[144,2048]{1,0:T(8,128)(2,1)S(1)}, bf16[144,2048]{1,0:T(8,128)(2,1)S(1)}, u32[]{:S(2)}, u32[]{:S(2)}) collective-permute-start(bf16[144,2048]{1,0:T(8,128)(2,1)S(1)} %collective-permute-done.2.refs_0_), channel_id=1, source_target_pairs={{0,4},{4,0},{1,5},{5,1},{2,6},{6,2},{3,7},{7,3},{8,12},{12,8},{9,1... | collective-permute-start | bytes 1769480 | tf_op jit(solution)/shard_map/ppermute | solution.py:167
  78.3 0.0 collective-permute-done.5.refs_3_
  78.3 0.0 collective-permute-done.7.refs_5_
  78.3 9.2 %all-to-all-done.2.hidden_ref = bf16[16,48,72]{2,1,0:T(8,128)(2,1)S(1)} async-done(((bf16[16,48,72]{2,1,0:T(8,128)(2,1)}), bf16[16,48,72]{2,1,0:T(8,128)(2,1)S(1)}, u32[]{:S(2)}, u32[]{:S(2)}) %all-to-all-start.2) | async-done | bytes 110624 | tf_op jit(solution)/shard_map/all_to_all | solution.py:19
  87.5 0.0 copy-done.2
  87.5 2.1 %shard_map.49.refs_2_ = f32[48,2048]{1,0:T(8,128)S(1)} custom-call(s32[1]{0:T(128)} %bitcast.here_ref, bf16[16,48,72]{2,1,0:T(8,128)(2,1)S(1)} %all-to-all-done.2.hidden_ref, bf16[144,2048]{1,0:T(8,128)(2,1)} %refs_0_.1, bf16[144,2048]{1,0:T(8,128)(2,1)S(1)} %copy-done.2, bf16[144,2048]{1,0:T(8,128)(2,1)} %collective-permute-done.4.refs_2_, ...), custom_call_target="tpu_custom_call" | custom-call | flops 10871635968 | bytes 3818496 | tf_op jit(solution)/shard_map/pallas_call | solution.py:129
  89.6 0.0 collective-permute-done.3.refs_1_
  89.6 0.4 shard_map.50
  90.0 0.1 reshape.12
  90.2 17.1 %all_to_all.20 = bf16[24,2,2048]{2,1,0:T(2,128)(2,1)S(1)} all-to-all(bf16[24,2,2048]{2,1,0:T(2,128)(2,1)S(1)} %reshape.12), channel_id=1, replica_groups=mesh['x'=4,'plane'=24,'core'=2,'tp'=4] {'plane'}, dimensions={0} | all-to-all | bytes 393216 | tf_op jit(solution)/shard_map/all_to_all | solution.py:19
  107.3 0.8 reduce_sum.12
  (2 shorter events, 0.1 us)
Async XLA Ops:
  0.0 0.7 copy-start
  0.7 16.5 %copy-start.3 = (bf16[144,2048]{1,0:T(8,128)(2,1)S(1)}, bf16[144,2048]{1,0:T(8,128)(2,1)}, u32[]{:S(2)}) copy-start(bf16[144,2048]{1,0:T(8,128)(2,1)} %param.5) | copy-start | bytes 1769476
  1.7 15.6 %copy-start.4 = (bf16[144,2048]{1,0:T(8,128)(2,1)S(1)}, bf16[144,2048]{1,0:T(8,128)(2,1)}, u32[]{:S(2)}) copy-start(bf16[144,2048]{1,0:T(8,128)(2,1)} %param.6) | copy-start | bytes 1769476
  1.7 37.0 %all-to-all-start = ((bf16[96,2,2048]{2,1,0:T(2,128)(2,1)}), bf16[96,2,2048]{2,1,0:T(2,128)(2,1)S(1)}, u32[]{:S(2)}, u32[]{:S(2)}) async-start(bf16[96,2,2048]{2,1,0:T(2,128)(2,1)} %shard_map.46), calls=%async_computation | async-start | bytes 1572864 | tf_op jit(solution)/shard_map/all_to_all | solution.py:19
  17.3 21.3 %collective-permute-start.1 = (bf16[288,2048]{1,0:T(8,128)(2,1)S(1)}, bf16[288,2048]{1,0:T(8,128)(2,1)S(1)}, u32[]{:S(2)}, u32[]{:S(2)}) collective-permute-start(bf16[288,2048]{1,0:T(8,128)(2,1)S(1)} %constant_dynamic-update-slice_fusion.refs_0_), channel_id=1, source_target_pairs={{0,4},{4,0},{1,5},{5,1},{2,6},{6,2},{3,7},{7,3},{8,12},{12,8},{9,1... | collective-permute-start | bytes 3538952 | tf_op jit(solution)/shard_map/ppermute | solution.py:154
  20.4 8.0 %collective-permute-start = (bf16[144,2048]{1,0:T(8,128)(2,1)}, bf16[144,2048]{1,0:T(8,128)(2,1)S(1)}, u32[]{:S(2)}, u32[]{:S(2)}) collective-permute-start(bf16[144,2048]{1,0:T(8,128)(2,1)} %refs_0_.1), channel_id=1, source_target_pairs={{0,4},{4,0},{1,5},{5,1},{2,6},{6,2},{3,7},{7,3},{8,12},{12,8},{9,1... | collective-permute-start | bytes 1769480 | tf_op jit(solution)/shard_map/ppermute | solution.py:162
  22.3 35.3 %collective-permute-start.4 = (bf16[144,2048]{1,0:T(8,128)(2,1)}, bf16[144,2048]{1,0:T(8,128)(2,1)}, u32[]{:S(2)}, u32[]{:S(2)}) collective-permute-start(bf16[144,2048]{1,0:T(8,128)(2,1)} %refs_0_.1), channel_id=1, source_target_pairs={{192,0},{384,192},{576,384},{0,576},{193,1},{385,193},{577,385},{1... | collective-permute-start | bytes 1769480 | tf_op jit(solution)/shard_map/ppermute | solution.py:159
  26.4 36.0 %collective-permute-start.6 = (bf16[144,2048]{1,0:T(8,128)(2,1)}, bf16[144,2048]{1,0:T(8,128)(2,1)}, u32[]{:S(2)}, u32[]{:S(2)}) collective-permute-start(bf16[144,2048]{1,0:T(8,128)(2,1)} %refs_0_.1), channel_id=1, source_target_pairs={{576,0},{0,192},{192,384},{384,576},{577,1},{1,193},{193,385},{385... | collective-permute-start | bytes 1769480 | tf_op jit(solution)/shard_map/ppermute | solution.py:159
  28.3 0.8 copy-start.1
  40.2 47.3 %copy-start.2 = (bf16[144,2048]{1,0:T(8,128)(2,1)S(1)}, bf16[144,2048]{1,0:T(8,128)(2,1)}, u32[]{:S(2)}) copy-start(bf16[144,2048]{1,0:T(8,128)(2,1)} %copy-done.1) | copy-start | bytes 1769476
  40.2 24.1 %all-to-all-start.1 = ((bf16[4,72,384]{2,1,0:T(8,128)(2,1)}), bf16[4,72,384]{2,1,0:T(8,128)(2,1)S(1)}, u32[]{:S(2)}, u32[]{:S(2)}) async-start(bf16[4,72,384]{2,1,0:T(8,128)(2,1)} %shard_map.47), calls=%async_computation.1 | async-start | bytes 442368 | tf_op jit(solution)/shard_map/all_to_all | solution.py:19
  53.4 22.2 %collective-permute-start.2 = (bf16[144,2048]{1,0:T(8,128)(2,1)}, bf16[144,2048]{1,0:T(8,128)(2,1)S(1)}, u32[]{:S(2)}, u32[]{:S(2)}) collective-permute-start(bf16[144,2048]{1,0:T(8,128)(2,1)} %refs_0_.1), channel_id=1, source_target_pairs={{384,0},{576,192},{0,384},{192,576},{385,1},{577,193},{1,385},{193... | collective-permute-start | bytes 1769480 | tf_op jit(solution)/shard_map/ppermute | solution.py:159
  57.7 20.6 %collective-permute-start.5 = (bf16[144,2048]{1,0:T(8,128)(2,1)}, bf16[144,2048]{1,0:T(8,128)(2,1)S(1)}, u32[]{:S(2)}, u32[]{:S(2)}) collective-permute-start(bf16[144,2048]{1,0:T(8,128)(2,1)} %collective-permute-done.4.refs_2_), channel_id=1, source_target_pairs={{0,4},{4,0},{1,5},{5,1},{2,6},{6,2},{3,7},{7,3},{8,12},{12,8},{9,1... | collective-permute-start | bytes 1769480 | tf_op jit(solution)/shard_map/ppermute | solution.py:167
  62.4 15.9 %collective-permute-start.7 = (bf16[144,2048]{1,0:T(8,128)(2,1)}, bf16[144,2048]{1,0:T(8,128)(2,1)S(1)}, u32[]{:S(2)}, u32[]{:S(2)}) collective-permute-start(bf16[144,2048]{1,0:T(8,128)(2,1)} %collective-permute-done.6.refs_4_), channel_id=1, source_target_pairs={{0,4},{4,0},{1,5},{5,1},{2,6},{6,2},{3,7},{7,3},{8,12},{12,8},{9,1... | collective-permute-start | bytes 1769480 | tf_op jit(solution)/shard_map/ppermute | solution.py:167
  65.2 22.3 %all-to-all-start.2 = ((bf16[16,48,72]{2,1,0:T(8,128)(2,1)}), bf16[16,48,72]{2,1,0:T(8,128)(2,1)S(1)}, u32[]{:S(2)}, u32[]{:S(2)}) async-start(bf16[16,48,72]{2,1,0:T(8,128)(2,1)} %bitcast.1), calls=%async_computation.2 | async-start | bytes 393216 | tf_op jit(solution)/shard_map/all_to_all | solution.py:19
  75.6 14.0 %collective-permute-start.3 = (bf16[144,2048]{1,0:T(8,128)(2,1)S(1)}, bf16[144,2048]{1,0:T(8,128)(2,1)S(1)}, u32[]{:S(2)}, u32[]{:S(2)}) collective-permute-start(bf16[144,2048]{1,0:T(8,128)(2,1)S(1)} %collective-permute-done.2.refs_0_), channel_id=1, source_target_pairs={{0,4},{4,0},{1,5},{5,1},{2,6},{6,2},{3,7},{7,3},{8,12},{12,8},{9,1... | collective-permute-start | bytes 1769480 | tf_op jit(solution)/shard_map/ppermute | solution.py:167

commit v13 on v11

--- a/solution.py
+++ b/solution.py
@@ -166,9 +166,10 @@
         {(step, core): weight for core, weight in enumerate(pair)}
         for step, pair in zip((0, *STEPS), pairs)
     ]
-    near = places[0] | places[1] | places[2]
+    near = places[0] | places[1] | {(STEPS[1], 0): gathered[1]}
+    far = {(STEPS[1], 1): swapped[1]} | places[3]
     terms = down_product(hidden, near, here, line, jnp.float32)
-    terms = down_product(hidden, places[3], here, line, jnp.bfloat16, terms)
+    terms = down_product(hidden, far, here, line, jnp.bfloat16, terms)
     terms = exchange(terms.reshape(plane, mine, width), PLANE)
     return jnp.sum(terms.astype(jnp.float32), axis=0).astype(jnp.bfloat16)
 

time: 109 us -> 111 us (1.018); the launches traced: 108 us -> 109 us
  starting transfers between devices: 64.4 us -> 69.3 us
  waiting for transfers between devices: 17.8 us -> 14 us
    all_to_all x3, waiting for transfers between devices: 17.8 us -> 11 us  [exchange(): return lax.all_to_all(chunks, axes, split_axis=0, concat_axis=0, tiled=True)]
    ppermute x3, starting transfers between devices: 9.62 us -> 14.2 us  [body(): swapped = [lax.ppermute(weight, CORE, swap) for weight in gathered]]
    ppermute x3, waiting for transfers between devices: 0.01 us -> 2.98 us  [body(): lax.ppermute(down_weight, X, [((i + step) % line, i) for i in range(line)])]
    ppermute x3, starting transfers between devices: 10.9 us -> 12.1 us  [body(): lax.ppermute(down_weight, X, [((i + step) % line, i) for i in range(line)])]
  transfers between devices with their start and end apart: 11 -> 11, of which waited for: 2 -> 3; matrix products, arithmetic and copies ran while one was open for 0% -> 0% of each run, Pallas kernels for 4% -> 4%
where the time goes in v13:
time: 111 us; the launch traced here: 109 us
  starting transfers between devices  69.3 us (62%)
  blocking collectives  16.9 us (15%)
  waiting for transfers between devices  14 us (13%)
  Pallas kernels  5.9 us (5%)
  local copies, waits for them, and re-layouts  1.76 us (2%)
    all_to_all x3, starting transfers between devices, exchange(): return lax.all_to_all(chunks, axes, split_axis=0, concat_axis=0, tiled=True)  38.1 us
    all_to_all x1, blocking collectives, exchange(): return lax.all_to_all(chunks, axes, split_axis=0, concat_axis=0, tiled=True)  16.9 us
    ppermute x3, starting transfers between devices, body(): swapped = [lax.ppermute(weight, CORE, swap) for weight in gathered]  14.2 us
    ppermute x3, starting transfers between devices, body(): lax.ppermute(down_weight, X, [((i + step) % line, i) for i in range(line)])  12.1 us
    all_to_all x3, waiting for transfers between devices, exchange(): return lax.all_to_all(chunks, axes, split_axis=0, concat_axis=0, tiled=True)  11 us
    ppermute x1, starting transfers between devices, body(): other_stack = lax.ppermute(stack, CORE, swap)  3.04 us
    ppermute x3, waiting for transfers between devices, body(): lax.ppermute(down_weight, X, [((i + step) % line, i) for i in range(line)])  2.98 us
    pallas_call x2, Pallas kernels, down_product(): pl.pallas_call(functools.partial(down_kernel, line, tuple(weights)), out_...  2.46 us
  transfers between devices with their start and end apart: 11, of which 3 were waited for; matrix products, arithmetic and copies ran while one was open for 0% of the time, Pallas kernels for 4%

profile of v13, /device:TPU:1, one launch (start us, length us, event | category | flops | bytes accessed | tf_op | source)
XLA Modules:
  0.0 108.9 jit_solution(17392572235059495036)
XLA Ops:
  0.0 0.0 copy-start
  0.0 0.7 copy-done
  0.7 0.0 copy-start.3
  0.7 1.0 shard_map.46
  1.7 0.0 copy-start.4
  1.7 15.5 %all-to-all-start = ((bf16[96,2,2048]{2,1,0:T(2,128)(2,1)}), bf16[96,2,2048]{2,1,0:T(2,128)(2,1)S(1)}, u32[]{:S(2)}, u32[]{:S(2)}) async-start(bf16[96,2,2048]{2,1,0:T(2,128)(2,1)} %shard_map.46), calls=%async_computation | async-start | bytes 1572864 | tf_op jit(solution)/shard_map/all_to_all | solution.py:19
  17.2 0.0 copy-done.3
  17.3 0.0 copy-done.4
  17.3 3.0 %collective-permute-start.1 = (bf16[288,2048]{1,0:T(8,128)(2,1)S(1)}, bf16[288,2048]{1,0:T(8,128)(2,1)S(1)}, u32[]{:S(2)}, u32[]{:S(2)}) collective-permute-start(bf16[288,2048]{1,0:T(8,128)(2,1)S(1)} %constant_dynamic-update-slice_fusion.refs_0_), channel_id=1, source_target_pairs={{0,4},{4,0},{1,5},{5,1},{2,6},{6,2},{3,7},{7,3},{8,12},{12,8},{9,1... | collective-permute-start | bytes 3538952 | tf_op jit(solution)/shard_map/ppermute | solution.py:150
  20.4 1.9 %collective-permute-start = (bf16[144,2048]{1,0:T(8,128)(2,1)}, bf16[144,2048]{1,0:T(8,128)(2,1)S(1)}, u32[]{:S(2)}, u32[]{:S(2)}) collective-permute-start(bf16[144,2048]{1,0:T(8,128)(2,1)} %refs_0_.1), channel_id=1, source_target_pairs={{0,4},{4,0},{1,5},{5,1},{2,6},{6,2},{3,7},{7,3},{8,12},{12,8},{9,1... | collective-permute-start | bytes 1769480 | tf_op jit(solution)/shard_map/ppermute | solution.py:158
  22.3 4.6 %collective-permute-start.6 = (bf16[144,2048]{1,0:T(8,128)(2,1)}, bf16[144,2048]{1,0:T(8,128)(2,1)}, u32[]{:S(2)}, u32[]{:S(2)}) collective-permute-start(bf16[144,2048]{1,0:T(8,128)(2,1)} %refs_0_.1), channel_id=1, source_target_pairs={{192,0},{384,192},{576,384},{0,576},{193,1},{385,193},{577,385},{1... | collective-permute-start | bytes 1769480 | tf_op jit(solution)/shard_map/ppermute | solution.py:155
  26.9 0.0 collective-permute-done.refs_1_
  26.9 0.0 copy-start.1
  26.9 0.8 copy-done.1
  27.7 10.5 %all-to-all-done.block_ref = bf16[96,2,2048]{2,1,0:T(2,128)(2,1)S(1)} async-done(((bf16[96,2,2048]{2,1,0:T(2,128)(2,1)}), bf16[96,2,2048]{2,1,0:T(2,128)(2,1)S(1)}, u32[]{:S(2)}, u32[]{:S(2)}) %all-to-all-start) | async-done | bytes 786464 | tf_op jit(solution)/shard_map/all_to_all | solution.py:19
  38.2 0.0 collective-permute-done.1.refs_1_
  38.2 1.6 %shard_map.47 = bf16[4,72,384]{2,1,0:T(8,128)(2,1)} custom-call(bf16[96,2,2048]{2,1,0:T(2,128)(2,1)S(1)} %all-to-all-done.block_ref, bf16[288,2048]{1,0:T(8,128)(2,1)S(1)} %constant_dynamic-update-slice_fusion.refs_0_, bf16[288,2048]{1,0:T(8,128)(2,1)S(1)} %collective-permute-done.1.refs_1_), custom_call_target="tpu_custom_call" | custom-call | flops 452984832 | bytes 3366912 | tf_op jit(solution)/shard_map/pallas_call | solution.py:71
  39.8 0.0 copy-start.2
  39.8 12.4 %all-to-all-start.1 = ((bf16[4,72,384]{2,1,0:T(8,128)(2,1)}), bf16[4,72,384]{2,1,0:T(8,128)(2,1)S(1)}, u32[]{:S(2)}, u32[]{:S(2)}) async-start(bf16[4,72,384]{2,1,0:T(8,128)(2,1)} %shard_map.47), calls=%async_computation.1 | async-start | bytes 442368 | tf_op jit(solution)/shard_map/all_to_all | solution.py:19
  52.2 3.1 %collective-permute-start.2 = (bf16[144,2048]{1,0:T(8,128)(2,1)}, bf16[144,2048]{1,0:T(8,128)(2,1)S(1)}, u32[]{:S(2)}, u32[]{:S(2)}) collective-permute-start(bf16[144,2048]{1,0:T(8,128)(2,1)} %refs_0_.1), channel_id=1, source_target_pairs={{576,0},{0,192},{192,384},{384,576},{577,1},{1,193},{193,385},{385... | collective-permute-start | bytes 1769480 | tf_op jit(solution)/shard_map/ppermute | solution.py:155
  55.3 4.4 %collective-permute-start.4 = (bf16[144,2048]{1,0:T(8,128)(2,1)}, bf16[144,2048]{1,0:T(8,128)(2,1)S(1)}, u32[]{:S(2)}, u32[]{:S(2)}) collective-permute-start(bf16[144,2048]{1,0:T(8,128)(2,1)} %refs_0_.1), channel_id=1, source_target_pairs={{384,0},{576,192},{0,384},{192,576},{385,1},{577,193},{1,385},{193... | collective-permute-start | bytes 1769480 | tf_op jit(solution)/shard_map/ppermute | solution.py:155
  59.7 0.0 collective-permute-done.6.refs_2_
  59.7 5.2 %collective-permute-start.7 = (bf16[144,2048]{1,0:T(8,128)(2,1)}, bf16[144,2048]{1,0:T(8,128)(2,1)}, u32[]{:S(2)}, u32[]{:S(2)}) collective-permute-start(bf16[144,2048]{1,0:T(8,128)(2,1)} %collective-permute-done.6.refs_2_), channel_id=1, source_target_pairs={{0,4},{4,0},{1,5},{5,1},{2,6},{6,2},{3,7},{7,3},{8,12},{12,8},{9,1... | collective-permute-start | bytes 1769480 | tf_op jit(solution)/shard_map/ppermute | solution.py:163
  64.9 0.0 all-to-all-done.1.parts_ref
  64.9 0.9 shard_map.48
  65.8 10.2 %all-to-all-start.2 = ((bf16[16,48,72]{2,1,0:T(8,128)(2,1)}), bf16[16,48,72]{2,1,0:T(8,128)(2,1)S(1)}, u32[]{:S(2)}, u32[]{:S(2)}) async-start(bf16[16,48,72]{2,1,0:T(8,128)(2,1)} %bitcast.1), calls=%async_computation.2 | async-start | bytes 393216 | tf_op jit(solution)/shard_map/all_to_all | solution.py:19
  76.0 0.0 collective-permute-done.2.refs_4_
  76.1 2.2 %collective-permute-start.3 = (bf16[144,2048]{1,0:T(8,128)(2,1)S(1)}, bf16[144,2048]{1,0:T(8,128)(2,1)S(1)}, u32[]{:S(2)}, u32[]{:S(2)}) collective-permute-start(bf16[144,2048]{1,0:T(8,128)(2,1)S(1)} %collective-permute-done.2.refs_4_), channel_id=1, source_target_pairs={{0,4},{4,0},{1,5},{5,1},{2,6},{6,2},{3,7},{7,3},{8,12},{12,8},{9,1... | collective-permute-start | bytes 1769480 | tf_op jit(solution)/shard_map/ppermute | solution.py:163
  78.3 3.0 %collective-permute-done.4.refs_1_ = bf16[144,2048]{1,0:T(8,128)(2,1)S(1)} collective-permute-done((bf16[144,2048]{1,0:T(8,128)(2,1)}, bf16[144,2048]{1,0:T(8,128)(2,1)S(1)}, u32[]{:S(2)}, u32[]{:S(2)}) %collective-permute-start.4) | collective-permute-done | bytes 589856 | tf_op jit(solution)/shard_map/ppermute | solution.py:155
  81.2 6.8 %collective-permute-start.5 = (bf16[144,2048]{1,0:T(8,128)(2,1)S(1)}, bf16[144,2048]{1,0:T(8,128)(2,1)S(1)}, u32[]{:S(2)}, u32[]{:S(2)}) collective-permute-start(bf16[144,2048]{1,0:T(8,128)(2,1)S(1)} %collective-permute-done.4.refs_1_), channel_id=1, source_target_pairs={{0,4},{4,0},{1,5},{5,1},{2,6},{6,2},{3,7},{7,3},{8,12},{12,8},{9,1... | collective-permute-start | bytes 1769480 | tf_op jit(solution)/shard_map/ppermute | solution.py:163
  88.0 0.0 collective-permute-done.7.refs_3_
  88.1 0.5 all-to-all-done.2.hidden_ref
  88.5 0.0 copy-done.2
  88.6 2.0 %shard_map.49.refs_3_ = f32[48,2048]{1,0:T(8,128)S(1)} custom-call(s32[1]{0:T(128)} %bitcast.here_ref, bf16[16,48,72]{2,1,0:T(8,128)(2,1)S(1)} %all-to-all-done.2.hidden_ref, bf16[144,2048]{1,0:T(8,128)(2,1)} %refs_0_.1, bf16[144,2048]{1,0:T(8,128)(2,1)S(1)} %copy-done.2, bf16[144,2048]{1,0:T(8,128)(2,1)} %collective-permute-done.6.refs_2_, ...), custom_call_target="tpu_custom_call" | custom-call | flops 9059696640 | bytes 3214848 | tf_op jit(solution)/shard_map/pallas_call | solution.py:125
  90.6 0.0 collective-permute-done.3.refs_0_
  90.6 0.0 collective-permute-done.5.refs_2_
  90.6 0.4 shard_map.50
  91.0 0.1 reshape.12
  91.2 16.9 %all_to_all.20 = bf16[24,2,2048]{2,1,0:T(2,128)(2,1)S(1)} all-to-all(bf16[24,2,2048]{2,1,0:T(2,128)(2,1)S(1)} %reshape.12), channel_id=1, replica_groups=mesh['x'=4,'plane'=24,'core'=2,'tp'=4] {'plane'}, dimensions={0} | all-to-all | bytes 393216 | tf_op jit(solution)/shard_map/all_to_all | solution.py:19
  108.1 0.8 reduce_sum.12
  (2 shorter events, 0.1 us)
Async XLA Ops:
  0.0 0.7 copy-start
  0.7 16.5 %copy-start.3 = (bf16[144,2048]{1,0:T(8,128)(2,1)S(1)}, bf16[144,2048]{1,0:T(8,128)(2,1)}, u32[]{:S(2)}) copy-start(bf16[144,2048]{1,0:T(8,128)(2,1)} %param.5) | copy-start | bytes 1769476
  1.7 15.6 %copy-start.4 = (bf16[144,2048]{1,0:T(8,128)(2,1)S(1)}, bf16[144,2048]{1,0:T(8,128)(2,1)}, u32[]{:S(2)}) copy-start(bf16[144,2048]{1,0:T(8,128)(2,1)} %param.6) | copy-start | bytes 1769476
  1.7 36.5 %all-to-all-start = ((bf16[96,2,2048]{2,1,0:T(2,128)(2,1)}), bf16[96,2,2048]{2,1,0:T(2,128)(2,1)S(1)}, u32[]{:S(2)}, u32[]{:S(2)}) async-start(bf16[96,2,2048]{2,1,0:T(2,128)(2,1)} %shard_map.46), calls=%async_computation | async-start | bytes 1572864 | tf_op jit(solution)/shard_map/all_to_all | solution.py:19
  17.3 20.9 %collective-permute-start.1 = (bf16[288,2048]{1,0:T(8,128)(2,1)S(1)}, bf16[288,2048]{1,0:T(8,128)(2,1)S(1)}, u32[]{:S(2)}, u32[]{:S(2)}) collective-permute-start(bf16[288,2048]{1,0:T(8,128)(2,1)S(1)} %constant_dynamic-update-slice_fusion.refs_0_), channel_id=1, source_target_pairs={{0,4},{4,0},{1,5},{5,1},{2,6},{6,2},{3,7},{7,3},{8,12},{12,8},{9,1... | collective-permute-start | bytes 3538952 | tf_op jit(solution)/shard_map/ppermute | solution.py:150
  20.4 6.5 %collective-permute-start = (bf16[144,2048]{1,0:T(8,128)(2,1)}, bf16[144,2048]{1,0:T(8,128)(2,1)S(1)}, u32[]{:S(2)}, u32[]{:S(2)}) collective-permute-start(bf16[144,2048]{1,0:T(8,128)(2,1)} %refs_0_.1), channel_id=1, source_target_pairs={{0,4},{4,0},{1,5},{5,1},{2,6},{6,2},{3,7},{7,3},{8,12},{12,8},{9,1... | collective-permute-start | bytes 1769480 | tf_op jit(solution)/shard_map/ppermute | solution.py:158
  22.3 37.4 %collective-permute-start.6 = (bf16[144,2048]{1,0:T(8,128)(2,1)}, bf16[144,2048]{1,0:T(8,128)(2,1)}, u32[]{:S(2)}, u32[]{:S(2)}) collective-permute-start(bf16[144,2048]{1,0:T(8,128)(2,1)} %refs_0_.1), channel_id=1, source_target_pairs={{192,0},{384,192},{576,384},{0,576},{193,1},{385,193},{577,385},{1... | collective-permute-start | bytes 1769480 | tf_op jit(solution)/shard_map/ppermute | solution.py:155
  26.9 0.8 copy-start.1
  39.8 48.8 %copy-start.2 = (bf16[144,2048]{1,0:T(8,128)(2,1)S(1)}, bf16[144,2048]{1,0:T(8,128)(2,1)}, u32[]{:S(2)}) copy-start(bf16[144,2048]{1,0:T(8,128)(2,1)} %copy-done.1) | copy-start | bytes 1769476
  39.8 25.2 %all-to-all-start.1 = ((bf16[4,72,384]{2,1,0:T(8,128)(2,1)}), bf16[4,72,384]{2,1,0:T(8,128)(2,1)S(1)}, u32[]{:S(2)}, u32[]{:S(2)}) async-start(bf16[4,72,384]{2,1,0:T(8,128)(2,1)} %shard_map.47), calls=%async_computation.1 | async-start | bytes 442368 | tf_op jit(solution)/shard_map/all_to_all | solution.py:19
  52.2 23.9 %collective-permute-start.2 = (bf16[144,2048]{1,0:T(8,128)(2,1)}, bf16[144,2048]{1,0:T(8,128)(2,1)S(1)}, u32[]{:S(2)}, u32[]{:S(2)}) collective-permute-start(bf16[144,2048]{1,0:T(8,128)(2,1)} %refs_0_.1), channel_id=1, source_target_pairs={{576,0},{0,192},{192,384},{384,576},{577,1},{1,193},{193,385},{385... | collective-permute-start | bytes 1769480 | tf_op jit(solution)/shard_map/ppermute | solution.py:155
  55.3 26.0 %collective-permute-start.4 = (bf16[144,2048]{1,0:T(8,128)(2,1)}, bf16[144,2048]{1,0:T(8,128)(2,1)S(1)}, u32[]{:S(2)}, u32[]{:S(2)}) collective-permute-start(bf16[144,2048]{1,0:T(8,128)(2,1)} %refs_0_.1), channel_id=1, source_target_pairs={{384,0},{576,192},{0,384},{192,576},{385,1},{577,193},{1,385},{193... | collective-permute-start | bytes 1769480 | tf_op jit(solution)/shard_map/ppermute | solution.py:155
  59.7 28.3 %collective-permute-start.7 = (bf16[144,2048]{1,0:T(8,128)(2,1)}, bf16[144,2048]{1,0:T(8,128)(2,1)}, u32[]{:S(2)}, u32[]{:S(2)}) collective-permute-start(bf16[144,2048]{1,0:T(8,128)(2,1)} %collective-permute-done.6.refs_2_), channel_id=1, source_target_pairs={{0,4},{4,0},{1,5},{5,1},{2,6},{6,2},{3,7},{7,3},{8,12},{12,8},{9,1... | collective-permute-start | bytes 1769480 | tf_op jit(solution)/shard_map/ppermute | solution.py:163
  65.8 22.7 %all-to-all-start.2 = ((bf16[16,48,72]{2,1,0:T(8,128)(2,1)}), bf16[16,48,72]{2,1,0:T(8,128)(2,1)S(1)}, u32[]{:S(2)}, u32[]{:S(2)}) async-start(bf16[16,48,72]{2,1,0:T(8,128)(2,1)} %bitcast.1), calls=%async_computation.2 | async-start | bytes 393216 | tf_op jit(solution)/shard_map/all_to_all | solution.py:19
  76.1 14.5 %collective-permute-start.3 = (bf16[144,2048]{1,0:T(8,128)(2,1)S(1)}, bf16[144,2048]{1,0:T(8,128)(2,1)S(1)}, u32[]{:S(2)}, u32[]{:S(2)}) collective-permute-start(bf16[144,2048]{1,0:T(8,128)(2,1)S(1)} %collective-permute-done.2.refs_4_), channel_id=1, source_target_pairs={{0,4},{4,0},{1,5},{5,1},{2,6},{6,2},{3,7},{7,3},{8,12},{12,8},{9,1... | collective-permute-start | bytes 1769480 | tf_op jit(solution)/shard_map/ppermute | solution.py:163
  81.2 9.3 %collective-permute-start.5 = (bf16[144,2048]{1,0:T(8,128)(2,1)S(1)}, bf16[144,2048]{1,0:T(8,128)(2,1)S(1)}, u32[]{:S(2)}, u32[]{:S(2)}) collective-permute-start(bf16[144,2048]{1,0:T(8,128)(2,1)S(1)} %collective-permute-done.4.refs_1_), channel_id=1, source_target_pairs={{0,4},{4,0},{1,5},{5,1},{2,6},{6,2},{3,7},{7,3},{8,12},{12,8},{9,1... | collective-permute-start | bytes 1769480 | tf_op jit(solution)/shard_map/ppermute | solution.py:163
